TPU v7x, 32 devices: a whole 2x2x4 slice. The times are simulated.
32 devices in a mesh: req: 4 (over y, x), tok: 8 (over z, core).
Axes of the slice: x: 2, y: 2, z: 4, core: 2. Of those that a mesh axis runs over, the one named last changes fastest.
Arguments:
- activations: bfloat16 [4, 128, 2048], P('req', 'tok'), may hold values from -4 to 4
- cache_entries: bfloat16 [4, 512, 4096], P('req', 'tok'), may hold values from -162 to 162
- cache_lengths: int32 [4], P('req'), may hold values from 128 to 512, as said below
- attention_gain: float32 [2048], replicated, may hold values from 0.5 to 1.5
- feedforward_gain: float32 [2048], replicated, may hold values from 0.5 to 1.5
- key_value_weight: bfloat16 [2048, 4096], P('tok', 'req'), may hold values from -0.125 to 0.125
- attention_router: bfloat16 [2048, 8], replicated, may hold values from -0.125 to 0.125
- attention_routes: int32 [4, 128, 2], P('req', 'tok'), may hold values from 0 to 7, all different within a row; in each aligned block of 16 rows (0 to 15, 16 to 31, ..., all dimensions but the last counted through in order) at most 6 rows name the same one
- query_weight: bfloat16 [8, 2048, 2048], P('tok'), may hold values from -0.125 to 0.125
- output_weight: bfloat16 [8, 2048, 2048], P('tok'), may hold values from -0.125 to 0.125
- feedforward_router: bfloat16 [2048, 8], replicated, may hold values from -0.125 to 0.125
- feedforward_routes: int32 [4, 128, 2], P('req', 'tok'), may hold values from 0 to 7, all different within a row; in each aligned block of 16 rows (0 to 15, 16 to 31, ..., all dimensions but the last counted through in order) at most 6 rows name the same one
- gate_up: bfloat16 [8, 2048, 11264], P('tok'), may hold values from -0.125 to 0.125
- down_weight: bfloat16 [8, 5632, 2048], P('tok'), may hold values from -0.078125 to 0.078125
Outputs:
- layer_output: bfloat16 [4, 128, 2048], P('req', 'tok')
- new_keys_values: bfloat16 [4, 128, 4096], P('req', 'tok')
Inputs may be any that keep to these rules, and one draw needn't show every extreme that they name: `cache_lengths`: some request's cache is full. `attention_routes`: each row names 2 different experts; in the rows of one device (aligned blocks of 16 rows, requests and tokens taken together in order) no expert is named by more than 6 rows, a bound that some block reaches. `feedforward_routes`: as for attention_routes.
All inputs are finite; a program needn't handle non-finite values.
Results may differ from a plain program's by a relative error of at most 0.015.
The roundings to bfloat16 on the way count: a program that leaves them out, or rounds other values in their place, can miss the bound.
Values may be sent and summed in bfloat16 or wider, within the bound.
No kernel may reach another device: no remote copies, remote signals or barrier semaphores. Data moves between devices by JAX's collectives and lax.ppermute only.
A program may use at most 192 MiB of HBM per device.

v0:
```python
import math

import jax
import jax.numpy as jnp
from jax import lax
from jax.sharding import PartitionSpec as P

HEADS = 16
HEAD_DIM = 128
CAP = 6


def normed(values, gain):
    scale_rows = lax.rsqrt(jnp.mean(values * values, axis=-1, keepdims=True) + 1e-06)
    return values * scale_rows * gain


def slot_matrix(routes, experts, capacity):
    row_count, top_count = routes.shape
    labels = jnp.arange(experts, dtype=jnp.int32)
    onehot = (routes.reshape(row_count * top_count, 1) == labels[None, :]).astype(jnp.int32)
    before = jnp.cumsum(onehot, axis=0) - onehot
    within = jnp.sum(before * onehot, axis=1)
    placed = routes.reshape(row_count * top_count) * capacity + within
    columns = jnp.arange(experts * capacity, dtype=jnp.int32)
    return (placed[:, None] == columns[None, :]).astype(jnp.float32)


def router_gates(hidden, router, routes):
    logits = jnp.dot(hidden, router, preferred_element_type=jnp.float32)
    picked = jnp.take_along_axis(logits, routes, axis=1)
    return jax.nn.sigmoid(2.0 * picked - jnp.sum(picked, axis=1, keepdims=True))


def token_matrices(pair_slots, gates, top_count):
    row_count = gates.shape[0]
    per_token = pair_slots.reshape(row_count, top_count, -1)
    picked = jnp.sum(per_token, axis=1)
    weighted = jnp.sum(per_token * gates[:, :, None], axis=1)
    return (picked, weighted)


def spread_slots(slot_rows, experts, groups, capacity):
    feat_width = slot_rows.shape[-1]
    shaped = slot_rows.reshape(experts, 1, capacity, feat_width)
    return jnp.broadcast_to(shaped, (experts, groups, capacity, feat_width)).reshape(
        experts * groups, capacity, feat_width
    )


def head_groups(rows, experts, groups, group_width):
    row_count = rows.shape[0]
    shaped = (
        rows.reshape(row_count, 2, groups, group_width)
        .transpose(2, 0, 1, 3)
        .reshape(groups, row_count, 2 * group_width)
    )
    return jnp.broadcast_to(shaped[None], (experts, groups, row_count, 2 * group_width)).reshape(
        experts * groups, row_count, 2 * group_width
    )


def group_sum(received, experts, groups, capacity):
    feat_width = received.shape[-1]
    summed = jnp.sum(
        received.reshape(experts, groups, capacity, feat_width).astype(jnp.float32), axis=1
    )
    return summed.reshape(experts * capacity, feat_width)


def expert_feedforward(received, gate_piece, down_piece):
    units = down_piece.shape[0]
    projected = jnp.einsum("scd,df->scf", received, gate_piece, preferred_element_type=jnp.float32)
    active = (jax.nn.silu(projected[..., :units]) * projected[..., units:]).astype(jnp.bfloat16)
    return jnp.einsum("scf,fd->scd", active, down_piece, preferred_element_type=jnp.float32).astype(
        jnp.bfloat16
    )


def local(
    activations,
    cache_entries,
    cache_lengths,
    attention_gain,
    feedforward_gain,
    key_value_weight,
    attention_router,
    attention_routes,
    query_weight,
    output_weight,
    feedforward_router,
    feedforward_routes,
    gate_up,
    down_weight,
):
    tok_count = lax.axis_size("tok")
    tok_index = lax.axis_index("tok")
    experts = attention_router.shape[1]
    groups = tok_count // experts
    query_rows = activations.shape[1]
    cache_rows = cache_entries.shape[1]
    top_count = attention_routes.shape[2]
    model_width = activations.shape[2]
    head_count = HEADS // groups
    group_width = head_count * HEAD_DIM
    block_span = cache_rows + query_rows
    score_scale = 1.0 / math.sqrt(HEAD_DIM)
    cache_part = cache_entries[0]
    residual_in = activations[0].astype(jnp.float32)
    hidden = normed(residual_in, attention_gain).astype(jnp.bfloat16)
    stacked = lax.all_gather(hidden, "req", axis=0, tiled=True)
    projected_part = jnp.dot(
        stacked,
        lax.all_gather(key_value_weight, "tok", axis=0, tiled=True),
        preferred_element_type=jnp.float32,
    )
    new_keys_values = lax.all_to_all(
        projected_part.astype(jnp.bfloat16), "req", split_axis=0, concat_axis=1, tiled=True
    )
    combined = jnp.concatenate([cache_part, new_keys_values], axis=0)
    group_keys = lax.all_to_all(
        head_groups(combined, experts, groups, group_width),
        "tok",
        split_axis=0,
        concat_axis=0,
        tiled=True,
    )
    attn_routes = attention_routes[0]
    attn_pairs = slot_matrix(attn_routes, experts, CAP)
    attn_gate = router_gates(hidden, attention_router, attn_routes)
    attn_pick, attn_weights = token_matrices(attn_pairs, attn_gate, top_count)
    slot_inputs = jnp.dot(
        attn_pick.T.astype(jnp.bfloat16), hidden, preferred_element_type=jnp.float32
    ).astype(jnp.bfloat16)
    token_place = tok_index * query_rows + jnp.arange(query_rows, dtype=jnp.int32)
    slot_place = jnp.sum(attn_pick.astype(jnp.int32) * token_place[:, None], axis=0)
    query_send = spread_slots(slot_inputs, experts, groups, CAP)
    place_send = jnp.broadcast_to(
        slot_place.reshape(experts, 1, CAP), (experts, groups, CAP)
    ).reshape(tok_count, CAP)
    length = cache_lengths[0]
    source = jnp.arange(tok_count, dtype=jnp.int32).reshape(groups, experts, 1)
    offset = jnp.arange(block_span, dtype=jnp.int32).reshape(1, 1, block_span)
    turn_shape = (groups, experts * block_span)
    cached = jnp.broadcast_to(offset < cache_rows, (groups, experts, block_span)).reshape(
        turn_shape
    )
    cache_usable = (source * cache_rows + offset < length).reshape(turn_shape)
    fresh_place = (source * query_rows + offset - cache_rows).reshape(turn_shape)
    key_turns = group_keys.reshape(groups, experts * block_span, 2, head_count, HEAD_DIM)
    slot_rows = lax.all_to_all(query_send, "tok", split_axis=0, concat_axis=0, tiled=True)
    slot_places = lax.all_to_all(place_send, "tok", split_axis=0, concat_axis=0, tiled=True)
    items = slot_rows.shape[1]
    query_three = (
        jnp.einsum("scd,df->scf", slot_rows, query_weight[0], preferred_element_type=jnp.float32)
        .astype(jnp.bfloat16)
        .reshape(tok_count * items, head_count, HEAD_DIM)
    )
    query_place = slot_places.reshape(tok_count * items)

    def one_turn(state_in, turn_data):
        row_max, row_sums, weighted = state_in
        keys_values, cached_turn, usable_turn, place_turn = turn_data
        usable = jnp.where(
            cached_turn[None, :], usable_turn[None, :], place_turn[None, :] <= query_place[:, None]
        )[None]
        scores = (
            jnp.einsum(
                "phd,khd->hpk", query_three, keys_values[:, 0], preferred_element_type=jnp.float32
            )
            * score_scale
        )
        scores = jnp.where(usable, scores, -1e30)
        new_max = jnp.maximum(row_max, jnp.max(scores, axis=-1))
        weights = jnp.where(usable, jnp.exp(scores - new_max[..., None]), 0.0).astype(jnp.bfloat16)
        factor = jnp.exp(row_max - new_max)
        row_sums = row_sums * factor + jnp.sum(weights.astype(jnp.float32), axis=-1)
        weighted = weighted * factor[..., None] + jnp.einsum(
            "hpk,khd->hpd", weights, keys_values[:, 1], preferred_element_type=jnp.float32
        )
        return ((new_max, row_sums, weighted), None)

    query_total = tok_count * items
    initial = (
        jnp.full((head_count, query_total), -1e30, jnp.float32),
        jnp.zeros((head_count, query_total), jnp.float32),
        jnp.zeros((head_count, query_total, HEAD_DIM), jnp.float32),
    )
    final_state, _ = lax.scan(one_turn, initial, (key_turns, cached, cache_usable, fresh_place))
    row_max, row_sums, weighted = final_state
    attended = (
        (weighted / row_sums[..., None])
        .astype(jnp.bfloat16)
        .transpose(1, 0, 2)
        .reshape(tok_count, items, group_width)
    )
    parts = jnp.einsum(
        "scf,fd->scd", attended, output_weight[0], preferred_element_type=jnp.float32
    ).astype(jnp.bfloat16)
    output_back = lax.all_to_all(parts, "tok", split_axis=0, concat_axis=0, tiled=True)
    output_sums = group_sum(output_back, experts, groups, CAP)
    mixed_rows = (
        residual_in + jnp.dot(attn_weights, output_sums, precision=lax.Precision.HIGHEST)
    ).astype(jnp.bfloat16)
    hidden_two = normed(mixed_rows.astype(jnp.float32), feedforward_gain).astype(jnp.bfloat16)
    ffn_routes = feedforward_routes[0]
    ffn_pairs = slot_matrix(ffn_routes, experts, CAP)
    ffn_gate = router_gates(hidden_two, feedforward_router, ffn_routes)
    ffn_pick, ffn_weights = token_matrices(ffn_pairs, ffn_gate, top_count)
    every_rows, every_routes = (
        lax.all_gather(hidden_two, "tok", axis=0, tiled=True),
        lax.all_gather(ffn_routes, "tok", axis=0, tiled=True),
    )
    routes_all = every_routes.reshape(tok_count, query_rows, top_count)

    def source_slots(routes_block):
        return slot_matrix(routes_block, experts, CAP)

    per_source = jax.vmap(source_slots)(routes_all)
    per_token = jnp.sum(per_source.reshape(tok_count, query_rows, top_count, experts, CAP), axis=2)
    expert_mask = (jnp.arange(experts, dtype=jnp.int32) == tok_index // groups).astype(jnp.float32)
    picked = jnp.einsum("sqec,e->sqc", per_token, expert_mask)
    received = jnp.einsum(
        "sqc,sqd->scd",
        picked.astype(jnp.bfloat16),
        every_rows.reshape(tok_count, query_rows, model_width),
        preferred_element_type=jnp.float32,
    ).astype(jnp.bfloat16)
    expert_parts = expert_feedforward(received, gate_up[0], down_weight[0])
    expert_back = lax.all_to_all(expert_parts, "tok", split_axis=0, concat_axis=0, tiled=True)
    expert_sums = group_sum(expert_back, experts, groups, CAP)
    layer_output = (
        mixed_rows.astype(jnp.float32)
        + jnp.dot(ffn_weights, expert_sums, precision=lax.Precision.HIGHEST)
    ).astype(jnp.bfloat16)
    return (layer_output[None], new_keys_values[None])


def solution(mesh):
    placed = (
        P("req", "tok", None),
        P("req", "tok", None),
        P("req"),
        P(),
        P(),
        P("tok", "req"),
        P(),
        P("req", "tok", None),
        P("tok", None, None),
        P("tok", None, None),
        P(),
        P("req", "tok", None),
        P("tok", None, None),
        P("tok", None, None),
    )
    return jax.shard_map(
        local,
        mesh=mesh,
        in_specs=placed,
        out_specs=(P("req", "tok", None), P("req", "tok", None)),
        check_vma=False,
    )
```

profile of v0, /device:TPU:0, one launch (start us, length us, event | category | flops | bytes accessed | tf_op | source)
XLA Modules:
  0.0 327.8 jit_solution(17640528903466010940)
XLA Ops:
  10.1 1.0 fusion.36
  11.1 0.9 fusion.38
  13.0 10.4 %all_gather.12 = bf16[64,2048]{1,0:T(8,128)(2,1)S(1)} all-gather(bf16[16,2048]{1,0:T(8,128)(2,1)S(1)} %fusion.38), channel_id=1, replica_groups=mesh['req'=4,'tok'=8] {'req'}, dimensions={0}, use_global_device_ids=true | all-gather | bytes 327680 | tf_op jit(solution)/shard_map/all_gather | solution.py:111
  23.6 35.9 %all-gather.3.cloned.1.call-done = bf16[2048,1024]{1,0:T(8,128)(2,1)} async-done(((bf16[256,1024]{1,0:T(8,128)(2,1)}), bf16[2048,1024]{1,0:T(8,128)(2,1)}) %all-gather.3.cloned.1.call-update) | async-done | bytes 4194320 | tf_op jit(solution)/shard_map/all_gather | solution.py:114
  59.5 3.7 %convolution_convert_fusion.2 = bf16[64,1024]{1,0:T(8,128)(2,1)} fusion(bf16[64,2048]{1,0:T(8,128)(2,1)S(1)} %all_gather.12, bf16[2048,1024]{1,0:T(8,128)(2,1)} %all-gather.3.cloned.1.call-done), kind=kOutput, calls=%fused_computation.33 | convolution fusion | flops 268500992 | bytes 4587520 | tf_op jit(solution)/shard_map/dot_general | solution.py:112
  63.2 3.6 %all-to-all-start.2 = ((bf16[4,16,1024]{2,1,0:T(8,128)(2,1)}), bf16[4,16,1024]{2,1,0:T(8,128)(2,1)S(1)}, u32[]{:S(2)}, u32[]{:S(2)}) async-start(bf16[4,16,1024]{2,1,0:T(8,128)(2,1)} %bitcast.9), calls=%async_computation.2 | async-start | bytes 262144 | tf_op jit(solution)/shard_map/all_to_all | solution.py:117
  67.6 4.3 %all-to-all-done.2 = bf16[4,16,1024]{2,1,0:T(8,128)(2,1)S(1)} async-done(((bf16[4,16,1024]{2,1,0:T(8,128)(2,1)}), bf16[4,16,1024]{2,1,0:T(8,128)(2,1)S(1)}, u32[]{:S(2)}, u32[]{:S(2)}) %all-to-all-start.2) | async-done | bytes 131104 | tf_op jit(solution)/shard_map/all_to_all | solution.py:117
  71.9 3.3 %all-to-all-start = ((s32[8,1,6]{2,1,0:T(1,128)}), s32[8,1,6]{2,1,0:T(1,128)S(1)}, u32[]{:S(2)}, u32[]{:S(2)}) async-start(s32[8,1,6]{2,1,0:T(1,128)} %bitcast.5), calls=%async_computation | async-start | bytes 8192 | tf_op jit(solution)/shard_map/all_to_all | solution.py:152
  75.4 0.8 reshape_reshape.2
  76.2 4.4 %all-to-all-done = s32[8,1,6]{2,1,0:T(1,128)S(1)} async-done(((s32[8,1,6]{2,1,0:T(1,128)}), s32[8,1,6]{2,1,0:T(1,128)S(1)}, u32[]{:S(2)}, u32[]{:S(2)}) %all-to-all-start) | async-done | bytes 224 | tf_op jit(solution)/shard_map/all_to_all | solution.py:152
  80.6 3.4 %all-to-all-start.1 = ((bf16[8,6,2048]{2,1,0:T(8,128)(2,1)}), bf16[8,6,2048]{2,1,0:T(8,128)(2,1)S(1)}, u32[]{:S(2)}, u32[]{:S(2)}) async-start(bf16[8,6,2048]{2,1,0:T(8,128)(2,1)} %reshape_reshape.2), calls=%async_computation.1 | async-start | bytes 524288 | tf_op jit(solution)/shard_map/all_to_all | solution.py:151
  84.1 9.6 %all-to-all-done.1 = bf16[8,6,2048]{2,1,0:T(8,128)(2,1)S(1)} async-done(((bf16[8,6,2048]{2,1,0:T(8,128)(2,1)}), bf16[8,6,2048]{2,1,0:T(8,128)(2,1)S(1)}, u32[]{:S(2)}, u32[]{:S(2)}) %all-to-all-start.1) | async-done | bytes 196640 | tf_op jit(solution)/shard_map/all_to_all | solution.py:151
  93.7 3.0 reshape.279
  96.7 4.8 %all-to-all-start.3 = ((bf16[8,80,4096]{2,1,0:T(8,128)(2,1)}), bf16[8,80,4096]{2,1,0:T(8,128)(2,1)}, u32[]{:S(2)}, u32[]{:S(2)}) async-start(bf16[8,80,4096]{2,1,0:T(8,128)(2,1)} %reshape.279), calls=%async_computation.3 | async-start | bytes 10485760 | tf_op jit(solution)/shard_map/all_to_all | solution.py:121
  103.5 120.4 %all-gather = s32[1,128,2]{2,0,1:T(1,128)S(1)} all-gather(s32[1,16,2]{2,0,1:T(1,128)S(1)} %copy.160), channel_id=2, replica_groups=mesh['req'=4,'tok'=8] {'tok'}, dimensions={1}, use_global_device_ids=true | all-gather | bytes 1152 | tf_op jit(solution)/shard_map/all_gather | solution.py:212
  224.6 0.8 reduce.15
  227.3 4.9 %fusion.10 = bf16[8,6,2048]{2,0,1:T(8,128)(2,1)S(1)} fusion(bf16[1,2048,2048]{2,1,0:T(8,128)(2,1)} %param.24, bf16[8,6,2048]{2,1,0:T(8,128)(2,1)S(1)} %all-to-all-done.1), kind=kOutput, calls=%fused_computation.15 | convolution fusion | flops 402751488 | bytes 8781824 | tf_op jit(solution)/shard_map/scd,df->scf/dot_general | solution.py:155
  232.6 4.1 %copy.173 = bf16[80,8,32,128]{3,2,1,0:T(8,128)(2,1)S(1)} copy(bf16[80,8,32,128]{3,1,2,0:T(8,128)(2,1)} %bitcast.35) | data formatting | bytes 10485760
  236.7 0.9 fusion.54
  237.6 1.6 fusion.23
  239.9 1.7 fusion.27
  241.9 4.9 %fusion.13 = bf16[8,6,2048]{2,0,1:T(8,128)(2,1)S(1)} fusion(bf16[1,2048,2048]{2,1,0:T(8,128)(2,1)} %param.25, bf16[8,6,2048]{2,1,0:T(8,128)(2,1)S(1)} %reshape.280), kind=kOutput, calls=%fused_computation.16 | convolution fusion | flops 402751488 | bytes 8781824 | tf_op jit(solution)/shard_map/scf,fd->scd/dot_general | solution.py:197
  246.8 0.8 copy.155
  247.6 3.9 %all-to-all-start.4 = ((bf16[8,6,2048]{2,1,0:T(8,128)(2,1)}), bf16[8,6,2048]{2,1,0:T(8,128)(2,1)S(1)}, u32[]{:S(2)}, u32[]{:S(2)}) async-start(bf16[8,6,2048]{2,1,0:T(8,128)(2,1)} %copy.155), calls=%async_computation.4 | async-start | bytes 524288 | tf_op jit(solution)/shard_map/all_to_all | solution.py:200
  252.6 8.6 %all-to-all-done.4 = bf16[8,6,2048]{2,1,0:T(8,128)(2,1)S(1)} async-done(((bf16[8,6,2048]{2,1,0:T(8,128)(2,1)}), bf16[8,6,2048]{2,1,0:T(8,128)(2,1)S(1)}, u32[]{:S(2)}, u32[]{:S(2)}) %all-to-all-start.4) | async-done | bytes 196640 | tf_op jit(solution)/shard_map/all_to_all | solution.py:200
  261.8 15.2 %all_gather.15 = bf16[128,2048]{1,0:T(8,128)(2,1)S(1)} all-gather(bf16[16,2048]{1,0:T(8,128)(2,1)S(1)} %multiply_convert_fusion), channel_id=1, replica_groups=mesh['req'=4,'tok'=8] {'tok'}, dimensions={0}, use_global_device_ids=true | all-gather | bytes 589824 | tf_op jit(solution)/shard_map/all_gather | solution.py:211
  278.2 18.3 %fusion = f32[8,6,11264]{2,0,1:T(8,128)S(1)} fusion(bf16[1,2048,11264]{2,1,0:T(8,128)(2,1)} %param.28, bf16[8,6,2048]{2,1,0:T(8,128)(2,1)S(1)} %convolution_convert_fusion), kind=kOutput, calls=%fused_computation.2 | convolution fusion | flops 2214592512 | bytes 48496640 | tf_op jit(solution)/shard_map/scd,df->scf/dot_general | solution.py:73
  296.4 9.7 %fusion.16 = bf16[8,6,2048]{2,0,1:T(8,128)(2,1)S(1)} fusion(bf16[1,5632,2048]{2,1,0:T(8,128)(2,1)} %param.29, f32[8,6,11264]{2,0,1:T(8,128)S(1)} %fusion), kind=kOutput, calls=%fused_computation.17 | convolution fusion | flops 1109016576 | bytes 25427968 | tf_op jit(solution)/shard_map/scf,fd->scd/dot_general | solution.py:75
  306.2 0.8 copy.166
  307.0 3.4 %all-to-all-start.5 = ((bf16[8,6,2048]{2,1,0:T(8,128)(2,1)}), bf16[8,6,2048]{2,1,0:T(8,128)(2,1)S(1)}, u32[]{:S(2)}, u32[]{:S(2)}) async-start(bf16[8,6,2048]{2,1,0:T(8,128)(2,1)} %copy.166), calls=%async_computation.5 | async-start | bytes 524288 | tf_op jit(solution)/shard_map/all_to_all | solution.py:230
  310.5 9.5 %all-to-all-done.5 = bf16[8,6,2048]{2,1,0:T(8,128)(2,1)S(1)} async-done(((bf16[8,6,2048]{2,1,0:T(8,128)(2,1)}), bf16[8,6,2048]{2,1,0:T(8,128)(2,1)S(1)}, u32[]{:S(2)}, u32[]{:S(2)}) %all-to-all-start.5) | async-done | bytes 196640 | tf_op jit(solution)/shard_map/all_to_all | solution.py:230
  320.1 0.8 fusion.22
  (106 shorter events, 13.3 us)
Async XLA Ops:
  7.2 4.9 %copy-start = (bf16[2048,8]{0,1:T(8,128)(2,1)S(1)}, bf16[2048,8]{0,1:T(8,128)(2,1)}, u32[]{:S(2)}) copy-start(bf16[2048,8]{0,1:T(8,128)(2,1)} %param.22) | copy-start | bytes 98308
  7.2 52.3 %all-gather.3.cloned.1.call-start = ((), (), s32[]{:S(2)}) async-start(), calls=%async_computation.6 | async-start | bytes 4718592 | tf_op jit(solution)/shard_map/all_gather | solution.py:114
  12.2 11.3 %copy-start.6 = (s32[1,16,2]{1,2,0:T(2,128)S(1)}, s32[1,16,2]{1,2,0:T(2,128)}, u32[]{:S(2)}) copy-start(s32[1,16,2]{1,2,0:T(2,128)} %param.23) | copy-start | bytes 388
  23.6 60.4 %copy-start.3 = (bf16[1,64,4096]{2,1,0:T(8,128)(2,1)S(1)}, bf16[1,64,4096]{2,1,0:T(8,128)(2,1)}, u32[]{:S(2)}) copy-start(bf16[1,64,4096]{2,1,0:T(8,128)(2,1)} %param.17) | copy-start | bytes 1572868
  63.2 8.7 %all-to-all-start.2 = ((bf16[4,16,1024]{2,1,0:T(8,128)(2,1)}), bf16[4,16,1024]{2,1,0:T(8,128)(2,1)S(1)}, u32[]{:S(2)}, u32[]{:S(2)}) async-start(bf16[4,16,1024]{2,1,0:T(8,128)(2,1)} %bitcast.9), calls=%async_computation.2 | async-start | bytes 262144 | tf_op jit(solution)/shard_map/all_to_all | solution.py:117
  71.9 8.7 %all-to-all-start = ((s32[8,1,6]{2,1,0:T(1,128)}), s32[8,1,6]{2,1,0:T(1,128)S(1)}, u32[]{:S(2)}, u32[]{:S(2)}) async-start(s32[8,1,6]{2,1,0:T(1,128)} %bitcast.5), calls=%async_computation | async-start | bytes 8192 | tf_op jit(solution)/shard_map/all_to_all | solution.py:152
  80.6 13.1 %all-to-all-start.1 = ((bf16[8,6,2048]{2,1,0:T(8,128)(2,1)}), bf16[8,6,2048]{2,1,0:T(8,128)(2,1)S(1)}, u32[]{:S(2)}, u32[]{:S(2)}) async-start(bf16[8,6,2048]{2,1,0:T(8,128)(2,1)} %reshape_reshape.2), calls=%async_computation.1 | async-start | bytes 524288 | tf_op jit(solution)/shard_map/all_to_all | solution.py:151
  96.7 4.8 %copy-start.5 = (s32[1,16,2]{1,2,0:T(2,128)S(1)}, s32[1,16,2]{1,2,0:T(2,128)}, u32[]{:S(2)}) copy-start(s32[1,16,2]{1,2,0:T(2,128)} %param.27) | copy-start | bytes 388
  96.7 135.9 %all-to-all-start.3 = ((bf16[8,80,4096]{2,1,0:T(8,128)(2,1)}), bf16[8,80,4096]{2,1,0:T(8,128)(2,1)}, u32[]{:S(2)}, u32[]{:S(2)}) async-start(bf16[8,80,4096]{2,1,0:T(8,128)(2,1)} %reshape.279), calls=%async_computation.3 | async-start | bytes 10485760 | tf_op jit(solution)/shard_map/all_to_all | solution.py:121
  246.8 14.5 %copy-start.2 = (bf16[1,16,2048]{2,1,0:T(8,128)(2,1)S(1)}, bf16[1,16,2048]{2,1,0:T(8,128)(2,1)}, u32[]{:S(2)}) copy-start(bf16[1,16,2048]{2,1,0:T(8,128)(2,1)} %param.16) | copy-start | bytes 196612
  246.8 14.9 %copy-start.7 = (f32[2048]{0:T(1024)S(1)}, f32[2048]{0:T(1024)}, u32[]{:S(2)}) copy-start(f32[2048]{0:T(1024)} %param.20) | copy-start | bytes 24580
  246.8 30.1 %copy-start.4 = (bf16[2048,8]{0,1:T(8,128)(2,1)S(1)}, bf16[2048,8]{0,1:T(8,128)(2,1)}, u32[]{:S(2)}) copy-start(bf16[2048,8]{0,1:T(8,128)(2,1)} %param.26) | copy-start | bytes 98308
  247.6 13.6 %all-to-all-start.4 = ((bf16[8,6,2048]{2,1,0:T(8,128)(2,1)}), bf16[8,6,2048]{2,1,0:T(8,128)(2,1)S(1)}, u32[]{:S(2)}, u32[]{:S(2)}) async-start(bf16[8,6,2048]{2,1,0:T(8,128)(2,1)} %copy.155), calls=%async_computation.4 | async-start | bytes 524288 | tf_op jit(solution)/shard_map/all_to_all | solution.py:200
  296.4 24.5 %copy-start.1 = (bf16[2048,8]{0,1:T(8,128)(2,1)S(1)}, bf16[2048,8]{0,1:T(8,128)(2,1)}, u32[]{:S(2)}) copy-start(bf16[2048,8]{0,1:T(8,128)(2,1)} %param.22) | copy-start | bytes 98308
  307.0 13.1 %all-to-all-start.5 = ((bf16[8,6,2048]{2,1,0:T(8,128)(2,1)}), bf16[8,6,2048]{2,1,0:T(8,128)(2,1)S(1)}, u32[]{:S(2)}, u32[]{:S(2)}) async-start(bf16[8,6,2048]{2,1,0:T(8,128)(2,1)} %copy.166), calls=%async_computation.5 | async-start | bytes 524288 | tf_op jit(solution)/shard_map/all_to_all | solution.py:230
Sparse Core Ops, SparseCore 0:
  9.6 49.8 all-gather.2
where the time goes:
time: 329 us; the launch traced here: 328 us
  blocking collectives  146 us (44%)
  waiting for transfers between devices  73 us (22%)
  matrix products  46.8 us (14%)
  starting transfers between devices  22.5 us (7%)
  local copies, waits for them, and re-layouts  17.6 us (5%)
  between operations  15.1 us (5%)
  other arithmetic  6.82 us (2%)
    all_gather x1, blocking collectives, local(): lax.all_gather(ffn_routes, 'tok', axis=0, tiled=True)  120 us
    all_gather x1, waiting for transfers between devices, local(): lax.all_gather(key_value_weight, 'tok', axis=0, tiled=True)  35.9 us
    dot_general x1, matrix products, expert_feedforward(): jnp.einsum('scd,df->scf', received, gate_piece, preferred_element_type=jn...  18.3 us
    all_gather x1, blocking collectives, local(): lax.all_gather(hidden_two, 'tok', axis=0, tiled=True)  15.2 us
    all_gather x1, blocking collectives, local(): stacked = lax.all_gather(hidden, 'req', axis=0, tiled=True)  10.4 us
    dot_general x1, matrix products, expert_feedforward(): jnp.einsum('scf,fd->scd', active, down_piece, preferred_element_type=jnp....  9.72 us
    all_to_all x1, waiting for transfers between devices, local(): lax.all_to_all(query_send, 'tok', split_axis=0, concat_axis=0, tiled=True)  9.6 us
    all_to_all x1, waiting for transfers between devices, local(): lax.all_to_all(expert_parts, 'tok', split_axis=0, concat_axis=0, tiled=True)  9.55 us
  transfers between devices with their start and end apart: 7, of which 6 were waited for; matrix products, arithmetic and copies ran while one was open for 5% of the time, Pallas kernels for 0%

commit v1 on v0

--- a/solution.py
+++ b/solution.py
@@ -3,6 +3,8 @@
 import jax
 import jax.numpy as jnp
 from jax import lax
+from jax.experimental import pallas as pl
+from jax.experimental.pallas import tpu as pltpu
 from jax.sharding import PartitionSpec as P
 
 HEADS = 16
@@ -236,6 +238,584 @@
     return (layer_output[None], new_keys_values[None])
 
 
+PAD = 8
+LANES = 128
+
+
+def permute(values, axis, pairs):
+    return lax.ppermute(values, axis, pairs)
+
+
+def swap_all(values, axis):
+    return lax.all_to_all(values, axis, split_axis=0, concat_axis=0, tiled=True)
+
+
+def whole_spec():
+    return pl.BlockSpec(memory_space=pltpu.VMEM)
+
+
+def index_spec():
+    return pl.BlockSpec(memory_space=pltpu.SMEM)
+
+
+def iota(shape, axis):
+    return lax.broadcasted_iota(jnp.int32, shape, axis)
+
+
+def padded_picks(routes, experts):
+    row_count = routes.shape[0]
+    shape = (row_count, experts * PAD)
+    column = iota(shape, 1)
+    expert, slot = column // PAD, column % PAD
+    first, second = routes[:, 0:1] == expert, routes[:, 1:2] == expert
+    named = jnp.where(first, 1.0, 0.0) + jnp.where(second, 1.0, 0.0)
+    earlier = (iota((row_count, row_count), 1) < iota((row_count, row_count), 0)).astype(
+        jnp.bfloat16
+    )
+    before = jnp.dot(
+        earlier, named.astype(jnp.bfloat16), preferred_element_type=jnp.float32
+    ).astype(jnp.int32)
+    here = (before == slot) & (slot < CAP)
+    return named * here.astype(jnp.float32), first
+
+
+def gate_weights(hidden, router, routes, picks, first):
+    experts = router.shape[1]
+    logits = jnp.dot(hidden, router, preferred_element_type=jnp.float32)
+    label = iota(logits.shape, 1)
+    one = jnp.sum(jnp.where(routes[:, 0:1] == label, logits, 0.0), axis=1, keepdims=True)
+    two = jnp.sum(jnp.where(routes[:, 1:2] == label, logits, 0.0), axis=1, keepdims=True)
+    gate_one = 1.0 / (1.0 + jnp.exp(two - one))
+    gate_two = 1.0 / (1.0 + jnp.exp(one - two))
+    return picks * jnp.where(first, gate_one, gate_two)
+
+
+def row_norm(values, gain):
+    mean = jnp.mean(values * values, axis=-1, keepdims=True)
+    return (values * lax.rsqrt(mean + 1e-06) * gain).astype(jnp.bfloat16)
+
+
+def pick_rows(picks, rows):
+    return lax.dot_general(
+        picks.astype(jnp.bfloat16),
+        rows,
+        (((0,), (0,)), ((), ())),
+        preferred_element_type=jnp.float32,
+    )
+
+
+def compact(rows):
+    count = rows.shape[0] // PAD * CAP
+    one, two = iota((count, rows.shape[0]), 0), iota((count, rows.shape[0]), 1)
+    chosen = ((one // CAP) * PAD + one % CAP == two).astype(jnp.bfloat16)
+    return jnp.dot(chosen, rows, preferred_element_type=jnp.float32)
+
+
+def spread(rows):
+    count = rows.shape[0] // CAP * PAD
+    one, two = iota((count, rows.shape[0]), 0), iota((count, rows.shape[0]), 1)
+    chosen = ((two // CAP) * PAD + two % CAP == one).astype(jnp.bfloat16)
+    return jnp.dot(chosen, rows, preferred_element_type=jnp.float32)
+
+
+def exact_mix(weights, rows):
+    high = weights.astype(jnp.bfloat16)
+    rest = weights - high.astype(jnp.float32)
+    middle = rest.astype(jnp.bfloat16)
+    low = (rest - middle.astype(jnp.float32)).astype(jnp.bfloat16)
+    count = weights.shape[0]
+    stacked = jnp.dot(
+        jnp.concatenate([high, middle, low], axis=0), rows, preferred_element_type=jnp.float32
+    )
+    return stacked[:count] + (stacked[count : 2 * count] + stacked[2 * count :])
+
+
+def prepare(activations, gain, router, routes, tok_count):
+    rows, width = activations.shape
+    experts = router.shape[1]
+    span = width // tok_count
+    half = rows // 2
+    per_row = width // (2 * span)
+
+    def body(act_ref, gain_ref, router_ref, route_ref, out_ref, weight_ref, wide, copy):
+        route = route_ref[...]
+        hidden = row_norm(act_ref[...].astype(jnp.float32), gain_ref[...])
+        picks, first = padded_picks(route, experts)
+        wide[...] = pick_rows(picks, hidden)
+        copy[...] = hidden.astype(jnp.float32)
+        for dest in range(tok_count):
+            chip, core = dest // 2, dest % 2
+            for place in range(half):
+                row = dest * PAD + CAP + place // per_row
+                for side in range(2):
+                    column = (place % per_row) * 2 * span + side * span
+                    source = (2 * chip + (core ^ side)) * span
+                    wide[row : row + 1, column : column + span] = copy[
+                        core * half + place : core * half + place + 1, source : source + span
+                    ]
+        out_ref[:, :, :width] = (
+            wide[...].astype(jnp.bfloat16).reshape(tok_count, PAD, width)
+        )
+        number = iota((rows, LANES), 0).astype(jnp.float32).astype(jnp.bfloat16)
+        out_ref[:, :, width:] = (
+            pick_rows(picks, number).astype(jnp.bfloat16).reshape(tok_count, PAD, LANES)
+        )
+        weight_ref[...] = gate_weights(hidden, router_ref[...], route, picks, first)
+
+    return pl.pallas_call(
+        body,
+        in_specs=[whole_spec()] * 4,
+        out_specs=[whole_spec()] * 2,
+        out_shape=[
+            jax.ShapeDtypeStruct((tok_count, PAD, width + LANES), jnp.bfloat16),
+            jax.ShapeDtypeStruct((rows, tok_count * PAD), jnp.float32),
+        ],
+        scratch_shapes=[
+            pltpu.VMEM((tok_count * PAD, width), jnp.float32),
+            pltpu.VMEM((rows, width), jnp.float32),
+        ],
+        compiler_params=pltpu.CompilerParams(vmem_limit_bytes=6 << 20),
+        name="prepare",
+    )(activations, gain.reshape(1, width), router, routes)
+
+
+def own_tokens(arrived, tok_count, width):
+    span = width // tok_count
+    per_row = width // (2 * span)
+    extra = PAD - CAP
+
+    def body(in_ref, out_ref, wide):
+        for source in range(tok_count):
+            rows = in_ref[source, :, :width].astype(jnp.float32)
+            for part in range(extra):
+                for place in range(per_row):
+                    row = source * extra * per_row + part * per_row + place
+                    wide[row : row + 1, :] = rows[
+                        CAP + part : CAP + part + 1, place * 2 * span : (place + 1) * 2 * span
+                    ]
+        out_ref[...] = wide[...].astype(jnp.bfloat16)
+
+    count = tok_count * extra * per_row
+    return pl.pallas_call(
+        body,
+        in_specs=[whole_spec()],
+        out_specs=whole_spec(),
+        out_shape=jax.ShapeDtypeStruct((count, 2 * span), jnp.bfloat16),
+        scratch_shapes=[pltpu.VMEM((count, 2 * span), jnp.float32)],
+        compiler_params=pltpu.CompilerParams(vmem_limit_bytes=4 << 20),
+        name="own_tokens",
+    )(arrived)
+
+
+def query_project(arrived, weight, cache_part, tok_count):
+    width = weight.shape[0]
+    span = width // tok_count
+    slots = tok_count * CAP
+    cache_rows = cache_part.shape[0]
+    height = slots + 2 * cache_rows + PAD
+    tile = 2 * span
+
+    def body(in_ref, weight_ref, key_ref, value_ref, out_ref, rows, places):
+        step = pl.program_id(0)
+
+        @pl.when(step == 0)
+        def _():
+            every = compact(in_ref[...].reshape(tok_count * PAD, width + LANES))
+            rows[...] = every[:, :width].astype(jnp.bfloat16)
+            local = every[:, width : width + LANES]
+            mine = iota(local.shape, 0)
+            placed = local + ((mine // CAP) * (2 * PAD)).astype(jnp.float32)
+            placed = jnp.where(mine == iota(local.shape, 1), placed, 0.0)
+            places[...] = jnp.broadcast_to(
+                jnp.sum(placed, axis=0, keepdims=True), places.shape
+            )
+
+        query = jnp.dot(rows[...], weight_ref[...], preferred_element_type=jnp.float32).astype(
+            jnp.bfloat16
+        )
+        line = places[...].astype(jnp.bfloat16)
+        for one in range(tile // span):
+            cols = slice(one * span, (one + 1) * span)
+            out_ref[one, :slots, :] = query[:, cols]
+            out_ref[one, slots : slots + cache_rows, :] = key_ref[:, cols]
+            out_ref[one, slots + cache_rows : slots + 2 * cache_rows, :] = value_ref[:, cols]
+            out_ref[one, slots + 2 * cache_rows :, :] = jnp.concatenate(
+                [line] * (span // LANES), axis=1
+            )
+
+    steps = width // tile
+    return pl.pallas_call(
+        body,
+        grid=(steps,),
+        in_specs=[
+            pl.BlockSpec(arrived.shape, lambda step: (0, 0, 0)),
+            pl.BlockSpec((width, tile), lambda step: (0, step)),
+            pl.BlockSpec((cache_rows, tile), lambda step: (0, step)),
+            pl.BlockSpec((cache_rows, tile), lambda step: (0, step + steps)),
+        ],
+        out_specs=pl.BlockSpec((tile // span, height, span), lambda step: (step, 0, 0)),
+        out_shape=jax.ShapeDtypeStruct((tok_count, height, span), jnp.bfloat16),
+        scratch_shapes=[
+            pltpu.VMEM((slots, width), jnp.bfloat16),
+            pltpu.VMEM((PAD, LANES), jnp.float32),
+        ],
+        compiler_params=pltpu.CompilerParams(vmem_limit_bytes=8 << 20),
+        name="query_project",
+    )(arrived, weight, cache_part, cache_part)
+
+
+def key_value_parts(tokens, weight, sibling, chip):
+    rows, depth = tokens[0].shape
+    half = depth // 2
+    quarter = weight.shape[1] // 4
+    count = len(tokens)
+
+    def body(chip_ref, *refs):
+        token_refs, weight_ref, sibling_ref = refs[:count], refs[count], refs[count + 1]
+        outs = refs[count + 2 :]
+        stacked = jnp.concatenate([one[...] for one in token_refs], axis=0)
+        for turn in range(4):
+            start = pl.multiple_of((chip_ref[0] ^ turn) * quarter, quarter)
+            part = jnp.dot(
+                stacked[:, :half],
+                weight_ref[:, pl.ds(start, quarter)],
+                preferred_element_type=jnp.float32,
+            ) + jnp.dot(
+                stacked[:, half:],
+                sibling_ref[:, pl.ds(start, quarter)],
+                preferred_element_type=jnp.float32,
+            )
+            outs[turn][...] = part.astype(outs[turn].dtype)
+
+    shapes = [
+        jax.ShapeDtypeStruct((count * rows, quarter), jnp.float32 if turn == 0 else jnp.bfloat16)
+        for turn in range(4)
+    ]
+    return pl.pallas_call(
+        body,
+        in_specs=[index_spec()] + [whole_spec()] * (count + 2),
+        out_specs=[whole_spec()] * 4,
+        out_shape=shapes,
+        compiler_params=pltpu.CompilerParams(vmem_limit_bytes=8 << 20),
+        name="key_value_parts",
+    )(chip.reshape(1), *tokens, weight, sibling)
+
+
+def key_value_sum(parts, own_req, core):
+    rows, quarter = parts[0].shape
+    block = rows // 4
+
+    def body(place_ref, *refs):
+        ins, outs = refs[:4], refs[4:]
+        source = (place_ref[0] // 2) * 2 + place_ref[1]
+        for turn in range(4):
+            start = pl.multiple_of((place_ref[0] ^ source ^ turn) * block, block)
+            total = ins[0][pl.ds(start, block), :]
+            for one in ins[1:]:
+                total = total + one[pl.ds(start, block), :].astype(jnp.float32)
+            outs[turn][...] = total.astype(jnp.bfloat16)
+
+    return pl.pallas_call(
+        body,
+        in_specs=[index_spec()] + [whole_spec()] * 4,
+        out_specs=[whole_spec()] * 4,
+        out_shape=[jax.ShapeDtypeStruct((block, quarter), jnp.bfloat16)] * 4,
+        compiler_params=pltpu.CompilerParams(vmem_limit_bytes=4 << 20),
+        name="key_value_sum",
+    )(jnp.stack([own_req, core]), *parts)
+
+
+def attention(message, scalars, fresh_blocks, cache_rows):
+    blocks, _, span = message.shape
+    heads = span // HEAD_DIM
+    slots = blocks * CAP
+    fresh_rows = fresh_blocks[0].shape[0]
+    half = fresh_rows // blocks
+    height = slots + 2 * 2 * half * 2
+    scale = 1.0 / math.sqrt(HEAD_DIM)
+    contract = (((1,), (1,)), ((), ()))
+
+    def body(scalar_ref, in_ref, *refs):
+        fresh_refs, out_ref = refs[:4], refs[4]
+        limit, req = scalar_ref[0], scalar_ref[1]
+        pieces = []
+        for source in range(4):
+            picked = fresh_refs[3][...]
+            for turn in range(3):
+                picked = jnp.where((req ^ source) == turn, fresh_refs[turn][...], picked)
+            pieces.append(picked)
+        new_keys = jnp.concatenate(pieces[:2], axis=0)
+        new_values = jnp.concatenate(pieces[2:], axis=0)
+        cache_usable = iota((1, blocks * cache_rows), 1) < limit
+        new_row = iota((1, 2 * fresh_rows), 1)
+        within = new_row % fresh_rows
+        new_place = (within // half) * (2 * half) + (new_row // fresh_rows) * half + within % half
+        places = []
+        for expert in range(blocks):
+            line = in_ref[expert, slots + 2 * cache_rows :, :LANES].astype(jnp.float32)[0:1]
+            chosen = iota((slots, LANES), 0) == iota((slots, LANES), 1)
+            places.append(jnp.sum(jnp.where(chosen, line, 0.0), axis=1, keepdims=True))
+        new_usable = new_place <= jnp.concatenate(places, axis=0).astype(jnp.int32)
+        flat = in_ref[:, :slots, :].reshape(blocks * slots, span)
+        keys = in_ref[:, slots : slots + cache_rows, :].reshape(blocks * cache_rows, span)
+        values = in_ref[:, slots + cache_rows : slots + 2 * cache_rows, :].reshape(
+            blocks * cache_rows, span
+        )
+        for head in range(heads):
+            cols = slice(head * HEAD_DIM, (head + 1) * HEAD_DIM)
+            query = flat[:, cols]
+            first = lax.dot_general(
+                query, keys[:, cols], contract, preferred_element_type=jnp.float32
+            )
+            second = lax.dot_general(
+                query, new_keys[:, cols], contract, preferred_element_type=jnp.float32
+            )
+            first = jnp.where(cache_usable, first * scale, -1e30)
+            second = jnp.where(new_usable, second * scale, -1e30)
+            top = jnp.maximum(
+                jnp.max(first, axis=-1, keepdims=True), jnp.max(second, axis=-1, keepdims=True)
+            )
+            first = jnp.exp(first - top).astype(jnp.bfloat16)
+            second = jnp.exp(second - top).astype(jnp.bfloat16)
+            sums = jnp.sum(first.astype(jnp.float32), axis=-1, keepdims=True) + jnp.sum(
+                second.astype(jnp.float32), axis=-1, keepdims=True
+            )
+            mixed = jnp.dot(first, values[:, cols], preferred_element_type=jnp.float32) + jnp.dot(
+                second, new_values[:, cols], preferred_element_type=jnp.float32
+            )
+            out_ref[:, :slots, cols] = (
+                (mixed / sums).astype(jnp.bfloat16).reshape(blocks, slots, HEAD_DIM)
+            )
+        for kind in range(2):
+            for part in range(2):
+                start = slots + kind * 2 * half + part * half
+                out_ref[:, start : start + half, :] = pieces[2 * kind + part].reshape(
+                    blocks, half, span
+                )
+
+    return pl.pallas_call(
+        body,
+        in_specs=[index_spec()] + [whole_spec()] * 5,
+        out_specs=whole_spec(),
+        out_shape=jax.ShapeDtypeStruct((blocks, slots + 4 * half, span), jnp.bfloat16),
+        compiler_params=pltpu.CompilerParams(vmem_limit_bytes=14 << 20),
+        name="attention",
+    )(scalars, message, *fresh_blocks)
+
+
+def output_project(arrived, weight, query_rows):
+    blocks, height, span = arrived.shape
+    slots = blocks * CAP
+    width = weight.shape[1]
+    tile = width // 4
+
+    def body(in_ref, weight_ref, out_ref, fresh_ref, rows):
+        @pl.when(pl.program_id(0) == 0)
+        def _():
+            for block in range(blocks):
+                cols = slice(block * span, (block + 1) * span)
+                rows[:, cols] = spread(in_ref[block, :slots, :]).astype(jnp.bfloat16)
+                fresh_ref[:, cols] = in_ref[block, slots : slots + query_rows, :]
+                fresh_ref[:, block * span + width : (block + 1) * span + width] = in_ref[
+                    block, slots + query_rows :, :
+                ]
+
+        part = jnp.dot(rows[...], weight_ref[...], preferred_element_type=jnp.float32)
+        out_ref[...] = part.astype(jnp.bfloat16).reshape(blocks, PAD, tile)
+
+    return pl.pallas_call(
+        body,
+        grid=(width // tile,),
+        in_specs=[
+            pl.BlockSpec(arrived.shape, lambda step: (0, 0, 0)),
+            pl.BlockSpec((blocks * span, tile), lambda step: (0, step)),
+        ],
+        out_specs=[
+            pl.BlockSpec((blocks, PAD, tile), lambda step: (0, 0, step)),
+            pl.BlockSpec((query_rows, 2 * width), lambda step: (0, 0)),
+        ],
+        out_shape=[
+            jax.ShapeDtypeStruct((blocks, PAD, width), jnp.bfloat16),
+            jax.ShapeDtypeStruct((query_rows, 2 * width), jnp.bfloat16),
+        ],
+        scratch_shapes=[pltpu.VMEM((blocks * PAD, blocks * span), jnp.bfloat16)],
+        compiler_params=pltpu.CompilerParams(vmem_limit_bytes=8 << 20),
+        name="output_project",
+    )(arrived, weight)
+
+
+def middle(activations, arrived, weights, gain, router, routes):
+    rows, width = activations.shape
+    blocks = arrived.shape[0]
+    experts = router.shape[1]
+
+    def body(act_ref, in_ref, old_ref, gain_ref, router_ref, route_ref, out_ref, mix_ref, new_ref):
+        route = route_ref[...]
+        added = exact_mix(old_ref[...], in_ref[...].reshape(blocks * PAD, width))
+        mixed = (act_ref[...].astype(jnp.float32) + added).astype(jnp.bfloat16)
+        mix_ref[...] = mixed
+        hidden = row_norm(mixed.astype(jnp.float32), gain_ref[...])
+        picks, first = padded_picks(route, experts)
+        out_ref[...] = (
+            pick_rows(picks, hidden).astype(jnp.bfloat16).reshape(blocks, PAD, width)
+        )
+        new_ref[...] = gate_weights(hidden, router_ref[...], route, picks, first)
+
+    return pl.pallas_call(
+        body,
+        in_specs=[whole_spec()] * 6,
+        out_specs=[whole_spec()] * 3,
+        out_shape=[
+            jax.ShapeDtypeStruct((blocks, PAD, width), jnp.bfloat16),
+            jax.ShapeDtypeStruct((rows, width), jnp.bfloat16),
+            jax.ShapeDtypeStruct((rows, blocks * PAD), jnp.float32),
+        ],
+        compiler_params=pltpu.CompilerParams(vmem_limit_bytes=6 << 20),
+        name="middle",
+    )(activations, arrived, weights, gain.reshape(1, width), router, routes)
+
+
+def finish(mixed, arrived, weights):
+    rows, width = mixed.shape
+
+    def body(mix_ref, in_ref, weight_ref, out_ref):
+        added = exact_mix(weight_ref[...], in_ref[...].reshape(-1, width))
+        out_ref[...] = (mix_ref[...].astype(jnp.float32) + added).astype(jnp.bfloat16)
+
+    return pl.pallas_call(
+        body,
+        in_specs=[whole_spec()] * 3,
+        out_specs=whole_spec(),
+        out_shape=jax.ShapeDtypeStruct((rows, width), jnp.bfloat16),
+        compiler_params=pltpu.CompilerParams(vmem_limit_bytes=4 << 20),
+        name="finish",
+    )(mixed, arrived, weights)
+
+
+def feedforward(arrived, gate_piece, down_piece):
+    blocks, _, width = arrived.shape
+    count = blocks * CAP
+    units = down_piece.shape[0]
+    tile = 512
+    steps = units // tile
+
+    def body(in_ref, gate_ref, up_ref, down_ref, out_ref, rows, total):
+        step = pl.program_id(0)
+
+        @pl.when(step == 0)
+        def _():
+            total[...] = jnp.zeros_like(total)
+            rows[...] = compact(in_ref[...].reshape(blocks * PAD, width)).astype(jnp.bfloat16)
+
+        row = rows[...]
+        gate = jnp.dot(row, gate_ref[...], preferred_element_type=jnp.float32)
+        up = jnp.dot(row, up_ref[...], preferred_element_type=jnp.float32)
+        active = (gate / (1.0 + jnp.exp(-gate)) * up).astype(jnp.bfloat16)
+        total[...] += jnp.dot(active, down_ref[...], preferred_element_type=jnp.float32)
+
+        @pl.when(step == steps - 1)
+        def _():
+            out_ref[...] = (
+                spread(total[...].astype(jnp.bfloat16))
+                .astype(jnp.bfloat16)
+                .reshape(blocks, PAD, width)
+            )
+
+    return pl.pallas_call(
+        body,
+        grid=(steps,),
+        in_specs=[
+            pl.BlockSpec(arrived.shape, lambda step: (0, 0, 0)),
+            pl.BlockSpec((width, tile), lambda step: (0, step)),
+            pl.BlockSpec((width, tile), lambda step: (0, step + steps)),
+            pl.BlockSpec((tile, width), lambda step: (step, 0)),
+        ],
+        out_specs=pl.BlockSpec(arrived.shape, lambda step: (0, 0, 0)),
+        out_shape=jax.ShapeDtypeStruct(arrived.shape, jnp.bfloat16),
+        scratch_shapes=[
+            pltpu.VMEM((count, width), jnp.bfloat16),
+            pltpu.VMEM((count, width), jnp.float32),
+        ],
+        compiler_params=pltpu.CompilerParams(vmem_limit_bytes=20 << 20),
+        cost_estimate=pl.CostEstimate(
+            flops=6 * count * width * units,
+            transcendentals=count * units,
+            bytes_accessed=6 * width * units,
+        ),
+        name="feedforward",
+    )(arrived, gate_piece, gate_piece, down_piece)
+
+
+def local_heads(
+    activations,
+    cache_entries,
+    cache_lengths,
+    attention_gain,
+    feedforward_gain,
+    key_value_weight,
+    attention_router,
+    attention_routes,
+    query_weight,
+    output_weight,
+    feedforward_router,
+    feedforward_routes,
+    gate_up,
+    down_weight,
+):
+    tok_count = lax.axis_size("tok")
+    req_count = lax.axis_size("req")
+    tok_index = lax.axis_index("tok")
+    req_index = lax.axis_index("req")
+    chip, core = tok_index // 2, tok_index % 2
+    query_rows, width = activations.shape[1:]
+    cache_rows = cache_entries.shape[1]
+
+    message, attn_weights = prepare(
+        activations[0], attention_gain, attention_router, attention_routes[0], tok_count
+    )
+    arrived = swap_all(message, "tok")
+    sibling = permute(key_value_weight, "tok", [(one, one ^ 1) for one in range(tok_count)])
+    mine = own_tokens(arrived, tok_count, width)
+    tokens = [mine] + [
+        permute(mine, "req", [(one, one ^ turn) for one in range(req_count)])
+        for turn in range(1, req_count)
+    ]
+    queries = query_project(arrived, query_weight[0], cache_entries[0], tok_count)
+    queries = swap_all(queries, "tok")
+    parts = key_value_parts(tokens, key_value_weight, sibling, chip)
+    parts = [parts[0]] + [
+        permute(parts[turn], "tok", [(one, one ^ (2 * turn)) for one in range(tok_count)])
+        for turn in range(1, 4)
+    ]
+    sums = key_value_sum(parts, req_index, core)
+    fresh_blocks = []
+    for turn in range(4):
+        pairs = []
+        for one in range(req_count * tok_count):
+            r, t = one // tok_count, one % tok_count
+            dest = ((r // 2) * 2 + t % 2) ^ turn
+            pairs.append((one, dest * tok_count + 4 * (r % 2) + t // 2))
+        fresh_blocks.append(permute(sums[turn], ("req", "tok"), pairs))
+    scalars = jnp.stack([cache_lengths[0], req_index])
+    attended = attention(queries, scalars, fresh_blocks, cache_rows)
+    attended = swap_all(attended, "tok")
+    parts_out, new_keys_values = output_project(attended, output_weight[0], query_rows)
+    output_back = swap_all(parts_out, "tok")
+    ffn_send, mixed_rows, ffn_weights = middle(
+        activations[0],
+        output_back,
+        attn_weights,
+        feedforward_gain,
+        feedforward_router,
+        feedforward_routes[0],
+    )
+    received = swap_all(ffn_send, "tok")
+    expert_parts = feedforward(received, gate_up[0], down_weight[0])
+    expert_back = swap_all(expert_parts, "tok")
+    layer_output = finish(mixed_rows, expert_back, ffn_weights)
+    return (layer_output[None], new_keys_values[None])
+
+
 def solution(mesh):
     placed = (
         P("req", "tok", None),
@@ -253,8 +833,10 @@
         P("tok", None, None),
         P("tok", None, None),
     )
+    sizes = dict(mesh.shape)
+    by_heads = sizes["tok"] == 8 and sizes["req"] == 4
     return jax.shard_map(
-        local,
+        local_heads if by_heads else local,
         mesh=mesh,
         in_specs=placed,
         out_specs=(P("req", "tok", None), P("req", "tok", None)),

time: 329 us -> 169 us (0.51)
  blocking collectives: 146 us -> 55.7 us
  matrix products: 46.8 us -> 0 us
  waiting for transfers between devices: 73 us -> 31 us
  Pallas kernels: 0 us -> 33.9 us
  between operations: 15.1 us -> 1.44 us
  other arithmetic: 6.82 us -> 0.15 us
    all_gather x3 -> x0, blocking collectives: 146 us -> none  [the longest x1 120 us: local(): lax.all_gather(ffn_routes, 'tok', axis=0, tiled=True)]
    all_to_all x0 -> x4, blocking collectives: none -> 55.7 us  [swap_all(): return lax.all_to_all(values, axis, split_axis=0, concat_axis=0, tiled=True)]
    dot_general x14 -> x0, matrix products: 46.8 us -> none  [the longest x1 18.3 us: expert_feedforward(): jnp.einsum('scd,df->scf', received, gate_piece, preferred_element_type=jn...]
    all_gather x1 -> x0, waiting for transfers between devices: 35.9 us -> none  [local(): lax.all_gather(key_value_weight, 'tok', axis=0, tiled=True)]
    pallas_call x0 -> x10, Pallas kernels: none -> 33.9 us  [the longest x1 21.8 us: feedforward(): pl.pallas_call(body, grid=(steps,), in_specs=[pl.BlockSpec(arrived.shape,...]
    all_to_all x6 -> x2, waiting for transfers between devices: 36.4 us -> 9.28 us  [swap_all(): return lax.all_to_all(values, axis, split_axis=0, concat_axis=0, tiled=True)]
    ppermute x0 -> x11, waiting for transfers between devices: none -> 21.7 us  [permute(): return lax.ppermute(values, axis, pairs)]
    ppermute x0 -> x11, starting transfers between devices: none -> 18.6 us  [permute(): return lax.ppermute(values, axis, pairs)]
  transfers between devices with their start and end apart: 7 -> 13, of which waited for: 6 -> 8; matrix products, arithmetic and copies ran while one was open for 5% -> 0% of each run, Pallas kernels for 0% -> 1%
where the time goes in v1:
time: 169 us; the launch traced here: 168 us
  blocking collectives  55.7 us (33%)
  Pallas kernels  33.9 us (20%)
  waiting for transfers between devices  31 us (18%)
  starting transfers between devices  25.6 us (15%)
  local copies, waits for them, and re-layouts  20.1 us (12%)
    all_to_all x4, blocking collectives, swap_all(): return lax.all_to_all(values, axis, split_axis=0, concat_axis=0, tiled=True)  55.7 us
    pallas_call x1, Pallas kernels, feedforward(): pl.pallas_call(body, grid=(steps,), in_specs=[pl.BlockSpec(arrived.shape,...  21.8 us
    ppermute x11, waiting for transfers between devices, permute(): return lax.ppermute(values, axis, pairs)  21.7 us
    unnamed x24, local copies, waits for them, and re-layouts  19.3 us
    ppermute x11, starting transfers between devices, permute(): return lax.ppermute(values, axis, pairs)  18.6 us
    all_to_all x2, waiting for transfers between devices, swap_all(): return lax.all_to_all(values, axis, split_axis=0, concat_axis=0, tiled=True)  9.28 us
    all_to_all x2, starting transfers between devices, swap_all(): return lax.all_to_all(values, axis, split_axis=0, concat_axis=0, tiled=True)  6.95 us
    pallas_call x1, Pallas kernels, query_project(): pl.pallas_call(body, grid=(steps,), in_specs=[pl.BlockSpec(arrived.shape,...  3.56 us
  transfers between devices with their start and end apart: 13, of which 8 were waited for; matrix products, arithmetic and copies ran while one was open for 0% of the time, Pallas kernels for 1%

profile of v1, /device:TPU:0, one launch (start us, length us, event | category | flops | bytes accessed | tf_op | source)
XLA Modules:
  0.0 167.9 jit_solution(5434382061363129583)
XLA Ops:
  0.7 1.1 copy.16.router_ref
  2.5 0.8 copy-done.5
  4.7 16.2 %all_to_all.30.in_ref = bf16[8,8,2176]{2,1,0:T(8,128)(2,1)S(1)} all-to-all(bf16[8,8,2176]{2,1,0:T(8,128)(2,1)S(1)} %get-tuple-element.17), channel_id=1, replica_groups=mesh['req'=4,'tok'=8] {'tok'}, dimensions={0} | all-to-all | bytes 557056 | tf_op jit(solution)/shard_map/all_to_all | solution.py:250
  20.9 3.4 %copy-done.1 = bf16[1,2048,2048]{2,1,0:T(8,128)(2,1)S(1)} copy-done((bf16[1,2048,2048]{2,1,0:T(8,128)(2,1)S(1)}, bf16[1,2048,2048]{2,1,0:T(8,128)(2,1)}, u32[]{:S(2)}) %copy-start.1) | copy-done | bytes 8388632
  24.3 1.0 copy-done.3
  25.3 3.6 %query_project.1 = bf16[8,184,256]{2,1,0:T(8,128)(2,1)} custom-call(bf16[8,8,2176]{2,1,0:T(8,128)(2,1)S(1)} %all_to_all.30.in_ref, bf16[2048,2048]{1,0:T(8,128)(2,1)S(1)} %bitcast.16, bf16[64,4096]{1,0:T(8,128)(2,1)S(1)} %bitcast.18, bf16[64,4096]{1,0:T(8,128)(2,1)S(1)} %bitcast.19), custom_call_target="tpu_custom_call" | custom-call | tf_op jit(solution)/shard_map/query_project/pallas_call | solution.py:447
  28.9 3.5 %all-to-all-start.1 = ((bf16[8,184,256]{2,1,0:T(8,128)(2,1)}), bf16[8,184,256]{2,1,0:T(8,128)(2,1)S(1)}, u32[]{:S(2)}, u32[]{:S(2)}) async-start(bf16[8,184,256]{2,1,0:T(8,128)(2,1)} %query_project.1), calls=%async_computation.1 | async-start | bytes 1507328 | tf_op jit(solution)/shard_map/all_to_all | solution.py:250
  32.9 1.6 collective-permute-start
  34.5 1.5 collective-permute-start.1
  36.5 0.8 collective-permute-done.refs_1_
  37.2 1.5 collective-permute-done.1.refs_2_
  38.7 2.4 %collective-permute-done.2.refs_3_ = bf16[64,512]{1,0:T(8,128)(2,1)S(1)} collective-permute-done((bf16[64,512]{1,0:T(8,128)(2,1)S(1)}, bf16[64,512]{1,0:T(8,128)(2,1)S(1)}, u32[]{:S(2)}, u32[]{:S(2)}) %collective-permute-start.2) | collective-permute-done | bytes 65568 | tf_op jit(solution)/shard_map/ppermute | solution.py:246
  41.1 1.0 copy-done.4
  42.6 1.8 %collective-permute-start.4 = (bf16[256,256]{1,0:T(8,128)(2,1)S(1)}, bf16[256,256]{1,0:T(8,128)(2,1)S(1)}, u32[]{:S(2)}, u32[]{:S(2)}) collective-permute-start(bf16[256,256]{1,0:T(8,128)(2,1)S(1)} %get-tuple-element.19), channel_id=1, source_target_pairs={{0,2},{1,3},{2,0},{3,1},{4,6},{5,7},{6,4},{7,5},{8,10},{9,11},{10,... | collective-permute-start | bytes 393224 | tf_op jit(solution)/shard_map/ppermute | solution.py:246
  44.4 2.4 %collective-permute-start.5 = (bf16[256,256]{1,0:T(8,128)(2,1)S(1)}, bf16[256,256]{1,0:T(8,128)(2,1)S(1)}, u32[]{:S(2)}, u32[]{:S(2)}) collective-permute-start(bf16[256,256]{1,0:T(8,128)(2,1)S(1)} %get-tuple-element.20), channel_id=1, source_target_pairs={{0,4},{1,5},{2,6},{3,7},{4,0},{5,1},{6,2},{7,3},{8,12},{9,13},{10,... | collective-permute-start | bytes 393224 | tf_op jit(solution)/shard_map/ppermute | solution.py:246
  47.8 1.2 collective-permute-done.4.refs_1_
  49.0 12.5 %collective-permute-done.5.refs_2_ = bf16[256,256]{1,0:T(8,128)(2,1)S(1)} collective-permute-done((bf16[256,256]{1,0:T(8,128)(2,1)S(1)}, bf16[256,256]{1,0:T(8,128)(2,1)S(1)}, u32[]{:S(2)}, u32[]{:S(2)}) %collective-permute-start.5) | collective-permute-done | bytes 131104 | tf_op jit(solution)/shard_map/ppermute | solution.py:246
  62.1 2.5 %collective-permute-start.10 = (bf16[64,256]{1,0:T(8,128)(2,1)S(1)}, bf16[64,256]{1,0:T(8,128)(2,1)S(1)}, u32[]{:S(2)}, u32[]{:S(2)}) collective-permute-start(bf16[64,256]{1,0:T(8,128)(2,1)S(1)} %get-tuple-element.25), channel_id=1, source_target_pairs={{0,24},{1,16},{2,25},{3,17},{4,26},{5,18},{6,27},{7,19},{8,28},{9,... | collective-permute-start | bytes 98312 | tf_op jit(solution)/shard_map/ppermute | solution.py:246
  65.3 6.6 %collective-permute-start.8 = (bf16[64,256]{1,0:T(8,128)(2,1)S(1)}, bf16[64,256]{1,0:T(8,128)(2,1)S(1)}, u32[]{:S(2)}, u32[]{:S(2)}) collective-permute-start(bf16[64,256]{1,0:T(8,128)(2,1)S(1)} %get-tuple-element.23), channel_id=1, source_target_pairs={{0,8},{1,0},{2,9},{3,1},{4,10},{5,2},{6,11},{7,3},{8,12},{9,4},{10... | collective-permute-start | bytes 98312 | tf_op jit(solution)/shard_map/ppermute | solution.py:246
  72.4 1.3 collective-permute-done.8.refs_1_
  73.8 2.0 %collective-permute-done.9.refs_2_ = bf16[64,256]{1,0:T(8,128)(2,1)S(1)} collective-permute-done((bf16[64,256]{1,0:T(8,128)(2,1)S(1)}, bf16[64,256]{1,0:T(8,128)(2,1)S(1)}, u32[]{:S(2)}, u32[]{:S(2)}) %collective-permute-start.9) | collective-permute-done | bytes 32800 | tf_op jit(solution)/shard_map/ppermute | solution.py:246
  75.8 1.8 %attention.1 = bf16[8,80,256]{2,1,0:T(8,128)(2,1)S(1)} custom-call(s32[2]{0:T(128)S(1)} %pad_add_fusion.scalar_ref, bf16[8,184,256]{2,1,0:T(8,128)(2,1)S(1)} %all-to-all-done.1.in_ref, bf16[64,256]{1,0:T(8,128)(2,1)S(1)} %collective-permute-done.7.refs_0_, bf16[64,256]{1,0:T(8,128)(2,1)S(1)} %collective-permute-done.8.refs_1_, ...), custom_call_target="tpu_custom_call" | custom-call | tf_op jit(solution)/shard_map/attention/pallas_call | solution.py:596
  77.6 15.2 %all_to_all.31.in_ref = bf16[8,80,256]{2,1,0:T(8,128)(2,1)S(1)} all-to-all(bf16[8,80,256]{2,1,0:T(8,128)(2,1)S(1)} %attention.1), channel_id=1, replica_groups=mesh['req'=4,'tok'=8] {'tok'}, dimensions={0} | all-to-all | bytes 655360 | tf_op jit(solution)/shard_map/all_to_all | solution.py:250
  92.7 3.4 %copy-done.2 = bf16[1,2048,2048]{2,1,0:T(8,128)(2,1)S(1)} copy-done((bf16[1,2048,2048]{2,1,0:T(8,128)(2,1)S(1)}, bf16[1,2048,2048]{2,1,0:T(8,128)(2,1)}, u32[]{:S(2)}) %copy-start.2) | copy-done | bytes 8388632
  96.1 3.5 %output_project.1 = (bf16[8,8,2048]{2,1,0:T(8,128)(2,1)}, bf16[16,4096]{1,0:T(8,128)(2,1)}) custom-call(bf16[8,80,256]{2,1,0:T(8,128)(2,1)S(1)} %all_to_all.31.in_ref, bf16[2048,2048]{1,0:T(8,128)(2,1)S(1)} %bitcast.17), custom_call_target="tpu_custom_call" | custom-call | tf_op jit(solution)/shard_map/output_project/pallas_call | solution.py:626
  99.6 3.4 %all-to-all-start.3 = ((bf16[8,8,2048]{2,1,0:T(8,128)(2,1)}), bf16[8,8,2048]{2,1,0:T(8,128)(2,1)S(1)}, u32[]{:S(2)}, u32[]{:S(2)}) async-start(bf16[8,8,2048]{2,1,0:T(8,128)(2,1)} %get-tuple-element.26), calls=%async_computation.3 | async-start | bytes 524288 | tf_op jit(solution)/shard_map/all_to_all | solution.py:250
  103.4 9.3 %all-to-all-done.3.in_ref = bf16[8,8,2048]{2,1,0:T(8,128)(2,1)S(1)} async-done(((bf16[8,8,2048]{2,1,0:T(8,128)(2,1)}), bf16[8,8,2048]{2,1,0:T(8,128)(2,1)S(1)}, u32[]{:S(2)}, u32[]{:S(2)}) %all-to-all-start.3) | async-done | bytes 262176 | tf_op jit(solution)/shard_map/all_to_all | solution.py:250
  113.3 12.1 %all_to_all.32.in_ref = bf16[8,8,2048]{2,1,0:T(8,128)(2,1)S(1)} all-to-all(bf16[8,8,2048]{2,1,0:T(8,128)(2,1)S(1)} %get-tuple-element.29), channel_id=1, replica_groups=mesh['req'=4,'tok'=8] {'tok'}, dimensions={0} | all-to-all | bytes 524288 | tf_op jit(solution)/shard_map/all_to_all | solution.py:250
  125.5 7.6 %copy-done = bf16[1,5632,2048]{2,1,0:T(8,128)(2,1)S(1)} copy-done((bf16[1,5632,2048]{2,1,0:T(8,128)(2,1)S(1)}, bf16[1,5632,2048]{2,1,0:T(8,128)(2,1)}, u32[]{:S(2)}) %copy-start) | copy-done | bytes 23068696
  133.0 21.8 %feedforward.1 = bf16[8,8,2048]{2,1,0:T(8,128)(2,1)S(1)} custom-call(bf16[8,8,2048]{2,1,0:T(8,128)(2,1)S(1)} %all_to_all.32.in_ref, bf16[2048,11264]{1,0:T(8,128)(2,1)} %bitcast.24, bf16[2048,11264]{1,0:T(8,128)(2,1)} %bitcast.25, bf16[5632,2048]{1,0:T(8,128)(2,1)S(1)} %bitcast.15), custom_call_target="tpu_custom_call" | custom-call | flops 3321888768 | bytes 69206016 | tf_op jit(solution)/shard_map/feedforward/pallas_call | solution.py:724
  154.9 12.1 %all_to_all.33.in_ref = bf16[8,8,2048]{2,1,0:T(8,128)(2,1)S(1)} all-to-all(bf16[8,8,2048]{2,1,0:T(8,128)(2,1)S(1)} %feedforward.1), channel_id=1, replica_groups=mesh['req'=4,'tok'=8] {'tok'}, dimensions={0} | all-to-all | bytes 524288 | tf_op jit(solution)/shard_map/all_to_all | solution.py:250
  167.0 0.8 finish.1
  (36 shorter events, 6.7 us)
Async XLA Ops:
  0.6 112.0 %copy-start.6 = (bf16[1,16,2048]{2,1,0:T(8,128)(2,1)S(1)}, bf16[1,16,2048]{2,1,0:T(8,128)(2,1)}, u32[]{:S(2)}) copy-start(bf16[1,16,2048]{2,1,0:T(8,128)(2,1)} %param.14) | copy-start | bytes 196612
  0.6 102.4 %copy-start.9 = (bf16[2048,8]{0,1:T(8,128)(2,1)S(1)}, bf16[2048,8]{0,1:T(8,128)(2,1)}, u32[]{:S(2)}) copy-start(bf16[2048,8]{0,1:T(8,128)(2,1)} %param.24) | copy-start | bytes 98308
  0.7 102.6 %copy-start.10 = (s32[1,16,2]{1,2,0:T(2,128)S(1)}, s32[1,16,2]{1,2,0:T(2,128)}, u32[]{:S(2)}) copy-start(s32[1,16,2]{1,2,0:T(2,128)} %param.25) | copy-start | bytes 388
  0.7 112.0 %copy-start.8 = (f32[2048]{0:T(1024)S(1)}, f32[2048]{0:T(1024)}, u32[]{:S(2)}) copy-start(f32[2048]{0:T(1024)} %param.18) | copy-start | bytes 24580
  2.5 0.8 copy-start.5
  3.3 0.7 copy-start.7
  20.9 3.4 %copy-start.1 = (bf16[1,2048,2048]{2,1,0:T(8,128)(2,1)S(1)}, bf16[1,2048,2048]{2,1,0:T(8,128)(2,1)}, u32[]{:S(2)}) copy-start(bf16[1,2048,2048]{2,1,0:T(8,128)(2,1)} %param.22) | copy-start | bytes 25165828
  24.3 1.0 copy-start.3
  28.9 46.9 %all-to-all-start.1 = ((bf16[8,184,256]{2,1,0:T(8,128)(2,1)}), bf16[8,184,256]{2,1,0:T(8,128)(2,1)S(1)}, u32[]{:S(2)}, u32[]{:S(2)}) async-start(bf16[8,184,256]{2,1,0:T(8,128)(2,1)} %query_project.1), calls=%async_computation.1 | async-start | bytes 1507328 | tf_op jit(solution)/shard_map/all_to_all | solution.py:250
  32.4 4.0 %collective-permute-start.3 = (bf16[256,1024]{1,0:T(8,128)(2,1)}, bf16[256,1024]{1,0:T(8,128)(2,1)S(1)}, u32[]{:S(2)}, u32[]{:S(2)}) collective-permute-start(bf16[256,1024]{1,0:T(8,128)(2,1)} %refs_4_.1), channel_id=1, source_target_pairs={{0,1},{1,0},{2,3},{3,2},{4,5},{5,4},{6,7},{7,6},{8,9},{9,8},{10,11... | collective-permute-start | bytes 1572872 | tf_op jit(solution)/shard_map/ppermute | solution.py:246
  32.9 4.3 %collective-permute-start = (bf16[64,512]{1,0:T(8,128)(2,1)S(1)}, bf16[64,512]{1,0:T(8,128)(2,1)S(1)}, u32[]{:S(2)}, u32[]{:S(2)}) collective-permute-start(bf16[64,512]{1,0:T(8,128)(2,1)S(1)} %own_tokens.1.refs_0_), channel_id=1, source_target_pairs={{0,8},{8,0},{16,24},{24,16},{1,9},{9,1},{17,25},{25,17},{2,10},{10... | collective-permute-start | bytes 196616 | tf_op jit(solution)/shard_map/ppermute | solution.py:246
  34.5 4.3 %collective-permute-start.1 = (bf16[64,512]{1,0:T(8,128)(2,1)S(1)}, bf16[64,512]{1,0:T(8,128)(2,1)S(1)}, u32[]{:S(2)}, u32[]{:S(2)}) collective-permute-start(bf16[64,512]{1,0:T(8,128)(2,1)S(1)} %own_tokens.1.refs_0_), channel_id=1, source_target_pairs={{0,16},{8,24},{16,0},{24,8},{1,17},{9,25},{17,1},{25,9},{2,18},{10... | collective-permute-start | bytes 196616 | tf_op jit(solution)/shard_map/ppermute | solution.py:246
  36.0 5.2 %collective-permute-start.2 = (bf16[64,512]{1,0:T(8,128)(2,1)S(1)}, bf16[64,512]{1,0:T(8,128)(2,1)S(1)}, u32[]{:S(2)}, u32[]{:S(2)}) collective-permute-start(bf16[64,512]{1,0:T(8,128)(2,1)S(1)} %own_tokens.1.refs_0_), channel_id=1, source_target_pairs={{0,24},{8,16},{16,8},{24,0},{1,25},{9,17},{17,9},{25,1},{2,26},{10... | collective-permute-start | bytes 196616 | tf_op jit(solution)/shard_map/ppermute | solution.py:246
  41.1 1.0 copy-start.4
  42.6 6.4 %collective-permute-start.4 = (bf16[256,256]{1,0:T(8,128)(2,1)S(1)}, bf16[256,256]{1,0:T(8,128)(2,1)S(1)}, u32[]{:S(2)}, u32[]{:S(2)}) collective-permute-start(bf16[256,256]{1,0:T(8,128)(2,1)S(1)} %get-tuple-element.19), channel_id=1, source_target_pairs={{0,2},{1,3},{2,0},{3,1},{4,6},{5,7},{6,4},{7,5},{8,10},{9,11},{10,... | collective-permute-start | bytes 393224 | tf_op jit(solution)/shard_map/ppermute | solution.py:246
  44.4 17.1 %collective-permute-start.5 = (bf16[256,256]{1,0:T(8,128)(2,1)S(1)}, bf16[256,256]{1,0:T(8,128)(2,1)S(1)}, u32[]{:S(2)}, u32[]{:S(2)}) collective-permute-start(bf16[256,256]{1,0:T(8,128)(2,1)S(1)} %get-tuple-element.20), channel_id=1, source_target_pairs={{0,4},{1,5},{2,6},{3,7},{4,0},{5,1},{6,2},{7,3},{8,12},{9,13},{10,... | collective-permute-start | bytes 393224 | tf_op jit(solution)/shard_map/ppermute | solution.py:246
  46.8 14.7 %collective-permute-start.6 = (bf16[256,256]{1,0:T(8,128)(2,1)S(1)}, bf16[256,256]{1,0:T(8,128)(2,1)S(1)}, u32[]{:S(2)}, u32[]{:S(2)}) collective-permute-start(bf16[256,256]{1,0:T(8,128)(2,1)S(1)} %get-tuple-element.21), channel_id=1, source_target_pairs={{0,6},{1,7},{2,4},{3,5},{4,2},{5,3},{6,0},{7,1},{8,14},{9,15},{10,... | collective-permute-start | bytes 393224 | tf_op jit(solution)/shard_map/ppermute | solution.py:246
  62.1 10.3 %collective-permute-start.10 = (bf16[64,256]{1,0:T(8,128)(2,1)S(1)}, bf16[64,256]{1,0:T(8,128)(2,1)S(1)}, u32[]{:S(2)}, u32[]{:S(2)}) collective-permute-start(bf16[64,256]{1,0:T(8,128)(2,1)S(1)} %get-tuple-element.25), channel_id=1, source_target_pairs={{0,24},{1,16},{2,25},{3,17},{4,26},{5,18},{6,27},{7,19},{8,28},{9,... | collective-permute-start | bytes 98312 | tf_op jit(solution)/shard_map/ppermute | solution.py:246
  64.6 7.8 %collective-permute-start.7 = (bf16[64,256]{1,0:T(8,128)(2,1)S(1)}, bf16[64,256]{1,0:T(8,128)(2,1)S(1)}, u32[]{:S(2)}, u32[]{:S(2)}) collective-permute-start(bf16[64,256]{1,0:T(8,128)(2,1)S(1)} %get-tuple-element.22), channel_id=1, source_target_pairs={{0,0},{1,8},{2,1},{3,9},{4,2},{5,10},{6,3},{7,11},{8,4},{9,12},{10... | collective-permute-start | bytes 98312 | tf_op jit(solution)/shard_map/ppermute | solution.py:246
  65.3 8.5 %collective-permute-start.8 = (bf16[64,256]{1,0:T(8,128)(2,1)S(1)}, bf16[64,256]{1,0:T(8,128)(2,1)S(1)}, u32[]{:S(2)}, u32[]{:S(2)}) collective-permute-start(bf16[64,256]{1,0:T(8,128)(2,1)S(1)} %get-tuple-element.23), channel_id=1, source_target_pairs={{0,8},{1,0},{2,9},{3,1},{4,10},{5,2},{6,11},{7,3},{8,12},{9,4},{10... | collective-permute-start | bytes 98312 | tf_op jit(solution)/shard_map/ppermute | solution.py:246
  71.9 3.9 %collective-permute-start.9 = (bf16[64,256]{1,0:T(8,128)(2,1)S(1)}, bf16[64,256]{1,0:T(8,128)(2,1)S(1)}, u32[]{:S(2)}, u32[]{:S(2)}) collective-permute-start(bf16[64,256]{1,0:T(8,128)(2,1)S(1)} %get-tuple-element.24), channel_id=1, source_target_pairs={{0,16},{1,24},{2,17},{3,25},{4,18},{5,26},{6,19},{7,27},{8,20},{9,... | collective-permute-start | bytes 98312 | tf_op jit(solution)/shard_map/ppermute | solution.py:246
  92.7 3.4 %copy-start.2 = (bf16[1,2048,2048]{2,1,0:T(8,128)(2,1)S(1)}, bf16[1,2048,2048]{2,1,0:T(8,128)(2,1)}, u32[]{:S(2)}) copy-start(bf16[1,2048,2048]{2,1,0:T(8,128)(2,1)} %param.23) | copy-start | bytes 25165828
  99.6 13.1 %all-to-all-start.3 = ((bf16[8,8,2048]{2,1,0:T(8,128)(2,1)}), bf16[8,8,2048]{2,1,0:T(8,128)(2,1)S(1)}, u32[]{:S(2)}, u32[]{:S(2)}) async-start(bf16[8,8,2048]{2,1,0:T(8,128)(2,1)} %get-tuple-element.26), calls=%async_computation.3 | async-start | bytes 524288 | tf_op jit(solution)/shard_map/all_to_all | solution.py:250
  125.5 7.6 %copy-start = (bf16[1,5632,2048]{2,1,0:T(8,128)(2,1)S(1)}, bf16[1,5632,2048]{2,1,0:T(8,128)(2,1)}, u32[]{:S(2)}) copy-start(bf16[1,5632,2048]{2,1,0:T(8,128)(2,1)} %param.27) | copy-start | bytes 69206016

commit v2 on v1

--- a/solution.py
+++ b/solution.py
@@ -240,6 +240,16 @@
 
 PAD = 8
 LANES = 128
+FF_TILE = 512
+
+
+def column_stream(source, buffers, sems, tile):
+    return [
+        pltpu.make_async_copy(
+            source.at[:, pl.ds(step * tile, tile)], buffers.at[step], sems.at[step]
+        )
+        for step in range(buffers.shape[0])
+    ]
 
 
 def permute(values, axis, pairs):
@@ -262,29 +272,52 @@
     return lax.broadcasted_iota(jnp.int32, shape, axis)
 
 
+def any_spec():
+    return pl.BlockSpec(memory_space=pl.ANY)
+
+
+def in_hbm(*arrays):
+    return [pltpu.with_memory_space_constraint(one, pltpu.HBM) for one in arrays]
+
+
+def in_vmem(*arrays):
+    return [pltpu.with_memory_space_constraint(one, pltpu.VMEM) for one in arrays]
+
+
+def load_all(pairs, sems):
+    copies = [
+        pltpu.make_async_copy(source, target, sems.at[number])
+        for number, (source, target) in enumerate(pairs)
+    ]
+    for one in copies:
+        one.start()
+    for one in copies:
+        one.wait()
+
+
 def padded_picks(routes, experts):
-    row_count = routes.shape[0]
-    shape = (row_count, experts * PAD)
-    column = iota(shape, 1)
-    expert, slot = column // PAD, column % PAD
-    first, second = routes[:, 0:1] == expert, routes[:, 1:2] == expert
+    row_count = routes.shape[1]
+    row = iota((experts * PAD, row_count), 0)
+    expert, slot = row // PAD, row % PAD
+    first, second = routes[0:1, :] == expert, routes[1:2, :] == expert
     named = jnp.where(first, 1.0, 0.0) + jnp.where(second, 1.0, 0.0)
-    earlier = (iota((row_count, row_count), 1) < iota((row_count, row_count), 0)).astype(
+    earlier = (iota((row_count, row_count), 0) < iota((row_count, row_count), 1)).astype(
         jnp.bfloat16
     )
     before = jnp.dot(
-        earlier, named.astype(jnp.bfloat16), preferred_element_type=jnp.float32
+        named.astype(jnp.bfloat16), earlier, preferred_element_type=jnp.float32
     ).astype(jnp.int32)
     here = (before == slot) & (slot < CAP)
     return named * here.astype(jnp.float32), first
 
 
 def gate_weights(hidden, router, routes, picks, first):
-    experts = router.shape[1]
-    logits = jnp.dot(hidden, router, preferred_element_type=jnp.float32)
-    label = iota(logits.shape, 1)
-    one = jnp.sum(jnp.where(routes[:, 0:1] == label, logits, 0.0), axis=1, keepdims=True)
-    two = jnp.sum(jnp.where(routes[:, 1:2] == label, logits, 0.0), axis=1, keepdims=True)
+    logits = lax.dot_general(
+        router, hidden, (((1,), (1,)), ((), ())), preferred_element_type=jnp.float32
+    )
+    label = iota(logits.shape, 0)
+    one = jnp.sum(jnp.where(routes[0:1, :] == label, logits, 0.0), axis=0, keepdims=True)
+    two = jnp.sum(jnp.where(routes[1:2, :] == label, logits, 0.0), axis=0, keepdims=True)
     gate_one = 1.0 / (1.0 + jnp.exp(two - one))
     gate_two = 1.0 / (1.0 + jnp.exp(one - two))
     return picks * jnp.where(first, gate_one, gate_two)
@@ -296,12 +329,7 @@
 
 
 def pick_rows(picks, rows):
-    return lax.dot_general(
-        picks.astype(jnp.bfloat16),
-        rows,
-        (((0,), (0,)), ((), ())),
-        preferred_element_type=jnp.float32,
-    )
+    return jnp.dot(picks.astype(jnp.bfloat16), rows, preferred_element_type=jnp.float32)
 
 
 def compact(rows):
@@ -323,21 +351,36 @@
     rest = weights - high.astype(jnp.float32)
     middle = rest.astype(jnp.bfloat16)
     low = (rest - middle.astype(jnp.float32)).astype(jnp.bfloat16)
-    count = weights.shape[0]
-    stacked = jnp.dot(
-        jnp.concatenate([high, middle, low], axis=0), rows, preferred_element_type=jnp.float32
+    count = weights.shape[1]
+    stacked = lax.dot_general(
+        jnp.concatenate([high, middle, low], axis=1),
+        rows,
+        (((0,), (0,)), ((), ())),
+        preferred_element_type=jnp.float32,
     )
     return stacked[:count] + (stacked[count : 2 * count] + stacked[2 * count :])
 
 
-def prepare(activations, gain, router, routes, tok_count):
+def prepare(activations, gain, router, routes, place, tok_count):
     rows, width = activations.shape
-    experts = router.shape[1]
+    experts = router.shape[0]
     span = width // tok_count
     half = rows // 2
     per_row = width // (2 * span)
 
-    def body(act_ref, gain_ref, router_ref, route_ref, out_ref, weight_ref, wide, copy):
+    def body(
+        place_ref, act_in, gain_in, router_in, route_in, out_ref, weight_ref,
+        act_ref, gain_ref, router_ref, route_ref, wide, copy, sems,
+    ):
+        load_all(
+            [
+                (act_in, act_ref),
+                (gain_in, gain_ref),
+                (router_in, router_ref),
+                (route_in, route_ref),
+            ],
+            sems,
+        )
         route = route_ref[...]
         hidden = row_norm(act_ref[...].astype(jnp.float32), gain_ref[...])
         picks, first = padded_picks(route, experts)
@@ -353,9 +396,7 @@
                     wide[row : row + 1, column : column + span] = copy[
                         core * half + place : core * half + place + 1, source : source + span
                     ]
-        out_ref[:, :, :width] = (
-            wide[...].astype(jnp.bfloat16).reshape(tok_count, PAD, width)
-        )
+        out_ref[:, :, :width] = wide[...].astype(jnp.bfloat16).reshape(tok_count, PAD, width)
         number = iota((rows, LANES), 0).astype(jnp.float32).astype(jnp.bfloat16)
         out_ref[:, :, width:] = (
             pick_rows(picks, number).astype(jnp.bfloat16).reshape(tok_count, PAD, LANES)
@@ -364,27 +405,83 @@
 
     return pl.pallas_call(
         body,
-        in_specs=[whole_spec()] * 4,
+        in_specs=[index_spec()] + [any_spec()] * 4,
         out_specs=[whole_spec()] * 2,
         out_shape=[
             jax.ShapeDtypeStruct((tok_count, PAD, width + LANES), jnp.bfloat16),
-            jax.ShapeDtypeStruct((rows, tok_count * PAD), jnp.float32),
+            jax.ShapeDtypeStruct((tok_count * PAD, rows), jnp.float32),
         ],
         scratch_shapes=[
+            pltpu.VMEM((rows, width), activations.dtype),
+            pltpu.VMEM((1, width), gain.dtype),
+            pltpu.VMEM(router.shape, router.dtype),
+            pltpu.VMEM(routes.shape, routes.dtype),
             pltpu.VMEM((tok_count * PAD, width), jnp.float32),
             pltpu.VMEM((rows, width), jnp.float32),
+            pltpu.SemaphoreType.DMA((4,)),
         ],
-        compiler_params=pltpu.CompilerParams(vmem_limit_bytes=6 << 20),
+        compiler_params=pltpu.CompilerParams(vmem_limit_bytes=4 << 20),
         name="prepare",
-    )(activations, gain.reshape(1, width), router, routes)
-
-
-def own_tokens(arrived, tok_count, width):
+    )(place, *in_hbm(activations, gain.reshape(1, width), router, routes))
+
+
+def cache_split(cache_part, place, after):
+    rows, width = cache_part.shape
+    count = 8
+    span = width // 2 // count
+
+    def body(index_ref, cache_ref, after_ref, *outs):
+        def piece(other):
+            start = pl.multiple_of((index_ref[2] ^ other) * span, span)
+            return cache_ref[:, pl.ds(start, span)], cache_ref[:, pl.ds(start + width // 2, span)]
+
+        for turn in range(4):
+            for side in range(2):
+                keys, values = piece(2 * turn + side)
+                if turn:
+                    out, base = outs[turn + 1], side * rows
+                else:
+                    out, base = outs[side], 0
+                out[base : base + rows, :span] = keys
+                out[base : base + rows, span:] = values
+
+    shapes = [(rows, 2 * span)] * 2 + [(2 * rows, 2 * span)] * 3
+    return pl.pallas_call(
+        body,
+        in_specs=[index_spec(), whole_spec(), any_spec()],
+        out_specs=[whole_spec()] * 5,
+        out_shape=[jax.ShapeDtypeStruct(one, cache_part.dtype) for one in shapes],
+        compiler_params=pltpu.CompilerParams(vmem_limit_bytes=4 << 20),
+        name="cache_split",
+    )(place, cache_part, after)
+
+
+def cache_relay(near, turned):
+    rows, width = near.shape
+
+    def body(near_ref, *refs):
+        out_ref = refs[-1]
+        out_ref[:rows, :] = near_ref[...]
+        for turn in range(1, 4):
+            out_ref[turn * rows : (turn + 1) * rows, :] = refs[turn - 1][rows:, :]
+
+    return pl.pallas_call(
+        body,
+        in_specs=[whole_spec()] * 4,
+        out_specs=whole_spec(),
+        out_shape=jax.ShapeDtypeStruct((4 * rows, width), near.dtype),
+        compiler_params=pltpu.CompilerParams(vmem_limit_bytes=3 << 20),
+        name="cache_relay",
+    )(near, *turned)
+
+
+def own_tokens(arrived, after, tok_count, width):
     span = width // tok_count
     per_row = width // (2 * span)
     extra = PAD - CAP
 
-    def body(in_ref, out_ref, wide):
+    def body(in_ref, *rest):
+        out_ref, wide = rest[len(after) :]
         for source in range(tok_count):
             rows = in_ref[source, :, :width].astype(jnp.float32)
             for part in range(extra):
@@ -398,84 +495,72 @@
     count = tok_count * extra * per_row
     return pl.pallas_call(
         body,
-        in_specs=[whole_spec()],
+        in_specs=[whole_spec()] + [any_spec()] * len(after),
         out_specs=whole_spec(),
         out_shape=jax.ShapeDtypeStruct((count, 2 * span), jnp.bfloat16),
         scratch_shapes=[pltpu.VMEM((count, 2 * span), jnp.float32)],
         compiler_params=pltpu.CompilerParams(vmem_limit_bytes=4 << 20),
         name="own_tokens",
-    )(arrived)
-
-
-def query_project(arrived, weight, cache_part, tok_count):
+    )(arrived, *after)
+
+
+def query_project(arrived, weight, after, tok_count):
     width = weight.shape[0]
     span = width // tok_count
     slots = tok_count * CAP
-    cache_rows = cache_part.shape[0]
-    height = slots + 2 * cache_rows + PAD
+    height = slots + PAD
     tile = 2 * span
-
-    def body(in_ref, weight_ref, key_ref, value_ref, out_ref, rows, places):
-        step = pl.program_id(0)
-
-        @pl.when(step == 0)
-        def _():
-            every = compact(in_ref[...].reshape(tok_count * PAD, width + LANES))
-            rows[...] = every[:, :width].astype(jnp.bfloat16)
-            local = every[:, width : width + LANES]
-            mine = iota(local.shape, 0)
-            placed = local + ((mine // CAP) * (2 * PAD)).astype(jnp.float32)
-            placed = jnp.where(mine == iota(local.shape, 1), placed, 0.0)
-            places[...] = jnp.broadcast_to(
-                jnp.sum(placed, axis=0, keepdims=True), places.shape
+    steps = width // tile
+
+    def body(in_ref, weight_ref, *rest):
+        out_ref, held, sems = rest[len(after) :]
+        copies = column_stream(weight_ref, held, sems, tile)
+        for one in copies:
+            one.start()
+        every = compact(in_ref[...].reshape(tok_count * PAD, width + LANES))
+        rows = every[:, :width].astype(jnp.bfloat16)
+        local = every[:, width : width + LANES]
+        mine = iota(local.shape, 0)
+        placed = local + ((mine // CAP) * (2 * PAD)).astype(jnp.float32)
+        placed = jnp.where(mine == iota(local.shape, 1), placed, 0.0)
+        line = jnp.broadcast_to(jnp.sum(placed, axis=0, keepdims=True), (PAD, LANES))
+        line = jnp.concatenate([line] * (span // LANES), axis=1).astype(jnp.bfloat16)
+        for step in range(steps):
+            copies[step].wait()
+            query = jnp.dot(rows, held[step], preferred_element_type=jnp.float32).astype(
+                jnp.bfloat16
             )
-
-        query = jnp.dot(rows[...], weight_ref[...], preferred_element_type=jnp.float32).astype(
-            jnp.bfloat16
-        )
-        line = places[...].astype(jnp.bfloat16)
-        for one in range(tile // span):
-            cols = slice(one * span, (one + 1) * span)
-            out_ref[one, :slots, :] = query[:, cols]
-            out_ref[one, slots : slots + cache_rows, :] = key_ref[:, cols]
-            out_ref[one, slots + cache_rows : slots + 2 * cache_rows, :] = value_ref[:, cols]
-            out_ref[one, slots + 2 * cache_rows :, :] = jnp.concatenate(
-                [line] * (span // LANES), axis=1
-            )
-
-    steps = width // tile
-    return pl.pallas_call(
-        body,
-        grid=(steps,),
-        in_specs=[
-            pl.BlockSpec(arrived.shape, lambda step: (0, 0, 0)),
-            pl.BlockSpec((width, tile), lambda step: (0, step)),
-            pl.BlockSpec((cache_rows, tile), lambda step: (0, step)),
-            pl.BlockSpec((cache_rows, tile), lambda step: (0, step + steps)),
-        ],
-        out_specs=pl.BlockSpec((tile // span, height, span), lambda step: (step, 0, 0)),
+            for one in range(tile // span):
+                place = step * (tile // span) + one
+                out_ref[place, :slots, :] = query[:, one * span : (one + 1) * span]
+                out_ref[place, slots:, :] = line
+
+    return pl.pallas_call(
+        body,
+        in_specs=[whole_spec(), any_spec()] + [any_spec()] * len(after),
+        out_specs=whole_spec(),
         out_shape=jax.ShapeDtypeStruct((tok_count, height, span), jnp.bfloat16),
         scratch_shapes=[
-            pltpu.VMEM((slots, width), jnp.bfloat16),
-            pltpu.VMEM((PAD, LANES), jnp.float32),
+            pltpu.VMEM((steps, width, tile), jnp.bfloat16),
+            pltpu.SemaphoreType.DMA((steps,)),
         ],
-        compiler_params=pltpu.CompilerParams(vmem_limit_bytes=8 << 20),
+        compiler_params=pltpu.CompilerParams(vmem_limit_bytes=14 << 20),
         name="query_project",
-    )(arrived, weight, cache_part, cache_part)
-
-
-def key_value_parts(tokens, weight, sibling, chip):
+    )(arrived, *in_hbm(weight), *after)
+
+
+def key_value_parts(tokens, weight, sibling, place):
     rows, depth = tokens[0].shape
     half = depth // 2
     quarter = weight.shape[1] // 4
     count = len(tokens)
 
-    def body(chip_ref, *refs):
+    def body(place_ref, *refs):
         token_refs, weight_ref, sibling_ref = refs[:count], refs[count], refs[count + 1]
         outs = refs[count + 2 :]
         stacked = jnp.concatenate([one[...] for one in token_refs], axis=0)
         for turn in range(4):
-            start = pl.multiple_of((chip_ref[0] ^ turn) * quarter, quarter)
+            start = pl.multiple_of(((place_ref[2] // 2) ^ turn) * quarter, quarter)
             part = jnp.dot(
                 stacked[:, :half],
                 weight_ref[:, pl.ds(start, quarter)],
@@ -498,18 +583,19 @@
         out_shape=shapes,
         compiler_params=pltpu.CompilerParams(vmem_limit_bytes=8 << 20),
         name="key_value_parts",
-    )(chip.reshape(1), *tokens, weight, sibling)
-
-
-def key_value_sum(parts, own_req, core):
+    )(place, *tokens, weight, sibling)
+
+
+def key_value_sum(parts, place):
     rows, quarter = parts[0].shape
     block = rows // 4
 
     def body(place_ref, *refs):
         ins, outs = refs[:4], refs[4:]
-        source = (place_ref[0] // 2) * 2 + place_ref[1]
+        req = place_ref[1]
+        source = (req // 2) * 2 + place_ref[2] % 2
         for turn in range(4):
-            start = pl.multiple_of((place_ref[0] ^ source ^ turn) * block, block)
+            start = pl.multiple_of((req ^ source ^ turn) * block, block)
             total = ins[0][pl.ds(start, block), :]
             for one in ins[1:]:
                 total = total + one[pl.ds(start, block), :].astype(jnp.float32)
@@ -522,22 +608,23 @@
         out_shape=[jax.ShapeDtypeStruct((block, quarter), jnp.bfloat16)] * 4,
         compiler_params=pltpu.CompilerParams(vmem_limit_bytes=4 << 20),
         name="key_value_sum",
-    )(jnp.stack([own_req, core]), *parts)
-
-
-def attention(message, scalars, fresh_blocks, cache_rows):
+    )(place, *parts)
+
+
+def attention(message, scalars, fresh_blocks, own, turned, relayed):
     blocks, _, span = message.shape
     heads = span // HEAD_DIM
     slots = blocks * CAP
     fresh_rows = fresh_blocks[0].shape[0]
     half = fresh_rows // blocks
-    height = slots + 2 * 2 * half * 2
+    cache_rows = own.shape[0]
     scale = 1.0 / math.sqrt(HEAD_DIM)
     contract = (((1,), (1,)), ((), ()))
 
     def body(scalar_ref, in_ref, *refs):
-        fresh_refs, out_ref = refs[:4], refs[4]
-        limit, req = scalar_ref[0], scalar_ref[1]
+        fresh_refs, own_ref, turned_refs, relay_ref = refs[:4], refs[4], refs[5:8], refs[8]
+        out_ref = refs[9]
+        limit, req, tok = scalar_ref[0], scalar_ref[1], scalar_ref[2]
         pieces = []
         for source in range(4):
             picked = fresh_refs[3][...]
@@ -546,21 +633,23 @@
             pieces.append(picked)
         new_keys = jnp.concatenate(pieces[:2], axis=0)
         new_values = jnp.concatenate(pieces[2:], axis=0)
-        cache_usable = iota((1, blocks * cache_rows), 1) < limit
+        key_row = iota((1, blocks * cache_rows), 1)
+        key_block = key_row // cache_rows
+        key_source = ((key_block % 4) * 2 + key_block // 4) ^ tok
+        cache_usable = key_source * cache_rows + key_row % cache_rows < limit
         new_row = iota((1, 2 * fresh_rows), 1)
         within = new_row % fresh_rows
         new_place = (within // half) * (2 * half) + (new_row // fresh_rows) * half + within % half
         places = []
         for expert in range(blocks):
-            line = in_ref[expert, slots + 2 * cache_rows :, :LANES].astype(jnp.float32)[0:1]
+            line = in_ref[expert, slots:, :LANES].astype(jnp.float32)[0:1]
             chosen = iota((slots, LANES), 0) == iota((slots, LANES), 1)
             places.append(jnp.sum(jnp.where(chosen, line, 0.0), axis=1, keepdims=True))
         new_usable = new_place <= jnp.concatenate(places, axis=0).astype(jnp.int32)
         flat = in_ref[:, :slots, :].reshape(blocks * slots, span)
-        keys = in_ref[:, slots : slots + cache_rows, :].reshape(blocks * cache_rows, span)
-        values = in_ref[:, slots + cache_rows : slots + 2 * cache_rows, :].reshape(
-            blocks * cache_rows, span
-        )
+        cached = [own_ref] + [one.at[:cache_rows] for one in turned_refs] + [relay_ref]
+        keys = jnp.concatenate([one[:, :span] for one in cached], axis=0)
+        values = jnp.concatenate([one[:, span:] for one in cached], axis=0)
         for head in range(heads):
             cols = slice(head * HEAD_DIM, (head + 1) * HEAD_DIM)
             query = flat[:, cols]
@@ -595,12 +684,12 @@
 
     return pl.pallas_call(
         body,
-        in_specs=[index_spec()] + [whole_spec()] * 5,
+        in_specs=[index_spec()] + [whole_spec()] * 10,
         out_specs=whole_spec(),
         out_shape=jax.ShapeDtypeStruct((blocks, slots + 4 * half, span), jnp.bfloat16),
         compiler_params=pltpu.CompilerParams(vmem_limit_bytes=14 << 20),
         name="attention",
-    )(scalars, message, *fresh_blocks)
+    )(scalars, message, *fresh_blocks, own, *turned, relayed)
 
 
 def output_project(arrived, weight, query_rows):
@@ -609,45 +698,46 @@
     width = weight.shape[1]
     tile = width // 4
 
-    def body(in_ref, weight_ref, out_ref, fresh_ref, rows):
-        @pl.when(pl.program_id(0) == 0)
-        def _():
-            for block in range(blocks):
-                cols = slice(block * span, (block + 1) * span)
-                rows[:, cols] = spread(in_ref[block, :slots, :]).astype(jnp.bfloat16)
-                fresh_ref[:, cols] = in_ref[block, slots : slots + query_rows, :]
-                fresh_ref[:, block * span + width : (block + 1) * span + width] = in_ref[
-                    block, slots + query_rows :, :
-                ]
-
-        part = jnp.dot(rows[...], weight_ref[...], preferred_element_type=jnp.float32)
-        out_ref[...] = part.astype(jnp.bfloat16).reshape(blocks, PAD, tile)
-
-    return pl.pallas_call(
-        body,
-        grid=(width // tile,),
-        in_specs=[
-            pl.BlockSpec(arrived.shape, lambda step: (0, 0, 0)),
-            pl.BlockSpec((blocks * span, tile), lambda step: (0, step)),
-        ],
-        out_specs=[
-            pl.BlockSpec((blocks, PAD, tile), lambda step: (0, 0, step)),
-            pl.BlockSpec((query_rows, 2 * width), lambda step: (0, 0)),
-        ],
+    def body(in_ref, weight_ref, out_ref, fresh_ref, held, sems):
+        copies = column_stream(weight_ref, held, sems, tile)
+        for one in copies:
+            one.start()
+        rows = []
+        for block in range(blocks):
+            cols = slice(block * span, (block + 1) * span)
+            rows.append(spread(in_ref[block, :slots, :]).astype(jnp.bfloat16))
+            fresh_ref[:, cols] = in_ref[block, slots : slots + query_rows, :]
+            fresh_ref[:, block * span + width : (block + 1) * span + width] = in_ref[
+                block, slots + query_rows :, :
+            ]
+        rows = jnp.concatenate(rows, axis=1)
+        for step in range(width // tile):
+            cols = slice(step * tile, (step + 1) * tile)
+            copies[step].wait()
+            part = jnp.dot(rows, held[step], preferred_element_type=jnp.float32)
+            out_ref[:, :, cols] = part.astype(jnp.bfloat16).reshape(blocks, PAD, tile)
+
+    return pl.pallas_call(
+        body,
+        in_specs=[whole_spec(), any_spec()],
+        out_specs=[whole_spec()] * 2,
         out_shape=[
             jax.ShapeDtypeStruct((blocks, PAD, width), jnp.bfloat16),
             jax.ShapeDtypeStruct((query_rows, 2 * width), jnp.bfloat16),
         ],
-        scratch_shapes=[pltpu.VMEM((blocks * PAD, blocks * span), jnp.bfloat16)],
-        compiler_params=pltpu.CompilerParams(vmem_limit_bytes=8 << 20),
+        scratch_shapes=[
+            pltpu.VMEM((width // tile, blocks * span, tile), jnp.bfloat16),
+            pltpu.SemaphoreType.DMA((width // tile,)),
+        ],
+        compiler_params=pltpu.CompilerParams(vmem_limit_bytes=14 << 20),
         name="output_project",
-    )(arrived, weight)
+    )(arrived, *in_hbm(weight))
 
 
 def middle(activations, arrived, weights, gain, router, routes):
     rows, width = activations.shape
     blocks = arrived.shape[0]
-    experts = router.shape[1]
+    experts = router.shape[0]
 
     def body(act_ref, in_ref, old_ref, gain_ref, router_ref, route_ref, out_ref, mix_ref, new_ref):
         route = route_ref[...]
@@ -668,9 +758,9 @@
         out_shape=[
             jax.ShapeDtypeStruct((blocks, PAD, width), jnp.bfloat16),
             jax.ShapeDtypeStruct((rows, width), jnp.bfloat16),
-            jax.ShapeDtypeStruct((rows, blocks * PAD), jnp.float32),
+            jax.ShapeDtypeStruct((blocks * PAD, rows), jnp.float32),
         ],
-        compiler_params=pltpu.CompilerParams(vmem_limit_bytes=6 << 20),
+        compiler_params=pltpu.CompilerParams(vmem_limit_bytes=4 << 20),
         name="middle",
     )(activations, arrived, weights, gain.reshape(1, width), router, routes)
 
@@ -696,54 +786,63 @@
     blocks, _, width = arrived.shape
     count = blocks * CAP
     units = down_piece.shape[0]
-    tile = 512
+    tile = FF_TILE
     steps = units // tile
-
-    def body(in_ref, gate_ref, up_ref, down_ref, out_ref, rows, total):
-        step = pl.program_id(0)
-
-        @pl.when(step == 0)
-        def _():
-            total[...] = jnp.zeros_like(total)
-            rows[...] = compact(in_ref[...].reshape(blocks * PAD, width)).astype(jnp.bfloat16)
-
-        row = rows[...]
-        gate = jnp.dot(row, gate_ref[...], preferred_element_type=jnp.float32)
-        up = jnp.dot(row, up_ref[...], preferred_element_type=jnp.float32)
-        active = (gate / (1.0 + jnp.exp(-gate)) * up).astype(jnp.bfloat16)
-        total[...] += jnp.dot(active, down_ref[...], preferred_element_type=jnp.float32)
-
-        @pl.when(step == steps - 1)
-        def _():
-            out_ref[...] = (
-                spread(total[...].astype(jnp.bfloat16))
-                .astype(jnp.bfloat16)
-                .reshape(blocks, PAD, width)
-            )
-
-    return pl.pallas_call(
-        body,
-        grid=(steps,),
-        in_specs=[
-            pl.BlockSpec(arrived.shape, lambda step: (0, 0, 0)),
-            pl.BlockSpec((width, tile), lambda step: (0, step)),
-            pl.BlockSpec((width, tile), lambda step: (0, step + steps)),
-            pl.BlockSpec((tile, width), lambda step: (step, 0)),
-        ],
-        out_specs=pl.BlockSpec(arrived.shape, lambda step: (0, 0, 0)),
+    slots = 4
+
+    def body(in_ref, gate_ref, down_ref, out_ref, gates, ups, downs, sems):
+        def copies(step):
+            slot = step % slots
+            return [
+                pltpu.make_async_copy(
+                    gate_ref.at[:, pl.ds(step * tile, tile)], gates.at[slot], sems.at[slot, 0]
+                ),
+                pltpu.make_async_copy(
+                    gate_ref.at[:, pl.ds(units + step * tile, tile)],
+                    ups.at[slot],
+                    sems.at[slot, 1],
+                ),
+                pltpu.make_async_copy(
+                    down_ref.at[pl.ds(step * tile, tile), :], downs.at[slot], sems.at[slot, 2]
+                ),
+            ]
+
+        for step in range(slots):
+            for one in copies(step):
+                one.start()
+        rows = compact(in_ref[...].reshape(blocks * PAD, width)).astype(jnp.bfloat16)
+        total = jnp.zeros((count, width), jnp.float32)
+        for step in range(steps):
+            slot = step % slots
+            gate_copy, up_copy, down_copy = copies(step)
+            gate_copy.wait()
+            gate = jnp.dot(rows, gates[slot], preferred_element_type=jnp.float32)
+            up_copy.wait()
+            up = jnp.dot(rows, ups[slot], preferred_element_type=jnp.float32)
+            active = (gate / (1.0 + jnp.exp(-gate)) * up).astype(jnp.bfloat16)
+            down_copy.wait()
+            total = total + jnp.dot(active, downs[slot], preferred_element_type=jnp.float32)
+            if step + slots < steps:
+                for one in copies(step + slots):
+                    one.start()
+        out_ref[...] = (
+            spread(total.astype(jnp.bfloat16)).astype(jnp.bfloat16).reshape(blocks, PAD, width)
+        )
+
+    return pl.pallas_call(
+        body,
+        in_specs=[whole_spec(), any_spec(), any_spec()],
+        out_specs=whole_spec(),
         out_shape=jax.ShapeDtypeStruct(arrived.shape, jnp.bfloat16),
         scratch_shapes=[
-            pltpu.VMEM((count, width), jnp.bfloat16),
-            pltpu.VMEM((count, width), jnp.float32),
+            pltpu.VMEM((slots, width, tile), jnp.bfloat16),
+            pltpu.VMEM((slots, width, tile), jnp.bfloat16),
+            pltpu.VMEM((slots, tile, width), jnp.bfloat16),
+            pltpu.SemaphoreType.DMA((slots, 3)),
         ],
-        compiler_params=pltpu.CompilerParams(vmem_limit_bytes=20 << 20),
-        cost_estimate=pl.CostEstimate(
-            flops=6 * count * width * units,
-            transcendentals=count * units,
-            bytes_accessed=6 * width * units,
-        ),
+        compiler_params=pltpu.CompilerParams(vmem_limit_bytes=32 << 20),
         name="feedforward",
-    )(arrived, gate_piece, gate_piece, down_piece)
+    )(arrived, *in_hbm(gate_piece, down_piece))
 
 
 def local_heads(
@@ -766,28 +865,37 @@
     req_count = lax.axis_size("req")
     tok_index = lax.axis_index("tok")
     req_index = lax.axis_index("req")
-    chip, core = tok_index // 2, tok_index % 2
     query_rows, width = activations.shape[1:]
-    cache_rows = cache_entries.shape[1]
-
+
+    attn_routes = attention_routes[0].T
+    ffn_routes = feedforward_routes[0].T
+    place = jnp.stack([cache_lengths[0], req_index, tok_index])
     message, attn_weights = prepare(
-        activations[0], attention_gain, attention_router, attention_routes[0], tok_count
+        activations[0], attention_gain, attention_router.T, attn_routes, place, tok_count
     )
     arrived = swap_all(message, "tok")
-    sibling = permute(key_value_weight, "tok", [(one, one ^ 1) for one in range(tok_count)])
-    mine = own_tokens(arrived, tok_count, width)
+    own_block, near, *turned = cache_split(cache_entries[0], place, attn_weights)
+    turned = [
+        permute(turned[turn - 1], "tok", [(one, one ^ (2 * turn)) for one in range(tok_count)])
+        for turn in range(1, 4)
+    ]
+    pair = [(one, one ^ 1) for one in range(tok_count)]
+    sibling = permute(key_value_weight, "tok", pair)
+    projected = query_project(arrived, query_weight[0], [], tok_count)
+    projected, *turned = lax.optimization_barrier((projected, *turned))
+    queries = swap_all(projected, "tok")
+    mine = own_tokens(arrived, [projected], tok_count, width)
+    relayed = permute(cache_relay(near, turned), "tok", pair)
     tokens = [mine] + [
         permute(mine, "req", [(one, one ^ turn) for one in range(req_count)])
         for turn in range(1, req_count)
     ]
-    queries = query_project(arrived, query_weight[0], cache_entries[0], tok_count)
-    queries = swap_all(queries, "tok")
-    parts = key_value_parts(tokens, key_value_weight, sibling, chip)
+    parts = key_value_parts(tokens, key_value_weight, sibling, place)
     parts = [parts[0]] + [
         permute(parts[turn], "tok", [(one, one ^ (2 * turn)) for one in range(tok_count)])
         for turn in range(1, 4)
     ]
-    sums = key_value_sum(parts, req_index, core)
+    sums = key_value_sum(parts, place)
     fresh_blocks = []
     for turn in range(4):
         pairs = []
@@ -796,8 +904,7 @@
             dest = ((r // 2) * 2 + t % 2) ^ turn
             pairs.append((one, dest * tok_count + 4 * (r % 2) + t // 2))
         fresh_blocks.append(permute(sums[turn], ("req", "tok"), pairs))
-    scalars = jnp.stack([cache_lengths[0], req_index])
-    attended = attention(queries, scalars, fresh_blocks, cache_rows)
+    attended = attention(queries, place, fresh_blocks, own_block, turned, relayed)
     attended = swap_all(attended, "tok")
     parts_out, new_keys_values = output_project(attended, output_weight[0], query_rows)
     output_back = swap_all(parts_out, "tok")
@@ -806,8 +913,8 @@
         output_back,
         attn_weights,
         feedforward_gain,
-        feedforward_router,
-        feedforward_routes[0],
+        feedforward_router.T,
+        ffn_routes,
     )
     received = swap_all(ffn_send, "tok")
     expert_parts = feedforward(received, gate_up[0], down_weight[0])

time: 169 us -> 152 us (0.90)
  local copies, waits for them, and re-layouts: 20.1 us -> 2.1 us
  waiting for transfers between devices: 31 us -> 24.3 us
  starting transfers between devices: 25.6 us -> 32 us
  Pallas kernels: 33.9 us -> 39.3 us
  blocking collectives: 55.7 us -> 51.9 us
    unnamed x24 -> x12, local copies, waits for them, and re-layouts: 19.3 us -> 2.1 us
    all_to_all x2, waiting for transfers between devices: 9.28 us -> 4.05 us  [swap_all(): return lax.all_to_all(values, axis, split_axis=0, concat_axis=0, tiled=True)]
    pallas_call x6 -> x8, Pallas kernels: 31.3 us -> 36.1 us  [the longest x1 22.1 us: feedforward(): pl.pallas_call(body, in_specs=[whole_spec(), any_spec(), any_spec()], out...]
    all_to_all x4, blocking collectives: 55.7 us -> 51.9 us  [swap_all(): return lax.all_to_all(values, axis, split_axis=0, concat_axis=0, tiled=True)]
    all_to_all x2, starting transfers between devices: 6.95 us -> 10.5 us  [swap_all(): return lax.all_to_all(values, axis, split_axis=0, concat_axis=0, tiled=True)]
    ppermute x11 -> x15, starting transfers between devices: 18.6 us -> 21.5 us  [permute(): return lax.ppermute(values, axis, pairs)]
    ppermute x11 -> x15, waiting for transfers between devices: 21.7 us -> 20.2 us  [permute(): return lax.ppermute(values, axis, pairs)]
  transfers between devices with their start and end apart: 13 -> 17, of which waited for: 8 -> 10; matrix products, arithmetic and copies ran while one was open for 0% -> 0% of each run, Pallas kernels for 1% -> 5%
where the time goes in v2:
time: 152 us; the launch traced here: 151 us
  blocking collectives  51.9 us (34%)
  Pallas kernels  39.3 us (26%)
  starting transfers between devices  32 us (21%)
  waiting for transfers between devices  24.3 us (16%)
  local copies, waits for them, and re-layouts  2.1 us (1%)
    all_to_all x4, blocking collectives, swap_all(): return lax.all_to_all(values, axis, split_axis=0, concat_axis=0, tiled=True)  51.9 us
    pallas_call x1, Pallas kernels, feedforward(): pl.pallas_call(body, in_specs=[whole_spec(), any_spec(), any_spec()], out...  22.1 us
    ppermute x15, starting transfers between devices, permute(): return lax.ppermute(values, axis, pairs)  21.5 us
    ppermute x15, waiting for transfers between devices, permute(): return lax.ppermute(values, axis, pairs)  20.2 us
    all_to_all x2, starting transfers between devices, swap_all(): return lax.all_to_all(values, axis, split_axis=0, concat_axis=0, tiled=True)  10.5 us
    pallas_call x1, Pallas kernels, query_project(): pl.pallas_call(body, in_specs=[whole_spec(), any_spec()] + [any_spec()] *...  4.75 us
    pallas_call x1, Pallas kernels, output_project(): pl.pallas_call(body, in_specs=[whole_spec(), any_spec()], out_specs=[whol...  4.25 us
    all_to_all x2, waiting for transfers between devices, swap_all(): return lax.all_to_all(values, axis, split_axis=0, concat_axis=0, tiled=True)  4.05 us
  transfers between devices with their start and end apart: 17, of which 10 were waited for; matrix products, arithmetic and copies ran while one was open for 0% of the time, Pallas kernels for 5%

profile of v2, /device:TPU:0, one launch (start us, length us, event | category | flops | bytes accessed | tf_op | source)
XLA Modules:
  0.0 151.1 jit_solution(14808396571830685189)
XLA Ops:
  1.4 2.5 %prepare.1 = (bf16[8,8,2176]{2,1,0:T(8,128)(2,1)}, f32[64,16]{1,0:T(8,128)S(1)}) custom-call(s32[3]{0:T(128)S(1)} %pad_add_fusion.place_ref.index_ref.scalar_ref, bf16[16,2048]{1,0:T(8,128)(2,1)} %bitcast.21, f32[1,2048]{1,0:T(1,128)} %bitcast.32, bf16[8,2048]{1,0:T(8,128)(2,1)} %bitcast.31, s32[2,16]{1,0:T(2,128)} %bitcast.33), custom_call_target="tpu_custom_call" | custom-call | tf_op jit(solution)/shard_map/prepare/pallas_call | solution.py:406
  4.0 6.3 %all-to-all-start = ((bf16[8,8,2176]{2,1,0:T(8,128)(2,1)}), bf16[8,8,2176]{2,1,0:T(8,128)(2,1)S(1)}, u32[]{:S(2)}, u32[]{:S(2)}) async-start(bf16[8,8,2176]{2,1,0:T(8,128)(2,1)} %get-tuple-element.26), calls=%async_computation | async-start | bytes 557056 | tf_op jit(solution)/shard_map/all_to_all | solution.py:260
  10.8 1.0 copy-done.1
  12.5 1.7 %collective-permute-start = (bf16[128,512]{1,0:T(8,128)(2,1)S(1)}, bf16[128,512]{1,0:T(8,128)(2,1)S(1)}, u32[]{:S(2)}, u32[]{:S(2)}) collective-permute-start(bf16[128,512]{1,0:T(8,128)(2,1)S(1)} %get-tuple-element.28), channel_id=1, source_target_pairs={{0,2},{1,3},{2,0},{3,1},{4,6},{5,7},{6,4},{7,5},{8,10},{9,11},{10,... | collective-permute-start | bytes 393224 | tf_op jit(solution)/shard_map/ppermute | solution.py:256
  14.2 2.4 %collective-permute-start.1 = (bf16[128,512]{1,0:T(8,128)(2,1)S(1)}, bf16[128,512]{1,0:T(8,128)(2,1)S(1)}, u32[]{:S(2)}, u32[]{:S(2)}) collective-permute-start(bf16[128,512]{1,0:T(8,128)(2,1)S(1)} %get-tuple-element.29), channel_id=1, source_target_pairs={{0,4},{1,5},{2,6},{3,7},{4,0},{5,1},{6,2},{7,3},{8,12},{9,13},{10,... | collective-permute-start | bytes 393224 | tf_op jit(solution)/shard_map/ppermute | solution.py:256
  16.9 4.0 %all-to-all-done.in_ref = bf16[8,8,2176]{2,1,0:T(8,128)(2,1)S(1)} async-done(((bf16[8,8,2176]{2,1,0:T(8,128)(2,1)}), bf16[8,8,2176]{2,1,0:T(8,128)(2,1)S(1)}, u32[]{:S(2)}, u32[]{:S(2)}) %all-to-all-start) | async-done | bytes 278560 | tf_op jit(solution)/shard_map/all_to_all | solution.py:260
  21.0 4.8 %query_project.1.rest_0_ = bf16[8,56,256]{2,1,0:T(8,128)(2,1)} custom-call(bf16[8,8,2176]{2,1,0:T(8,128)(2,1)S(1)} %all-to-all-done.in_ref, bf16[2048,2048]{1,0:T(8,128)(2,1)} %bitcast.28), custom_call_target="tpu_custom_call" | custom-call | tf_op jit(solution)/shard_map/query_project/pallas_call | solution.py:538
  25.7 3.6 %collective-permute-done.1.refs_1_.refs_6_ = bf16[128,512]{1,0:T(8,128)(2,1)S(1)} collective-permute-done((bf16[128,512]{1,0:T(8,128)(2,1)S(1)}, bf16[128,512]{1,0:T(8,128)(2,1)S(1)}, u32[]{:S(2)}, u32[]{:S(2)}) %collective-permute-start.1) | collective-permute-done | bytes 131104 | tf_op jit(solution)/shard_map/ppermute | solution.py:256
  29.3 4.2 %all-to-all-start.1 = ((bf16[8,56,256]{2,1,0:T(8,128)(2,1)}), bf16[8,56,256]{2,1,0:T(8,128)(2,1)S(1)}, u32[]{:S(2)}, u32[]{:S(2)}) async-start(bf16[8,56,256]{2,1,0:T(8,128)(2,1)} %query_project.1.rest_0_), calls=%async_computation.1 | async-start | bytes 458752 | tf_op jit(solution)/shard_map/all_to_all | solution.py:260
  34.2 1.6 %collective-permute-start.3 = (bf16[64,512]{1,0:T(8,128)(2,1)S(1)}, bf16[64,512]{1,0:T(8,128)(2,1)S(1)}, u32[]{:S(2)}, u32[]{:S(2)}) collective-permute-start(bf16[64,512]{1,0:T(8,128)(2,1)S(1)} %own_tokens.1.refs_0_), channel_id=1, source_target_pairs={{0,8},{8,0},{16,24},{24,16},{1,9},{9,1},{17,25},{25,17},{2,10},{10... | collective-permute-start | bytes 196616 | tf_op jit(solution)/shard_map/ppermute | solution.py:256
  35.7 1.5 %collective-permute-start.4 = (bf16[64,512]{1,0:T(8,128)(2,1)S(1)}, bf16[64,512]{1,0:T(8,128)(2,1)S(1)}, u32[]{:S(2)}, u32[]{:S(2)}) collective-permute-start(bf16[64,512]{1,0:T(8,128)(2,1)S(1)} %own_tokens.1.refs_0_), channel_id=1, source_target_pairs={{0,16},{8,24},{16,0},{24,8},{1,17},{9,25},{17,1},{25,9},{2,18},{10... | collective-permute-start | bytes 196616 | tf_op jit(solution)/shard_map/ppermute | solution.py:256
  37.7 0.8 collective-permute-done.3.refs_1_
  38.5 1.5 collective-permute-done.4.refs_2_
  40.0 2.4 %collective-permute-done.5.refs_3_ = bf16[64,512]{1,0:T(8,128)(2,1)S(1)} collective-permute-done((bf16[64,512]{1,0:T(8,128)(2,1)S(1)}, bf16[64,512]{1,0:T(8,128)(2,1)S(1)}, u32[]{:S(2)}, u32[]{:S(2)}) %collective-permute-start.5) | collective-permute-done | bytes 65568 | tf_op jit(solution)/shard_map/ppermute | solution.py:256
  42.4 1.0 copy-done
  43.5 1.0 key_value_parts.1
  44.5 1.7 %collective-permute-start.7 = (bf16[256,256]{1,0:T(8,128)(2,1)S(1)}, bf16[256,256]{1,0:T(8,128)(2,1)S(1)}, u32[]{:S(2)}, u32[]{:S(2)}) collective-permute-start(bf16[256,256]{1,0:T(8,128)(2,1)S(1)} %get-tuple-element.33), channel_id=1, source_target_pairs={{0,2},{1,3},{2,0},{3,1},{4,6},{5,7},{6,4},{7,5},{8,10},{9,11},{10,... | collective-permute-start | bytes 393224 | tf_op jit(solution)/shard_map/ppermute | solution.py:256
  46.2 2.4 %collective-permute-start.8 = (bf16[256,256]{1,0:T(8,128)(2,1)S(1)}, bf16[256,256]{1,0:T(8,128)(2,1)S(1)}, u32[]{:S(2)}, u32[]{:S(2)}) collective-permute-start(bf16[256,256]{1,0:T(8,128)(2,1)S(1)} %get-tuple-element.34), channel_id=1, source_target_pairs={{0,4},{1,5},{2,6},{3,7},{4,0},{5,1},{6,2},{7,3},{8,12},{9,13},{10,... | collective-permute-start | bytes 393224 | tf_op jit(solution)/shard_map/ppermute | solution.py:256
  48.9 1.8 %collective-permute-done.7.refs_1_ = bf16[256,256]{1,0:T(8,128)(2,1)S(1)} collective-permute-done((bf16[256,256]{1,0:T(8,128)(2,1)S(1)}, bf16[256,256]{1,0:T(8,128)(2,1)S(1)}, u32[]{:S(2)}, u32[]{:S(2)}) %collective-permute-start.7) | collective-permute-done | bytes 131104 | tf_op jit(solution)/shard_map/ppermute | solution.py:256
  50.8 7.2 %collective-permute-done.8.refs_2_ = bf16[256,256]{1,0:T(8,128)(2,1)S(1)} collective-permute-done((bf16[256,256]{1,0:T(8,128)(2,1)S(1)}, bf16[256,256]{1,0:T(8,128)(2,1)S(1)}, u32[]{:S(2)}, u32[]{:S(2)}) %collective-permute-start.8) | collective-permute-done | bytes 131104 | tf_op jit(solution)/shard_map/ppermute | solution.py:256
  59.2 5.6 %collective-permute-start.11 = (bf16[64,256]{1,0:T(8,128)(2,1)S(1)}, bf16[64,256]{1,0:T(8,128)(2,1)S(1)}, u32[]{:S(2)}, u32[]{:S(2)}) collective-permute-start(bf16[64,256]{1,0:T(8,128)(2,1)S(1)} %get-tuple-element.37), channel_id=1, source_target_pairs={{0,8},{1,0},{2,9},{3,1},{4,10},{5,2},{6,11},{7,3},{8,12},{9,4},{10... | collective-permute-start | bytes 98312 | tf_op jit(solution)/shard_map/ppermute | solution.py:256
  65.5 1.0 collective-permute-start.13
  66.6 2.4 %collective-permute-done.12.refs_2_ = bf16[64,256]{1,0:T(8,128)(2,1)S(1)} collective-permute-done((bf16[64,256]{1,0:T(8,128)(2,1)S(1)}, bf16[64,256]{1,0:T(8,128)(2,1)S(1)}, u32[]{:S(2)}, u32[]{:S(2)}) %collective-permute-start.12) | collective-permute-done | bytes 32800 | tf_op jit(solution)/shard_map/ppermute | solution.py:256
  69.4 1.8 %attention.1 = bf16[8,80,256]{2,1,0:T(8,128)(2,1)S(1)} custom-call(s32[3]{0:T(128)S(1)} %pad_add_fusion.place_ref.index_ref.scalar_ref, bf16[8,56,256]{2,1,0:T(8,128)(2,1)S(1)} %all-to-all-done.1.in_ref, bf16[64,256]{1,0:T(8,128)(2,1)S(1)} %collective-permute-done.10.refs_0_, bf16[64,256]{1,0:T(8,128)(2,1)S(1)} %collective-permute-done.11.refs_1_, ...), custom_call_target="tpu_custom_call" | custom-call | tf_op jit(solution)/shard_map/attention/pallas_call | solution.py:685
  71.2 15.4 %all_to_all.30.in_ref = bf16[8,80,256]{2,1,0:T(8,128)(2,1)S(1)} all-to-all(bf16[8,80,256]{2,1,0:T(8,128)(2,1)S(1)} %attention.1), channel_id=1, replica_groups=mesh['req'=4,'tok'=8] {'tok'}, dimensions={0} | all-to-all | bytes 655360 | tf_op jit(solution)/shard_map/all_to_all | solution.py:260
  86.6 4.2 %output_project.1 = (bf16[8,8,2048]{2,1,0:T(8,128)(2,1)S(1)}, bf16[16,4096]{1,0:T(8,128)(2,1)}) custom-call(bf16[8,80,256]{2,1,0:T(8,128)(2,1)S(1)} %all_to_all.30.in_ref, bf16[2048,2048]{1,0:T(8,128)(2,1)} %bitcast.29), custom_call_target="tpu_custom_call" | custom-call | tf_op jit(solution)/shard_map/output_project/pallas_call | solution.py:720
  90.9 12.1 %all_to_all.31.in_ref = bf16[8,8,2048]{2,1,0:T(8,128)(2,1)S(1)} all-to-all(bf16[8,8,2048]{2,1,0:T(8,128)(2,1)S(1)} %get-tuple-element.45), channel_id=1, replica_groups=mesh['req'=4,'tok'=8] {'tok'}, dimensions={0} | all-to-all | bytes 524288 | tf_op jit(solution)/shard_map/all_to_all | solution.py:260
  103.1 0.7 middle.1
  103.7 12.1 %all_to_all.32.in_ref = bf16[8,8,2048]{2,1,0:T(8,128)(2,1)S(1)} all-to-all(bf16[8,8,2048]{2,1,0:T(8,128)(2,1)S(1)} %get-tuple-element.47), channel_id=1, replica_groups=mesh['req'=4,'tok'=8] {'tok'}, dimensions={0} | all-to-all | bytes 524288 | tf_op jit(solution)/shard_map/all_to_all | solution.py:260
  115.9 22.1 %feedforward.1 = bf16[8,8,2048]{2,1,0:T(8,128)(2,1)S(1)} custom-call(bf16[8,8,2048]{2,1,0:T(8,128)(2,1)S(1)} %all_to_all.32.in_ref, bf16[2048,11264]{1,0:T(8,128)(2,1)} %bitcast.26, bf16[5632,2048]{1,0:T(8,128)(2,1)} %bitcast.27), custom_call_target="tpu_custom_call" | custom-call | tf_op jit(solution)/shard_map/feedforward/pallas_call | solution.py:832
  138.0 12.1 %all_to_all.33.in_ref = bf16[8,8,2048]{2,1,0:T(8,128)(2,1)S(1)} all-to-all(bf16[8,8,2048]{2,1,0:T(8,128)(2,1)S(1)} %feedforward.1), channel_id=1, replica_groups=mesh['req'=4,'tok'=8] {'tok'}, dimensions={0} | all-to-all | bytes 524288 | tf_op jit(solution)/shard_map/all_to_all | solution.py:260
  150.2 0.9 finish.1
  (31 shorter events, 5.5 us)
Async XLA Ops:
  0.6 102.4 %copy-start.2 = (bf16[1,16,2048]{2,1,0:T(8,128)(2,1)S(1)}, bf16[1,16,2048]{2,1,0:T(8,128)(2,1)}, u32[]{:S(2)}) copy-start(bf16[1,16,2048]{2,1,0:T(8,128)(2,1)} %param.14) | copy-start | bytes 196612
  0.6 102.4 %copy-start.4 = (f32[2048]{0:T(1024)S(1)}, f32[2048]{0:T(1024)}, u32[]{:S(2)}) copy-start(f32[2048]{0:T(1024)} %param.18) | copy-start | bytes 24580
  0.7 102.4 %copy-start.3 = (bf16[2048,8]{0,1:T(8,128)(2,1)S(1)}, bf16[2048,8]{0,1:T(8,128)(2,1)}, u32[]{:S(2)}) copy-start(bf16[2048,8]{0,1:T(8,128)(2,1)} %param.24) | copy-start | bytes 98308
  0.7 102.4 %copy-start.5 = (s32[1,16,2]{1,2,0:T(2,128)S(1)}, s32[1,16,2]{1,2,0:T(2,128)}, u32[]{:S(2)}) copy-start(s32[1,16,2]{1,2,0:T(2,128)} %param.25) | copy-start | bytes 388
  4.0 17.0 %all-to-all-start = ((bf16[8,8,2176]{2,1,0:T(8,128)(2,1)}), bf16[8,8,2176]{2,1,0:T(8,128)(2,1)S(1)}, u32[]{:S(2)}, u32[]{:S(2)}) async-start(bf16[8,8,2176]{2,1,0:T(8,128)(2,1)} %get-tuple-element.26), calls=%async_computation | async-start | bytes 557056 | tf_op jit(solution)/shard_map/all_to_all | solution.py:260
  10.3 27.4 %collective-permute-start.6 = (bf16[256,1024]{1,0:T(8,128)(2,1)}, bf16[256,1024]{1,0:T(8,128)(2,1)S(1)}, u32[]{:S(2)}, u32[]{:S(2)}) collective-permute-start(bf16[256,1024]{1,0:T(8,128)(2,1)} %refs_4_.1), channel_id=1, source_target_pairs={{0,1},{1,0},{2,3},{3,2},{4,5},{5,4},{6,7},{7,6},{8,9},{9,8},{10,11... | collective-permute-start | bytes 1572872 | tf_op jit(solution)/shard_map/ppermute | solution.py:256
  10.8 1.0 copy-start.1
  12.5 13.3 %collective-permute-start = (bf16[128,512]{1,0:T(8,128)(2,1)S(1)}, bf16[128,512]{1,0:T(8,128)(2,1)S(1)}, u32[]{:S(2)}, u32[]{:S(2)}) collective-permute-start(bf16[128,512]{1,0:T(8,128)(2,1)S(1)} %get-tuple-element.28), channel_id=1, source_target_pairs={{0,2},{1,3},{2,0},{3,1},{4,6},{5,7},{6,4},{7,5},{8,10},{9,11},{10,... | collective-permute-start | bytes 393224 | tf_op jit(solution)/shard_map/ppermute | solution.py:256
  14.2 15.1 %collective-permute-start.1 = (bf16[128,512]{1,0:T(8,128)(2,1)S(1)}, bf16[128,512]{1,0:T(8,128)(2,1)S(1)}, u32[]{:S(2)}, u32[]{:S(2)}) collective-permute-start(bf16[128,512]{1,0:T(8,128)(2,1)S(1)} %get-tuple-element.29), channel_id=1, source_target_pairs={{0,4},{1,5},{2,6},{3,7},{4,0},{5,1},{6,2},{7,3},{8,12},{9,13},{10,... | collective-permute-start | bytes 393224 | tf_op jit(solution)/shard_map/ppermute | solution.py:256
  16.6 12.8 %collective-permute-start.2 = (bf16[128,512]{1,0:T(8,128)(2,1)S(1)}, bf16[128,512]{1,0:T(8,128)(2,1)S(1)}, u32[]{:S(2)}, u32[]{:S(2)}) collective-permute-start(bf16[128,512]{1,0:T(8,128)(2,1)S(1)} %get-tuple-element.30), channel_id=1, source_target_pairs={{0,6},{1,7},{2,4},{3,5},{4,2},{5,3},{6,0},{7,1},{8,14},{9,15},{10,... | collective-permute-start | bytes 393224 | tf_op jit(solution)/shard_map/ppermute | solution.py:256
  29.3 40.1 %all-to-all-start.1 = ((bf16[8,56,256]{2,1,0:T(8,128)(2,1)}), bf16[8,56,256]{2,1,0:T(8,128)(2,1)S(1)}, u32[]{:S(2)}, u32[]{:S(2)}) async-start(bf16[8,56,256]{2,1,0:T(8,128)(2,1)} %query_project.1.rest_0_), calls=%async_computation.1 | async-start | bytes 458752 | tf_op jit(solution)/shard_map/all_to_all | solution.py:260
  33.5 35.9 %collective-permute-start.14 = (bf16[256,512]{1,0:T(8,128)(2,1)S(1)}, bf16[256,512]{1,0:T(8,128)(2,1)S(1)}, u32[]{:S(2)}, u32[]{:S(2)}) collective-permute-start(bf16[256,512]{1,0:T(8,128)(2,1)S(1)} %cache_relay.1), channel_id=1, source_target_pairs={{0,1},{1,0},{2,3},{3,2},{4,5},{5,4},{6,7},{7,6},{8,9},{9,8},{10,11... | collective-permute-start | bytes 786440 | tf_op jit(solution)/shard_map/ppermute | solution.py:256
  34.2 4.3 %collective-permute-start.3 = (bf16[64,512]{1,0:T(8,128)(2,1)S(1)}, bf16[64,512]{1,0:T(8,128)(2,1)S(1)}, u32[]{:S(2)}, u32[]{:S(2)}) collective-permute-start(bf16[64,512]{1,0:T(8,128)(2,1)S(1)} %own_tokens.1.refs_0_), channel_id=1, source_target_pairs={{0,8},{8,0},{16,24},{24,16},{1,9},{9,1},{17,25},{25,17},{2,10},{10... | collective-permute-start | bytes 196616 | tf_op jit(solution)/shard_map/ppermute | solution.py:256
  35.7 4.3 %collective-permute-start.4 = (bf16[64,512]{1,0:T(8,128)(2,1)S(1)}, bf16[64,512]{1,0:T(8,128)(2,1)S(1)}, u32[]{:S(2)}, u32[]{:S(2)}) collective-permute-start(bf16[64,512]{1,0:T(8,128)(2,1)S(1)} %own_tokens.1.refs_0_), channel_id=1, source_target_pairs={{0,16},{8,24},{16,0},{24,8},{1,17},{9,25},{17,1},{25,9},{2,18},{10... | collective-permute-start | bytes 196616 | tf_op jit(solution)/shard_map/ppermute | solution.py:256
  37.2 5.2 %collective-permute-start.5 = (bf16[64,512]{1,0:T(8,128)(2,1)S(1)}, bf16[64,512]{1,0:T(8,128)(2,1)S(1)}, u32[]{:S(2)}, u32[]{:S(2)}) collective-permute-start(bf16[64,512]{1,0:T(8,128)(2,1)S(1)} %own_tokens.1.refs_0_), channel_id=1, source_target_pairs={{0,24},{8,16},{16,8},{24,0},{1,25},{9,17},{17,9},{25,1},{2,26},{10... | collective-permute-start | bytes 196616 | tf_op jit(solution)/shard_map/ppermute | solution.py:256
  42.4 1.0 copy-start
  44.5 6.3 %collective-permute-start.7 = (bf16[256,256]{1,0:T(8,128)(2,1)S(1)}, bf16[256,256]{1,0:T(8,128)(2,1)S(1)}, u32[]{:S(2)}, u32[]{:S(2)}) collective-permute-start(bf16[256,256]{1,0:T(8,128)(2,1)S(1)} %get-tuple-element.33), channel_id=1, source_target_pairs={{0,2},{1,3},{2,0},{3,1},{4,6},{5,7},{6,4},{7,5},{8,10},{9,11},{10,... | collective-permute-start | bytes 393224 | tf_op jit(solution)/shard_map/ppermute | solution.py:256
  46.2 11.7 %collective-permute-start.8 = (bf16[256,256]{1,0:T(8,128)(2,1)S(1)}, bf16[256,256]{1,0:T(8,128)(2,1)S(1)}, u32[]{:S(2)}, u32[]{:S(2)}) collective-permute-start(bf16[256,256]{1,0:T(8,128)(2,1)S(1)} %get-tuple-element.34), channel_id=1, source_target_pairs={{0,4},{1,5},{2,6},{3,7},{4,0},{5,1},{6,2},{7,3},{8,12},{9,13},{10,... | collective-permute-start | bytes 393224 | tf_op jit(solution)/shard_map/ppermute | solution.py:256
  48.6 9.4 %collective-permute-start.9 = (bf16[256,256]{1,0:T(8,128)(2,1)S(1)}, bf16[256,256]{1,0:T(8,128)(2,1)S(1)}, u32[]{:S(2)}, u32[]{:S(2)}) collective-permute-start(bf16[256,256]{1,0:T(8,128)(2,1)S(1)} %get-tuple-element.35), channel_id=1, source_target_pairs={{0,6},{1,7},{2,4},{3,5},{4,2},{5,3},{6,0},{7,1},{8,14},{9,15},{10,... | collective-permute-start | bytes 393224 | tf_op jit(solution)/shard_map/ppermute | solution.py:256
  58.5 8.0 %collective-permute-start.10 = (bf16[64,256]{1,0:T(8,128)(2,1)S(1)}, bf16[64,256]{1,0:T(8,128)(2,1)S(1)}, u32[]{:S(2)}, u32[]{:S(2)}) collective-permute-start(bf16[64,256]{1,0:T(8,128)(2,1)S(1)} %get-tuple-element.36), channel_id=1, source_target_pairs={{0,0},{1,8},{2,1},{3,9},{4,2},{5,10},{6,3},{7,11},{8,4},{9,12},{10... | collective-permute-start | bytes 98312 | tf_op jit(solution)/shard_map/ppermute | solution.py:256
  59.2 7.3 %collective-permute-start.11 = (bf16[64,256]{1,0:T(8,128)(2,1)S(1)}, bf16[64,256]{1,0:T(8,128)(2,1)S(1)}, u32[]{:S(2)}, u32[]{:S(2)}) collective-permute-start(bf16[64,256]{1,0:T(8,128)(2,1)S(1)} %get-tuple-element.37), channel_id=1, source_target_pairs={{0,8},{1,0},{2,9},{3,1},{4,10},{5,2},{6,11},{7,3},{8,12},{9,4},{10... | collective-permute-start | bytes 98312 | tf_op jit(solution)/shard_map/ppermute | solution.py:256
  64.8 4.2 %collective-permute-start.12 = (bf16[64,256]{1,0:T(8,128)(2,1)S(1)}, bf16[64,256]{1,0:T(8,128)(2,1)S(1)}, u32[]{:S(2)}, u32[]{:S(2)}) collective-permute-start(bf16[64,256]{1,0:T(8,128)(2,1)S(1)} %get-tuple-element.38), channel_id=1, source_target_pairs={{0,16},{1,24},{2,17},{3,25},{4,18},{5,26},{6,19},{7,27},{8,20},{9,... | collective-permute-start | bytes 98312 | tf_op jit(solution)/shard_map/ppermute | solution.py:256
  65.5 4.0 %collective-permute-start.13 = (bf16[64,256]{1,0:T(8,128)(2,1)S(1)}, bf16[64,256]{1,0:T(8,128)(2,1)S(1)}, u32[]{:S(2)}, u32[]{:S(2)}) collective-permute-start(bf16[64,256]{1,0:T(8,128)(2,1)S(1)} %get-tuple-element.39), channel_id=1, source_target_pairs={{0,24},{1,16},{2,25},{3,17},{4,26},{5,18},{6,27},{7,19},{8,28},{9,... | collective-permute-start | bytes 98312 | tf_op jit(solution)/shard_map/ppermute | solution.py:256

commit v3 on v2

--- a/solution.py
+++ b/solution.py
@@ -425,12 +425,16 @@
     )(place, *in_hbm(activations, gain.reshape(1, width), router, routes))
 
 
-def cache_split(cache_part, place, after):
+def cache_split(cache_part, side, place, after):
     rows, width = cache_part.shape
     count = 8
     span = width // 2 // count
 
-    def body(index_ref, cache_ref, after_ref, *outs):
+    def body(index_ref, cache_ref, side_ref, after_ref, *refs):
+        outs, side_out, sem = refs[:5], refs[5], refs[6]
+        side_copy = pltpu.make_async_copy(side_ref, side_out, sem)
+        side_copy.start()
+
         def piece(other):
             start = pl.multiple_of((index_ref[2] ^ other) * span, span)
             return cache_ref[:, pl.ds(start, span)], cache_ref[:, pl.ds(start + width // 2, span)]
@@ -444,16 +448,19 @@
                     out, base = outs[side], 0
                 out[base : base + rows, :span] = keys
                 out[base : base + rows, span:] = values
+        side_copy.wait()
 
     shapes = [(rows, 2 * span)] * 2 + [(2 * rows, 2 * span)] * 3
     return pl.pallas_call(
         body,
-        in_specs=[index_spec(), whole_spec(), any_spec()],
-        out_specs=[whole_spec()] * 5,
-        out_shape=[jax.ShapeDtypeStruct(one, cache_part.dtype) for one in shapes],
+        in_specs=[index_spec(), whole_spec(), any_spec(), any_spec()],
+        out_specs=[whole_spec()] * 6,
+        out_shape=[jax.ShapeDtypeStruct(one, cache_part.dtype) for one in shapes]
+        + [pltpu.VMEM(side.shape, side.dtype)],
+        scratch_shapes=[pltpu.SemaphoreType.DMA(())],
         compiler_params=pltpu.CompilerParams(vmem_limit_bytes=4 << 20),
         name="cache_split",
-    )(place, cache_part, after)
+    )(place, cache_part, *in_hbm(side), after)
 
 
 def cache_relay(near, turned):
@@ -534,7 +541,6 @@
                 place = step * (tile // span) + one
                 out_ref[place, :slots, :] = query[:, one * span : (one + 1) * span]
                 out_ref[place, slots:, :] = line
-
     return pl.pallas_call(
         body,
         in_specs=[whole_spec(), any_spec()] + [any_spec()] * len(after),
@@ -545,11 +551,12 @@
             pltpu.SemaphoreType.DMA((steps,)),
         ],
         compiler_params=pltpu.CompilerParams(vmem_limit_bytes=14 << 20),
+        cost_estimate=pl.CostEstimate(flops=0, transcendentals=0, bytes_accessed=40 << 20),
         name="query_project",
     )(arrived, *in_hbm(weight), *after)
 
 
-def key_value_parts(tokens, weight, sibling, place):
+def key_value_parts(tokens, weight, sibling, place, after):
     rows, depth = tokens[0].shape
     half = depth // 2
     quarter = weight.shape[1] // 4
@@ -557,7 +564,7 @@
 
     def body(place_ref, *refs):
         token_refs, weight_ref, sibling_ref = refs[:count], refs[count], refs[count + 1]
-        outs = refs[count + 2 :]
+        outs = refs[count + 2 + len(after) :]
         stacked = jnp.concatenate([one[...] for one in token_refs], axis=0)
         for turn in range(4):
             start = pl.multiple_of(((place_ref[2] // 2) ^ turn) * quarter, quarter)
@@ -578,20 +585,20 @@
     ]
     return pl.pallas_call(
         body,
-        in_specs=[index_spec()] + [whole_spec()] * (count + 2),
+        in_specs=[index_spec()] + [whole_spec()] * (count + 2) + [any_spec()] * len(after),
         out_specs=[whole_spec()] * 4,
         out_shape=shapes,
         compiler_params=pltpu.CompilerParams(vmem_limit_bytes=8 << 20),
         name="key_value_parts",
-    )(place, *tokens, weight, sibling)
-
-
-def key_value_sum(parts, place):
+    )(place, *tokens, weight, sibling, *after)
+
+
+def key_value_sum(parts, place, after):
     rows, quarter = parts[0].shape
     block = rows // 4
 
     def body(place_ref, *refs):
-        ins, outs = refs[:4], refs[4:]
+        ins, outs = refs[:4], refs[5:]
         req = place_ref[1]
         source = (req // 2) * 2 + place_ref[2] % 2
         for turn in range(4):
@@ -603,12 +610,12 @@
 
     return pl.pallas_call(
         body,
-        in_specs=[index_spec()] + [whole_spec()] * 4,
+        in_specs=[index_spec()] + [whole_spec()] * 4 + [any_spec()],
         out_specs=[whole_spec()] * 4,
         out_shape=[jax.ShapeDtypeStruct((block, quarter), jnp.bfloat16)] * 4,
         compiler_params=pltpu.CompilerParams(vmem_limit_bytes=4 << 20),
         name="key_value_sum",
-    )(place, *parts)
+    )(place, *parts, after)
 
 
 def attention(message, scalars, fresh_blocks, own, turned, relayed):
@@ -874,28 +881,31 @@
         activations[0], attention_gain, attention_router.T, attn_routes, place, tok_count
     )
     arrived = swap_all(message, "tok")
-    own_block, near, *turned = cache_split(cache_entries[0], place, attn_weights)
+    own_block, near, *turned, weight_held = cache_split(
+        cache_entries[0], key_value_weight, place, attn_weights
+    )
     turned = [
         permute(turned[turn - 1], "tok", [(one, one ^ (2 * turn)) for one in range(tok_count)])
         for turn in range(1, 4)
     ]
     pair = [(one, one ^ 1) for one in range(tok_count)]
     sibling = permute(key_value_weight, "tok", pair)
-    projected = query_project(arrived, query_weight[0], [], tok_count)
-    projected, *turned = lax.optimization_barrier((projected, *turned))
-    queries = swap_all(projected, "tok")
-    mine = own_tokens(arrived, [projected], tok_count, width)
-    relayed = permute(cache_relay(near, turned), "tok", pair)
+    mine = own_tokens(arrived, [sibling]+turned[:1], tok_count, width)
     tokens = [mine] + [
         permute(mine, "req", [(one, one ^ turn) for one in range(req_count)])
         for turn in range(1, req_count)
     ]
-    parts = key_value_parts(tokens, key_value_weight, sibling, place)
+    parts = key_value_parts(tokens, weight_held, sibling, place, turned)
+    projected = query_project(arrived, query_weight[0], parts[:1], tok_count)
     parts = [parts[0]] + [
         permute(parts[turn], "tok", [(one, one ^ (2 * turn)) for one in range(tok_count)])
         for turn in range(1, 4)
     ]
-    sums = key_value_sum(parts, place)
+    projected, *gate = lax.optimization_barrier((projected, *parts[1:], *turned))
+    parts[1:], turned = gate[:3], gate[3:]
+    sums = key_value_sum(parts, place, projected)
+    queries = swap_all(projected, "tok")
+    relayed = permute(cache_relay(near, turned), "tok", pair)
     fresh_blocks = []
     for turn in range(4):
         pairs = []

time: 152 us -> 145 us (0.954)
  waiting for transfers between devices: 24.3 us -> 16 us
    ppermute x15, waiting for transfers between devices: 20.2 us -> 16 us  [permute(): return lax.ppermute(values, axis, pairs)]
    all_to_all x2, waiting for transfers between devices: 4.05 us -> 0.01 us  [swap_all(): return lax.all_to_all(values, axis, split_axis=0, concat_axis=0, tiled=True)]
    ppermute x15, starting transfers between devices: 21.5 us -> 23.4 us  [permute(): return lax.ppermute(values, axis, pairs)]
  transfers between devices with their start and end apart: 17 -> 17, of which waited for: 10 -> 7; matrix products, arithmetic and copies ran while one was open for 0% -> 0% of each run, Pallas kernels for 5% -> 7%
where the time goes in v3:
time: 145 us
  blocking collectives  53 us (37%)
  Pallas kernels  40.3 us (28%)
  starting transfers between devices  33 us (23%)
  waiting for transfers between devices  16 us (11%)
    all_to_all x4, blocking collectives, swap_all(): return lax.all_to_all(values, axis, split_axis=0, concat_axis=0, tiled=True)  53 us
    ppermute x15, starting transfers between devices, permute(): return lax.ppermute(values, axis, pairs)  23.4 us
    pallas_call x1, Pallas kernels, feedforward(): pl.pallas_call(body, in_specs=[whole_spec(), any_spec(), any_spec()], out...  22.1 us
    ppermute x15, waiting for transfers between devices, permute(): return lax.ppermute(values, axis, pairs)  16 us
    all_to_all x2, starting transfers between devices, swap_all(): return lax.all_to_all(values, axis, split_axis=0, concat_axis=0, tiled=True)  9.57 us
    pallas_call x1, Pallas kernels, query_project(): pl.pallas_call(body, in_specs=[whole_spec(), any_spec()] + [any_spec()] *...  4.75 us
    pallas_call x1, Pallas kernels, output_project(): pl.pallas_call(body, in_specs=[whole_spec(), any_spec()], out_specs=[whol...  4.25 us
  transfers between devices with their start and end apart: 17, of which 7 were waited for; matrix products, arithmetic and copies ran while one was open for 0% of the time, Pallas kernels for 7%

profile of v3, /device:TPU:0, one launch (start us, length us, event | category | flops | bytes accessed | tf_op | source)
XLA Modules:
  0.0 144.8 jit_solution(1553724932653057593)
XLA Ops:
  1.9 2.5 %prepare.1 = (bf16[8,8,2176]{2,1,0:T(8,128)(2,1)}, f32[64,16]{1,0:T(8,128)S(1)}) custom-call(s32[3]{0:T(128)S(1)} %pad_add_fusion.place_ref.index_ref.scalar_ref, bf16[16,2048]{1,0:T(8,128)(2,1)} %bitcast.21, f32[1,2048]{1,0:T(1,128)} %bitcast.32, bf16[8,2048]{1,0:T(8,128)(2,1)} %bitcast.31, s32[2,16]{1,0:T(2,128)} %bitcast.33), custom_call_target="tpu_custom_call" | custom-call | tf_op jit(solution)/shard_map/prepare/pallas_call | solution.py:406
  4.4 6.0 %all-to-all-start = ((bf16[8,8,2176]{2,1,0:T(8,128)(2,1)}), bf16[8,8,2176]{2,1,0:T(8,128)(2,1)S(1)}, u32[]{:S(2)}, u32[]{:S(2)}) async-start(bf16[8,8,2176]{2,1,0:T(8,128)(2,1)} %get-tuple-element.30), calls=%async_computation | async-start | bytes 557056 | tf_op jit(solution)/shard_map/all_to_all | solution.py:260
  10.5 1.0 copy-done
  11.5 1.6 %cache_split.1 = (bf16[64,512]{1,0:T(8,128)(2,1)S(1)}, bf16[64,512]{1,0:T(8,128)(2,1)S(1)}, bf16[128,512]{1,0:T(8,128)(2,1)S(1)}, bf16[128,512]{1,0:T(8,128)(2,1...) custom-call(s32[3]{0:T(128)S(1)} %pad_add_fusion.place_ref.index_ref.scalar_ref, ...), custom_call_target="tpu_custom_call" | custom-call | tf_op jit(solution)/shard_map/cache_split/pallas_call | solution.py:454
  13.1 2.1 %collective-permute-start.1 = (bf16[128,512]{1,0:T(8,128)(2,1)S(1)}, bf16[128,512]{1,0:T(8,128)(2,1)S(1)}, u32[]{:S(2)}, u32[]{:S(2)}) collective-permute-start(bf16[128,512]{1,0:T(8,128)(2,1)S(1)} %get-tuple-element.32), channel_id=1, source_target_pairs={{0,2},{1,3},{2,0},{3,1},{4,6},{5,7},{6,4},{7,5},{8,10},{9,11},{10,... | collective-permute-start | bytes 393224 | tf_op jit(solution)/shard_map/ppermute | solution.py:256
  15.2 2.4 %collective-permute-start.5 = (bf16[128,512]{1,0:T(8,128)(2,1)S(1)}, bf16[128,512]{1,0:T(8,128)(2,1)S(1)}, u32[]{:S(2)}, u32[]{:S(2)}) collective-permute-start(bf16[128,512]{1,0:T(8,128)(2,1)S(1)} %get-tuple-element.34), channel_id=1, source_target_pairs={{0,4},{1,5},{2,6},{3,7},{4,0},{5,1},{6,2},{7,3},{8,12},{9,13},{10,... | collective-permute-start | bytes 393224 | tf_op jit(solution)/shard_map/ppermute | solution.py:256
  17.6 6.4 %collective-permute-done.1.rest_1_.refs_6_.refs_0_.refs_5_ = bf16[128,512]{1,0:T(8,128)(2,1)S(1)} collective-permute-done((bf16[128,512]{1,0:T(8,128)(2,1)S(1)}, bf16[128,512]{1,0:T(8,128)(2,1)S(1)}, u32[]{:S(2)}, u32[]{:S(2)}) %collective-permute-start.1) | collective-permute-done | bytes 131104 | tf_op jit(solution)/shard_map/ppermute | solution.py:256
  24.1 2.5 %collective-permute-start.4 = (bf16[64,512]{1,0:T(8,128)(2,1)S(1)}, bf16[64,512]{1,0:T(8,128)(2,1)S(1)}, u32[]{:S(2)}, u32[]{:S(2)}) collective-permute-start(bf16[64,512]{1,0:T(8,128)(2,1)S(1)} %own_tokens.1.refs_0_), channel_id=1, source_target_pairs={{0,24},{8,16},{16,8},{24,0},{1,25},{9,17},{17,9},{25,1},{2,26},{10... | collective-permute-start | bytes 196616 | tf_op jit(solution)/shard_map/ppermute | solution.py:256
  27.6 1.9 %collective-permute-done.5.refs_7_.refs_1_.refs_6_ = bf16[128,512]{1,0:T(8,128)(2,1)S(1)} collective-permute-done((bf16[128,512]{1,0:T(8,128)(2,1)S(1)}, bf16[128,512]{1,0:T(8,128)(2,1)S(1)}, u32[]{:S(2)}, u32[]{:S(2)}) %collective-permute-start.5) | collective-permute-done | bytes 131104 | tf_op jit(solution)/shard_map/ppermute | solution.py:256
  29.5 1.4 collective-permute-done.3.refs_2_
  31.4 1.0 key_value_parts.1
  32.4 1.1 collective-permute-start.7
  34.0 2.8 %collective-permute-start.9 = (bf16[256,256]{1,0:T(8,128)(2,1)S(1)}, bf16[256,256]{1,0:T(8,128)(2,1)S(1)}, u32[]{:S(2)}, u32[]{:S(2)}) collective-permute-start(bf16[256,256]{1,0:T(8,128)(2,1)S(1)} %get-tuple-element.39), channel_id=1, source_target_pairs={{0,6},{1,7},{2,4},{3,5},{4,2},{5,3},{6,0},{7,1},{8,14},{9,15},{10,... | collective-permute-start | bytes 393224 | tf_op jit(solution)/shard_map/ppermute | solution.py:256
  36.8 4.8 %query_project.1.refs_4_ = bf16[8,56,256]{2,1,0:T(8,128)(2,1)} custom-call(bf16[8,8,2176]{2,1,0:T(8,128)(2,1)S(1)} %all-to-all-done.in_ref, bf16[2048,2048]{1,0:T(8,128)(2,1)} %bitcast.28, f32[256,256]{1,0:T(8,128)S(1)} %get-tuple-element.36.rest_0_.refs_0_), custom_call_target="tpu_custom_call" | custom-call | bytes 41943040 | tf_op jit(solution)/shard_map/query_project/pallas_call | solution.py:544
  41.6 4.3 %collective-permute-done.8.refs_2_ = bf16[256,256]{1,0:T(8,128)(2,1)S(1)} collective-permute-done((bf16[256,256]{1,0:T(8,128)(2,1)S(1)}, bf16[256,256]{1,0:T(8,128)(2,1)S(1)}, u32[]{:S(2)}, u32[]{:S(2)}) %collective-permute-start.8) | collective-permute-done | bytes 131104 | tf_op jit(solution)/shard_map/ppermute | solution.py:256
  45.9 3.6 %all-to-all-start.1 = ((bf16[8,56,256]{2,1,0:T(8,128)(2,1)}), bf16[8,56,256]{2,1,0:T(8,128)(2,1)S(1)}, u32[]{:S(2)}, u32[]{:S(2)}) async-start(bf16[8,56,256]{2,1,0:T(8,128)(2,1)} %query_project.1.refs_4_), calls=%async_computation.1 | async-start | bytes 458752 | tf_op jit(solution)/shard_map/all_to_all | solution.py:260
  49.5 0.6 collective-permute-start.14
  50.1 0.6 key_value_sum.1
  50.7 0.7 collective-permute-start.10
  51.4 5.3 %collective-permute-start.11 = (bf16[64,256]{1,0:T(8,128)(2,1)S(1)}, bf16[64,256]{1,0:T(8,128)(2,1)S(1)}, u32[]{:S(2)}, u32[]{:S(2)}) collective-permute-start(bf16[64,256]{1,0:T(8,128)(2,1)S(1)} %get-tuple-element.45), channel_id=1, source_target_pairs={{0,8},{1,0},{2,9},{3,1},{4,10},{5,2},{6,11},{7,3},{8,12},{9,4},{10... | collective-permute-start | bytes 98312 | tf_op jit(solution)/shard_map/ppermute | solution.py:256
  56.7 1.5 %collective-permute-start.12 = (bf16[64,256]{1,0:T(8,128)(2,1)S(1)}, bf16[64,256]{1,0:T(8,128)(2,1)S(1)}, u32[]{:S(2)}, u32[]{:S(2)}) collective-permute-start(bf16[64,256]{1,0:T(8,128)(2,1)S(1)} %get-tuple-element.46), channel_id=1, source_target_pairs={{0,16},{1,24},{2,17},{3,25},{4,18},{5,26},{6,19},{7,27},{8,20},{9,... | collective-permute-start | bytes 98312 | tf_op jit(solution)/shard_map/ppermute | solution.py:256
  58.2 2.3 %collective-permute-start.13 = (bf16[64,256]{1,0:T(8,128)(2,1)S(1)}, bf16[64,256]{1,0:T(8,128)(2,1)S(1)}, u32[]{:S(2)}, u32[]{:S(2)}) collective-permute-start(bf16[64,256]{1,0:T(8,128)(2,1)S(1)} %get-tuple-element.47), channel_id=1, source_target_pairs={{0,24},{1,16},{2,25},{3,17},{4,26},{5,18},{6,27},{7,19},{8,28},{9,... | collective-permute-start | bytes 98312 | tf_op jit(solution)/shard_map/ppermute | solution.py:256
  60.6 1.5 %collective-permute-done.13.refs_3_ = bf16[64,256]{1,0:T(8,128)(2,1)S(1)} collective-permute-done((bf16[64,256]{1,0:T(8,128)(2,1)S(1)}, bf16[64,256]{1,0:T(8,128)(2,1)S(1)}, u32[]{:S(2)}, u32[]{:S(2)}) %collective-permute-start.13) | collective-permute-done | bytes 32800 | tf_op jit(solution)/shard_map/ppermute | solution.py:256
  62.1 1.7 %attention.1 = bf16[8,80,256]{2,1,0:T(8,128)(2,1)S(1)} custom-call(s32[3]{0:T(128)S(1)} %pad_add_fusion.place_ref.index_ref.scalar_ref, bf16[8,56,256]{2,1,0:T(8,128)(2,1)S(1)} %all-to-all-done.1.in_ref, bf16[64,256]{1,0:T(8,128)(2,1)S(1)} %collective-permute-done.10.refs_0_, bf16[64,256]{1,0:T(8,128)(2,1)S(1)} %collective-permute-done.11.refs_1_, ...), custom_call_target="tpu_custom_call" | custom-call | tf_op jit(solution)/shard_map/attention/pallas_call | solution.py:692
  63.8 16.5 %all_to_all.30.in_ref = bf16[8,80,256]{2,1,0:T(8,128)(2,1)S(1)} all-to-all(bf16[8,80,256]{2,1,0:T(8,128)(2,1)S(1)} %attention.1), channel_id=1, replica_groups=mesh['req'=4,'tok'=8] {'tok'}, dimensions={0} | all-to-all | bytes 655360 | tf_op jit(solution)/shard_map/all_to_all | solution.py:260
  80.3 4.2 %output_project.1 = (bf16[8,8,2048]{2,1,0:T(8,128)(2,1)S(1)}, bf16[16,4096]{1,0:T(8,128)(2,1)}) custom-call(bf16[8,80,256]{2,1,0:T(8,128)(2,1)S(1)} %all_to_all.30.in_ref, bf16[2048,2048]{1,0:T(8,128)(2,1)} %bitcast.29), custom_call_target="tpu_custom_call" | custom-call | tf_op jit(solution)/shard_map/output_project/pallas_call | solution.py:727
  84.6 12.1 %all_to_all.31.in_ref = bf16[8,8,2048]{2,1,0:T(8,128)(2,1)S(1)} all-to-all(bf16[8,8,2048]{2,1,0:T(8,128)(2,1)S(1)} %get-tuple-element.53), channel_id=1, replica_groups=mesh['req'=4,'tok'=8] {'tok'}, dimensions={0} | all-to-all | bytes 524288 | tf_op jit(solution)/shard_map/all_to_all | solution.py:260
  96.8 0.7 middle.1
  97.5 12.1 %all_to_all.32.in_ref = bf16[8,8,2048]{2,1,0:T(8,128)(2,1)S(1)} all-to-all(bf16[8,8,2048]{2,1,0:T(8,128)(2,1)S(1)} %get-tuple-element.55), channel_id=1, replica_groups=mesh['req'=4,'tok'=8] {'tok'}, dimensions={0} | all-to-all | bytes 524288 | tf_op jit(solution)/shard_map/all_to_all | solution.py:260
  109.6 22.1 %feedforward.1 = bf16[8,8,2048]{2,1,0:T(8,128)(2,1)S(1)} custom-call(bf16[8,8,2048]{2,1,0:T(8,128)(2,1)S(1)} %all_to_all.32.in_ref, bf16[2048,11264]{1,0:T(8,128)(2,1)} %bitcast.26, bf16[5632,2048]{1,0:T(8,128)(2,1)} %bitcast.27), custom_call_target="tpu_custom_call" | custom-call | tf_op jit(solution)/shard_map/feedforward/pallas_call | solution.py:839
  131.7 12.1 %all_to_all.33.in_ref = bf16[8,8,2048]{2,1,0:T(8,128)(2,1)S(1)} all-to-all(bf16[8,8,2048]{2,1,0:T(8,128)(2,1)S(1)} %feedforward.1), channel_id=1, replica_groups=mesh['req'=4,'tok'=8] {'tok'}, dimensions={0} | all-to-all | bytes 524288 | tf_op jit(solution)/shard_map/all_to_all | solution.py:260
  143.9 0.9 finish.1
  (29 shorter events, 3.0 us)
Async XLA Ops:
  0.6 96.1 %copy-start.1 = (bf16[1,16,2048]{2,1,0:T(8,128)(2,1)S(1)}, bf16[1,16,2048]{2,1,0:T(8,128)(2,1)}, u32[]{:S(2)}) copy-start(bf16[1,16,2048]{2,1,0:T(8,128)(2,1)} %param.14) | copy-start | bytes 196612
  0.6 96.1 %copy-start.4 = (s32[1,16,2]{1,2,0:T(2,128)S(1)}, s32[1,16,2]{1,2,0:T(2,128)}, u32[]{:S(2)}) copy-start(s32[1,16,2]{1,2,0:T(2,128)} %param.25) | copy-start | bytes 388
  0.7 96.1 %copy-start.2 = (bf16[2048,8]{0,1:T(8,128)(2,1)S(1)}, bf16[2048,8]{0,1:T(8,128)(2,1)}, u32[]{:S(2)}) copy-start(bf16[2048,8]{0,1:T(8,128)(2,1)} %param.24) | copy-start | bytes 98308
  0.7 96.1 %copy-start.3 = (f32[2048]{0:T(1024)S(1)}, f32[2048]{0:T(1024)}, u32[]{:S(2)}) copy-start(f32[2048]{0:T(1024)} %param.18) | copy-start | bytes 24580
  0.7 23.3 %collective-permute-start = (bf16[256,1024]{1,0:T(8,128)(2,1)}, bf16[256,1024]{1,0:T(8,128)(2,1)S(1)}, u32[]{:S(2)}, u32[]{:S(2)}) collective-permute-start(bf16[256,1024]{1,0:T(8,128)(2,1)} %side_ref.1), channel_id=1, source_target_pairs={{0,1},{1,0},{2,3},{3,2},{4,5},{5,4},{6,7},{7,6},{8,9},{9,8},{10,11... | collective-permute-start | bytes 1572872 | tf_op jit(solution)/shard_map/ppermute | solution.py:256
  4.4 19.5 %all-to-all-start = ((bf16[8,8,2176]{2,1,0:T(8,128)(2,1)}), bf16[8,8,2176]{2,1,0:T(8,128)(2,1)S(1)}, u32[]{:S(2)}, u32[]{:S(2)}) async-start(bf16[8,8,2176]{2,1,0:T(8,128)(2,1)} %get-tuple-element.30), calls=%async_computation | async-start | bytes 557056 | tf_op jit(solution)/shard_map/all_to_all | solution.py:260
  10.4 1.0 copy-start
  13.1 10.9 %collective-permute-start.1 = (bf16[128,512]{1,0:T(8,128)(2,1)S(1)}, bf16[128,512]{1,0:T(8,128)(2,1)S(1)}, u32[]{:S(2)}, u32[]{:S(2)}) collective-permute-start(bf16[128,512]{1,0:T(8,128)(2,1)S(1)} %get-tuple-element.32), channel_id=1, source_target_pairs={{0,2},{1,3},{2,0},{3,1},{4,6},{5,7},{6,4},{7,5},{8,10},{9,11},{10,... | collective-permute-start | bytes 393224 | tf_op jit(solution)/shard_map/ppermute | solution.py:256
  15.2 14.3 %collective-permute-start.5 = (bf16[128,512]{1,0:T(8,128)(2,1)S(1)}, bf16[128,512]{1,0:T(8,128)(2,1)S(1)}, u32[]{:S(2)}, u32[]{:S(2)}) collective-permute-start(bf16[128,512]{1,0:T(8,128)(2,1)S(1)} %get-tuple-element.34), channel_id=1, source_target_pairs={{0,4},{1,5},{2,6},{3,7},{4,0},{5,1},{6,2},{7,3},{8,12},{9,13},{10,... | collective-permute-start | bytes 393224 | tf_op jit(solution)/shard_map/ppermute | solution.py:256
  17.5 12.0 %collective-permute-start.6 = (bf16[128,512]{1,0:T(8,128)(2,1)S(1)}, bf16[128,512]{1,0:T(8,128)(2,1)S(1)}, u32[]{:S(2)}, u32[]{:S(2)}) collective-permute-start(bf16[128,512]{1,0:T(8,128)(2,1)S(1)} %get-tuple-element.35), channel_id=1, source_target_pairs={{0,6},{1,7},{2,4},{3,5},{4,2},{5,3},{6,0},{7,1},{8,14},{9,15},{10,... | collective-permute-start | bytes 393224 | tf_op jit(solution)/shard_map/ppermute | solution.py:256
  24.1 5.4 %collective-permute-start.4 = (bf16[64,512]{1,0:T(8,128)(2,1)S(1)}, bf16[64,512]{1,0:T(8,128)(2,1)S(1)}, u32[]{:S(2)}, u32[]{:S(2)}) collective-permute-start(bf16[64,512]{1,0:T(8,128)(2,1)S(1)} %own_tokens.1.refs_0_), channel_id=1, source_target_pairs={{0,24},{8,16},{16,8},{24,0},{1,25},{9,17},{17,9},{25,1},{2,26},{10... | collective-permute-start | bytes 196616 | tf_op jit(solution)/shard_map/ppermute | solution.py:256
  26.6 4.3 %collective-permute-start.3 = (bf16[64,512]{1,0:T(8,128)(2,1)S(1)}, bf16[64,512]{1,0:T(8,128)(2,1)S(1)}, u32[]{:S(2)}, u32[]{:S(2)}) collective-permute-start(bf16[64,512]{1,0:T(8,128)(2,1)S(1)} %own_tokens.1.refs_0_), channel_id=1, source_target_pairs={{0,16},{8,24},{16,0},{24,8},{1,17},{9,25},{17,1},{25,9},{2,18},{10... | collective-permute-start | bytes 196616 | tf_op jit(solution)/shard_map/ppermute | solution.py:256
  27.1 4.3 %collective-permute-start.2 = (bf16[64,512]{1,0:T(8,128)(2,1)S(1)}, bf16[64,512]{1,0:T(8,128)(2,1)S(1)}, u32[]{:S(2)}, u32[]{:S(2)}) collective-permute-start(bf16[64,512]{1,0:T(8,128)(2,1)S(1)} %own_tokens.1.refs_0_), channel_id=1, source_target_pairs={{0,8},{8,0},{16,24},{24,16},{1,9},{9,1},{17,25},{25,17},{2,10},{10... | collective-permute-start | bytes 196616 | tf_op jit(solution)/shard_map/ppermute | solution.py:256
  32.4 9.2 %collective-permute-start.7 = (bf16[256,256]{1,0:T(8,128)(2,1)S(1)}, bf16[256,256]{1,0:T(8,128)(2,1)S(1)}, u32[]{:S(2)}, u32[]{:S(2)}) collective-permute-start(bf16[256,256]{1,0:T(8,128)(2,1)S(1)} %get-tuple-element.37), channel_id=1, source_target_pairs={{0,2},{1,3},{2,0},{3,1},{4,6},{5,7},{6,4},{7,5},{8,10},{9,11},{10,... | collective-permute-start | bytes 393224 | tf_op jit(solution)/shard_map/ppermute | solution.py:256
  33.5 12.4 %collective-permute-start.8 = (bf16[256,256]{1,0:T(8,128)(2,1)S(1)}, bf16[256,256]{1,0:T(8,128)(2,1)S(1)}, u32[]{:S(2)}, u32[]{:S(2)}) collective-permute-start(bf16[256,256]{1,0:T(8,128)(2,1)S(1)} %get-tuple-element.38), channel_id=1, source_target_pairs={{0,4},{1,5},{2,6},{3,7},{4,0},{5,1},{6,2},{7,3},{8,12},{9,13},{10,... | collective-permute-start | bytes 393224 | tf_op jit(solution)/shard_map/ppermute | solution.py:256
  34.0 11.9 %collective-permute-start.9 = (bf16[256,256]{1,0:T(8,128)(2,1)S(1)}, bf16[256,256]{1,0:T(8,128)(2,1)S(1)}, u32[]{:S(2)}, u32[]{:S(2)}) collective-permute-start(bf16[256,256]{1,0:T(8,128)(2,1)S(1)} %get-tuple-element.39), channel_id=1, source_target_pairs={{0,6},{1,7},{2,4},{3,5},{4,2},{5,3},{6,0},{7,1},{8,14},{9,15},{10,... | collective-permute-start | bytes 393224 | tf_op jit(solution)/shard_map/ppermute | solution.py:256
  45.9 16.2 %all-to-all-start.1 = ((bf16[8,56,256]{2,1,0:T(8,128)(2,1)}), bf16[8,56,256]{2,1,0:T(8,128)(2,1)S(1)}, u32[]{:S(2)}, u32[]{:S(2)}) async-start(bf16[8,56,256]{2,1,0:T(8,128)(2,1)} %query_project.1.refs_4_), calls=%async_computation.1 | async-start | bytes 458752 | tf_op jit(solution)/shard_map/all_to_all | solution.py:260
  49.5 12.6 %collective-permute-start.14 = (bf16[256,512]{1,0:T(8,128)(2,1)S(1)}, bf16[256,512]{1,0:T(8,128)(2,1)S(1)}, u32[]{:S(2)}, u32[]{:S(2)}) collective-permute-start(bf16[256,512]{1,0:T(8,128)(2,1)S(1)} %cache_relay.1), channel_id=1, source_target_pairs={{0,1},{1,0},{2,3},{3,2},{4,5},{5,4},{6,7},{7,6},{8,9},{9,8},{10,11... | collective-permute-start | bytes 786440 | tf_op jit(solution)/shard_map/ppermute | solution.py:256
  50.7 9.8 %collective-permute-start.10 = (bf16[64,256]{1,0:T(8,128)(2,1)S(1)}, bf16[64,256]{1,0:T(8,128)(2,1)S(1)}, u32[]{:S(2)}, u32[]{:S(2)}) collective-permute-start(bf16[64,256]{1,0:T(8,128)(2,1)S(1)} %get-tuple-element.44), channel_id=1, source_target_pairs={{0,0},{1,8},{2,1},{3,9},{4,2},{5,10},{6,3},{7,11},{8,4},{9,12},{10... | collective-permute-start | bytes 98312 | tf_op jit(solution)/shard_map/ppermute | solution.py:256
  51.4 9.1 %collective-permute-start.11 = (bf16[64,256]{1,0:T(8,128)(2,1)S(1)}, bf16[64,256]{1,0:T(8,128)(2,1)S(1)}, u32[]{:S(2)}, u32[]{:S(2)}) collective-permute-start(bf16[64,256]{1,0:T(8,128)(2,1)S(1)} %get-tuple-element.45), channel_id=1, source_target_pairs={{0,8},{1,0},{2,9},{3,1},{4,10},{5,2},{6,11},{7,3},{8,12},{9,4},{10... | collective-permute-start | bytes 98312 | tf_op jit(solution)/shard_map/ppermute | solution.py:256
  56.7 3.9 %collective-permute-start.12 = (bf16[64,256]{1,0:T(8,128)(2,1)S(1)}, bf16[64,256]{1,0:T(8,128)(2,1)S(1)}, u32[]{:S(2)}, u32[]{:S(2)}) collective-permute-start(bf16[64,256]{1,0:T(8,128)(2,1)S(1)} %get-tuple-element.46), channel_id=1, source_target_pairs={{0,16},{1,24},{2,17},{3,25},{4,18},{5,26},{6,19},{7,27},{8,20},{9,... | collective-permute-start | bytes 98312 | tf_op jit(solution)/shard_map/ppermute | solution.py:256
  58.2 3.9 %collective-permute-start.13 = (bf16[64,256]{1,0:T(8,128)(2,1)S(1)}, bf16[64,256]{1,0:T(8,128)(2,1)S(1)}, u32[]{:S(2)}, u32[]{:S(2)}) collective-permute-start(bf16[64,256]{1,0:T(8,128)(2,1)S(1)} %get-tuple-element.47), channel_id=1, source_target_pairs={{0,24},{1,16},{2,25},{3,17},{4,26},{5,18},{6,27},{7,19},{8,28},{9,... | collective-permute-start | bytes 98312 | tf_op jit(solution)/shard_map/ppermute | solution.py:256

commit v4 on v3

--- a/solution.py
+++ b/solution.py
@@ -361,7 +361,7 @@
     return stacked[:count] + (stacked[count : 2 * count] + stacked[2 * count :])
 
 
-def prepare(activations, gain, router, routes, place, tok_count):
+def prepare(activations, gain, router, routes, tok_count):
     rows, width = activations.shape
     experts = router.shape[0]
     span = width // tok_count
@@ -369,7 +369,7 @@
     per_row = width // (2 * span)
 
     def body(
-        place_ref, act_in, gain_in, router_in, route_in, out_ref, weight_ref,
+        act_in, gain_in, router_in, route_in, out_ref, weight_ref,
         act_ref, gain_ref, router_ref, route_ref, wide, copy, sems,
     ):
         load_all(
@@ -405,7 +405,7 @@
 
     return pl.pallas_call(
         body,
-        in_specs=[index_spec()] + [any_spec()] * 4,
+        in_specs=[any_spec()] * 4,
         out_specs=[whole_spec()] * 2,
         out_shape=[
             jax.ShapeDtypeStruct((tok_count, PAD, width + LANES), jnp.bfloat16),
@@ -422,7 +422,7 @@
         ],
         compiler_params=pltpu.CompilerParams(vmem_limit_bytes=4 << 20),
         name="prepare",
-    )(place, *in_hbm(activations, gain.reshape(1, width), router, routes))
+    )(*in_hbm(activations, gain.reshape(1, width), router, routes))
 
 
 def cache_split(cache_part, side, place, after):
@@ -431,36 +431,33 @@
     span = width // 2 // count
 
     def body(index_ref, cache_ref, side_ref, after_ref, *refs):
-        outs, side_out, sem = refs[:5], refs[5], refs[6]
-        side_copy = pltpu.make_async_copy(side_ref, side_out, sem)
-        side_copy.start()
-
-        def piece(other):
-            start = pl.multiple_of((index_ref[2] ^ other) * span, span)
-            return cache_ref[:, pl.ds(start, span)], cache_ref[:, pl.ds(start + width // 2, span)]
-
-        for turn in range(4):
-            for side in range(2):
-                keys, values = piece(2 * turn + side)
-                if turn:
-                    out, base = outs[turn + 1], side * rows
-                else:
-                    out, base = outs[side], 0
-                out[base : base + rows, :span] = keys
-                out[base : base + rows, span:] = values
-        side_copy.wait()
+        outs, side_out, sems = refs[:5], refs[5], refs[6]
+        pairs = []
+        for number in range(count):
+            turn, side = number // 2, number % 2
+            out, base = (outs[turn + 1], side * rows) if turn else (outs[side], 0)
+            start = pl.multiple_of((index_ref[2] ^ number) * span, span)
+            for kind in range(2):
+                pairs.append(
+                    (
+                        cache_ref.at[:, pl.ds(kind * (width // 2) + start, span)],
+                        out.at[base : base + rows, kind * span : (kind + 1) * span],
+                    )
+                )
+        pairs.append((side_ref, side_out))
+        load_all(pairs, sems)
 
     shapes = [(rows, 2 * span)] * 2 + [(2 * rows, 2 * span)] * 3
     return pl.pallas_call(
         body,
-        in_specs=[index_spec(), whole_spec(), any_spec(), any_spec()],
+        in_specs=[index_spec()] + [any_spec()] * 3,
         out_specs=[whole_spec()] * 6,
         out_shape=[jax.ShapeDtypeStruct(one, cache_part.dtype) for one in shapes]
         + [pltpu.VMEM(side.shape, side.dtype)],
-        scratch_shapes=[pltpu.SemaphoreType.DMA(())],
+        scratch_shapes=[pltpu.SemaphoreType.DMA((2 * count + 1,))],
         compiler_params=pltpu.CompilerParams(vmem_limit_bytes=4 << 20),
         name="cache_split",
-    )(place, cache_part, *in_hbm(side), after)
+    )(place, *in_hbm(cache_part, side), after)
 
 
 def cache_relay(near, turned):
@@ -878,7 +875,7 @@
     ffn_routes = feedforward_routes[0].T
     place = jnp.stack([cache_lengths[0], req_index, tok_index])
     message, attn_weights = prepare(
-        activations[0], attention_gain, attention_router.T, attn_routes, place, tok_count
+        activations[0], attention_gain, attention_router.T, attn_routes, tok_count
     )
     arrived = swap_all(message, "tok")
     own_block, near, *turned, weight_held = cache_split(
@@ -890,7 +887,7 @@
     ]
     pair = [(one, one ^ 1) for one in range(tok_count)]
     sibling = permute(key_value_weight, "tok", pair)
-    mine = own_tokens(arrived, [sibling]+turned[:1], tok_count, width)
+    mine = own_tokens(arrived, [sibling], tok_count, width)
     tokens = [mine] + [
         permute(mine, "req", [(one, one ^ turn) for one in range(req_count)])
         for turn in range(1, req_count)

time: 145 us -> 144 us (level)
  waiting for transfers between devices: 16 us -> 14 us
  starting transfers between devices: 33 us -> 34.8 us
    ppermute x15, waiting for transfers between devices: 16 us -> 10.6 us  [permute(): return lax.ppermute(values, axis, pairs)]
    all_to_all x2, waiting for transfers between devices: 0.01 us -> 3.37 us  [swap_all(): return lax.all_to_all(values, axis, split_axis=0, concat_axis=0, tiled=True)]
    ppermute x15, starting transfers between devices: 23.4 us -> 25.2 us  [permute(): return lax.ppermute(values, axis, pairs)]
  transfers between devices with their start and end apart: 17 -> 17, of which waited for: 7 -> 5; matrix products, arithmetic and copies ran while one was open for 0% -> 0% of each run, Pallas kernels for 7% -> 7%
where the time goes in v4:
time: 144 us; the launch traced here: 143 us
  blocking collectives  52.9 us (37%)
  Pallas kernels  40.2 us (28%)
  starting transfers between devices  34.8 us (24%)
  waiting for transfers between devices  14 us (10%)
  between operations  1.45 us (1%)
    all_to_all x4, blocking collectives, swap_all(): return lax.all_to_all(values, axis, split_axis=0, concat_axis=0, tiled=True)  52.9 us
    ppermute x15, starting transfers between devices, permute(): return lax.ppermute(values, axis, pairs)  25.2 us
    pallas_call x1, Pallas kernels, feedforward(): pl.pallas_call(body, in_specs=[whole_spec(), any_spec(), any_spec()], out...  22.1 us
    ppermute x15, waiting for transfers between devices, permute(): return lax.ppermute(values, axis, pairs)  10.6 us
    all_to_all x2, starting transfers between devices, swap_all(): return lax.all_to_all(values, axis, split_axis=0, concat_axis=0, tiled=True)  9.62 us
    pallas_call x1, Pallas kernels, query_project(): pl.pallas_call(body, in_specs=[whole_spec(), any_spec()] + [any_spec()] *...  4.76 us
    pallas_call x1, Pallas kernels, output_project(): pl.pallas_call(body, in_specs=[whole_spec(), any_spec()], out_specs=[whol...  4.25 us
    all_to_all x2, waiting for transfers between devices, swap_all(): return lax.all_to_all(values, axis, split_axis=0, concat_axis=0, tiled=True)  3.37 us
  transfers between devices with their start and end apart: 17, of which 5 were waited for; matrix products, arithmetic and copies ran while one was open for 0% of the time, Pallas kernels for 7%

profile of v4, /device:TPU:0, one launch (start us, length us, event | category | flops | bytes accessed | tf_op | source)
XLA Modules:
  0.0 143.5 jit_solution(11418187443655062514)
XLA Ops:
  0.7 0.5 collective-permute-start
  1.2 2.0 %prepare.1 = (bf16[8,8,2176]{2,1,0:T(8,128)(2,1)}, f32[64,16]{1,0:T(8,128)S(1)}) custom-call(bf16[16,2048]{1,0:T(8,128)(2,1)} %bitcast.20, f32[1,2048]{1,0:T(1,128)} %bitcast.32, bf16[8,2048]{1,0:T(8,128)(2,1)} %bitcast.31, s32[2,16]{1,0:T(2,128)} %bitcast.33), custom_call_target="tpu_custom_call" | custom-call | tf_op jit(solution)/shard_map/prepare/pallas_call | solution.py:406
  3.2 6.0 %all-to-all-start = ((bf16[8,8,2176]{2,1,0:T(8,128)(2,1)}), bf16[8,8,2176]{2,1,0:T(8,128)(2,1)S(1)}, u32[]{:S(2)}, u32[]{:S(2)}) async-start(bf16[8,8,2176]{2,1,0:T(8,128)(2,1)} %get-tuple-element.30), calls=%async_computation | async-start | bytes 557056 | tf_op jit(solution)/shard_map/all_to_all | solution.py:260
  9.9 2.0 %cache_split.1 = (bf16[64,512]{1,0:T(8,128)(2,1)S(1)}, bf16[64,512]{1,0:T(8,128)(2,1)S(1)}, bf16[128,512]{1,0:T(8,128)(2,1)S(1)}, bf16[128,512]{1,0:T(8,128)(2,1...) custom-call(s32[3]{0:T(128)S(1)} %pad_add_fusion.index_ref.place_ref.scalar_ref, ...), custom_call_target="tpu_custom_call" | custom-call | tf_op jit(solution)/shard_map/cache_split/pallas_call | solution.py:451
  11.9 2.1 %collective-permute-start.4 = (bf16[128,512]{1,0:T(8,128)(2,1)S(1)}, bf16[128,512]{1,0:T(8,128)(2,1)S(1)}, u32[]{:S(2)}, u32[]{:S(2)}) collective-permute-start(bf16[128,512]{1,0:T(8,128)(2,1)S(1)} %get-tuple-element.33), channel_id=1, source_target_pairs={{0,2},{1,3},{2,0},{3,1},{4,6},{5,7},{6,4},{7,5},{8,10},{9,11},{10,... | collective-permute-start | bytes 393224 | tf_op jit(solution)/shard_map/ppermute | solution.py:256
  14.0 2.4 %collective-permute-start.5 = (bf16[128,512]{1,0:T(8,128)(2,1)S(1)}, bf16[128,512]{1,0:T(8,128)(2,1)S(1)}, u32[]{:S(2)}, u32[]{:S(2)}) collective-permute-start(bf16[128,512]{1,0:T(8,128)(2,1)S(1)} %get-tuple-element.34), channel_id=1, source_target_pairs={{0,4},{1,5},{2,6},{3,7},{4,0},{5,1},{6,2},{7,3},{8,12},{9,13},{10,... | collective-permute-start | bytes 393224 | tf_op jit(solution)/shard_map/ppermute | solution.py:256
  16.5 3.4 %all-to-all-done.in_ref = bf16[8,8,2176]{2,1,0:T(8,128)(2,1)S(1)} async-done(((bf16[8,8,2176]{2,1,0:T(8,128)(2,1)}), bf16[8,8,2176]{2,1,0:T(8,128)(2,1)S(1)}, u32[]{:S(2)}, u32[]{:S(2)}) %all-to-all-start) | async-done | bytes 278560 | tf_op jit(solution)/shard_map/all_to_all | solution.py:260
  19.9 2.5 %collective-permute-start.3 = (bf16[64,512]{1,0:T(8,128)(2,1)S(1)}, bf16[64,512]{1,0:T(8,128)(2,1)S(1)}, u32[]{:S(2)}, u32[]{:S(2)}) collective-permute-start(bf16[64,512]{1,0:T(8,128)(2,1)S(1)} %own_tokens.1.refs_0_), channel_id=1, source_target_pairs={{0,24},{8,16},{16,8},{24,0},{1,25},{9,17},{17,9},{25,1},{2,26},{10... | collective-permute-start | bytes 196616 | tf_op jit(solution)/shard_map/ppermute | solution.py:256
  22.9 1.4 collective-permute-start.1
  24.3 3.9 %collective-permute-done.5.refs_7_.refs_1_.refs_6_ = bf16[128,512]{1,0:T(8,128)(2,1)S(1)} collective-permute-done((bf16[128,512]{1,0:T(8,128)(2,1)S(1)}, bf16[128,512]{1,0:T(8,128)(2,1)S(1)}, u32[]{:S(2)}, u32[]{:S(2)}) %collective-permute-start.5) | collective-permute-done | bytes 131104 | tf_op jit(solution)/shard_map/ppermute | solution.py:256
  28.2 1.0 key_value_parts.1
  29.2 2.9 %collective-permute-start.7 = (bf16[256,256]{1,0:T(8,128)(2,1)S(1)}, bf16[256,256]{1,0:T(8,128)(2,1)S(1)}, u32[]{:S(2)}, u32[]{:S(2)}) collective-permute-start(bf16[256,256]{1,0:T(8,128)(2,1)S(1)} %get-tuple-element.37), channel_id=1, source_target_pairs={{0,2},{1,3},{2,0},{3,1},{4,6},{5,7},{6,4},{7,5},{8,10},{9,11},{10,... | collective-permute-start | bytes 393224 | tf_op jit(solution)/shard_map/ppermute | solution.py:256
  32.2 2.4 %collective-permute-start.9 = (bf16[256,256]{1,0:T(8,128)(2,1)S(1)}, bf16[256,256]{1,0:T(8,128)(2,1)S(1)}, u32[]{:S(2)}, u32[]{:S(2)}) collective-permute-start(bf16[256,256]{1,0:T(8,128)(2,1)S(1)} %get-tuple-element.39), channel_id=1, source_target_pairs={{0,6},{1,7},{2,4},{3,5},{4,2},{5,3},{6,0},{7,1},{8,14},{9,15},{10,... | collective-permute-start | bytes 393224 | tf_op jit(solution)/shard_map/ppermute | solution.py:256
  34.6 4.8 %query_project.1.refs_4_ = bf16[8,56,256]{2,1,0:T(8,128)(2,1)} custom-call(bf16[8,8,2176]{2,1,0:T(8,128)(2,1)S(1)} %all-to-all-done.in_ref, bf16[2048,2048]{1,0:T(8,128)(2,1)} %bitcast.27, f32[256,256]{1,0:T(8,128)S(1)} %get-tuple-element.36.rest_0_.refs_0_), custom_call_target="tpu_custom_call" | custom-call | bytes 41943040 | tf_op jit(solution)/shard_map/query_project/pallas_call | solution.py:541
  39.4 5.1 %collective-permute-done.8.refs_2_ = bf16[256,256]{1,0:T(8,128)(2,1)S(1)} collective-permute-done((bf16[256,256]{1,0:T(8,128)(2,1)S(1)}, bf16[256,256]{1,0:T(8,128)(2,1)S(1)}, u32[]{:S(2)}, u32[]{:S(2)}) %collective-permute-start.8) | collective-permute-done | bytes 131104 | tf_op jit(solution)/shard_map/ppermute | solution.py:256
  44.5 3.6 %all-to-all-start.1 = ((bf16[8,56,256]{2,1,0:T(8,128)(2,1)}), bf16[8,56,256]{2,1,0:T(8,128)(2,1)S(1)}, u32[]{:S(2)}, u32[]{:S(2)}) async-start(bf16[8,56,256]{2,1,0:T(8,128)(2,1)} %query_project.1.refs_4_), calls=%async_computation.1 | async-start | bytes 458752 | tf_op jit(solution)/shard_map/all_to_all | solution.py:260
  48.1 0.6 collective-permute-start.14
  48.7 0.6 key_value_sum.1
  49.3 0.7 collective-permute-start.10
  50.0 5.3 %collective-permute-start.11 = (bf16[64,256]{1,0:T(8,128)(2,1)S(1)}, bf16[64,256]{1,0:T(8,128)(2,1)S(1)}, u32[]{:S(2)}, u32[]{:S(2)}) collective-permute-start(bf16[64,256]{1,0:T(8,128)(2,1)S(1)} %get-tuple-element.45), channel_id=1, source_target_pairs={{0,8},{1,0},{2,9},{3,1},{4,10},{5,2},{6,11},{7,3},{8,12},{9,4},{10... | collective-permute-start | bytes 98312 | tf_op jit(solution)/shard_map/ppermute | solution.py:256
  55.3 1.5 %collective-permute-start.12 = (bf16[64,256]{1,0:T(8,128)(2,1)S(1)}, bf16[64,256]{1,0:T(8,128)(2,1)S(1)}, u32[]{:S(2)}, u32[]{:S(2)}) collective-permute-start(bf16[64,256]{1,0:T(8,128)(2,1)S(1)} %get-tuple-element.46), channel_id=1, source_target_pairs={{0,16},{1,24},{2,17},{3,25},{4,18},{5,26},{6,19},{7,27},{8,20},{9,... | collective-permute-start | bytes 98312 | tf_op jit(solution)/shard_map/ppermute | solution.py:256
  56.9 2.3 %collective-permute-start.13 = (bf16[64,256]{1,0:T(8,128)(2,1)S(1)}, bf16[64,256]{1,0:T(8,128)(2,1)S(1)}, u32[]{:S(2)}, u32[]{:S(2)}) collective-permute-start(bf16[64,256]{1,0:T(8,128)(2,1)S(1)} %get-tuple-element.47), channel_id=1, source_target_pairs={{0,24},{1,16},{2,25},{3,17},{4,26},{5,18},{6,27},{7,19},{8,28},{9,... | collective-permute-start | bytes 98312 | tf_op jit(solution)/shard_map/ppermute | solution.py:256
  59.2 1.5 %collective-permute-done.13.refs_3_ = bf16[64,256]{1,0:T(8,128)(2,1)S(1)} collective-permute-done((bf16[64,256]{1,0:T(8,128)(2,1)S(1)}, bf16[64,256]{1,0:T(8,128)(2,1)S(1)}, u32[]{:S(2)}, u32[]{:S(2)}) %collective-permute-start.13) | collective-permute-done | bytes 32800 | tf_op jit(solution)/shard_map/ppermute | solution.py:256
  60.7 1.8 %attention.1 = bf16[8,80,256]{2,1,0:T(8,128)(2,1)S(1)} custom-call(s32[3]{0:T(128)S(1)} %pad_add_fusion.index_ref.place_ref.scalar_ref, bf16[8,56,256]{2,1,0:T(8,128)(2,1)S(1)} %all-to-all-done.1.in_ref, bf16[64,256]{1,0:T(8,128)(2,1)S(1)} %collective-permute-done.10.refs_0_, bf16[64,256]{1,0:T(8,128)(2,1)S(1)} %collective-permute-done.11.refs_1_, ...), custom_call_target="tpu_custom_call" | custom-call | tf_op jit(solution)/shard_map/attention/pallas_call | solution.py:689
  62.5 16.5 %all_to_all.30.in_ref = bf16[8,80,256]{2,1,0:T(8,128)(2,1)S(1)} all-to-all(bf16[8,80,256]{2,1,0:T(8,128)(2,1)S(1)} %attention.1), channel_id=1, replica_groups=mesh['req'=4,'tok'=8] {'tok'}, dimensions={0} | all-to-all | bytes 655360 | tf_op jit(solution)/shard_map/all_to_all | solution.py:260
  79.0 4.2 %output_project.1 = (bf16[8,8,2048]{2,1,0:T(8,128)(2,1)S(1)}, bf16[16,4096]{1,0:T(8,128)(2,1)}) custom-call(bf16[8,80,256]{2,1,0:T(8,128)(2,1)S(1)} %all_to_all.30.in_ref, bf16[2048,2048]{1,0:T(8,128)(2,1)} %bitcast.28), custom_call_target="tpu_custom_call" | custom-call | tf_op jit(solution)/shard_map/output_project/pallas_call | solution.py:724
  83.2 12.1 %all_to_all.31.in_ref = bf16[8,8,2048]{2,1,0:T(8,128)(2,1)S(1)} all-to-all(bf16[8,8,2048]{2,1,0:T(8,128)(2,1)S(1)} %get-tuple-element.53), channel_id=1, replica_groups=mesh['req'=4,'tok'=8] {'tok'}, dimensions={0} | all-to-all | bytes 524288 | tf_op jit(solution)/shard_map/all_to_all | solution.py:260
  95.4 0.7 middle.1
  96.1 12.1 %all_to_all.32.in_ref = bf16[8,8,2048]{2,1,0:T(8,128)(2,1)S(1)} all-to-all(bf16[8,8,2048]{2,1,0:T(8,128)(2,1)S(1)} %get-tuple-element.55), channel_id=1, replica_groups=mesh['req'=4,'tok'=8] {'tok'}, dimensions={0} | all-to-all | bytes 524288 | tf_op jit(solution)/shard_map/all_to_all | solution.py:260
  108.3 22.1 %feedforward.1 = bf16[8,8,2048]{2,1,0:T(8,128)(2,1)S(1)} custom-call(bf16[8,8,2048]{2,1,0:T(8,128)(2,1)S(1)} %all_to_all.32.in_ref, bf16[2048,11264]{1,0:T(8,128)(2,1)} %bitcast.25, bf16[5632,2048]{1,0:T(8,128)(2,1)} %bitcast.26), custom_call_target="tpu_custom_call" | custom-call | tf_op jit(solution)/shard_map/feedforward/pallas_call | solution.py:836
  130.4 12.1 %all_to_all.33.in_ref = bf16[8,8,2048]{2,1,0:T(8,128)(2,1)S(1)} all-to-all(bf16[8,8,2048]{2,1,0:T(8,128)(2,1)S(1)} %feedforward.1), channel_id=1, replica_groups=mesh['req'=4,'tok'=8] {'tok'}, dimensions={0} | all-to-all | bytes 524288 | tf_op jit(solution)/shard_map/all_to_all | solution.py:260
  142.5 0.9 finish.1
  (27 shorter events, 0.9 us)
Async XLA Ops:
  0.6 94.8 %copy-start = (bf16[1,16,2048]{2,1,0:T(8,128)(2,1)S(1)}, bf16[1,16,2048]{2,1,0:T(8,128)(2,1)}, u32[]{:S(2)}) copy-start(bf16[1,16,2048]{2,1,0:T(8,128)(2,1)} %param.14) | copy-start | bytes 196612
  0.6 94.7 %copy-start.3 = (s32[1,16,2]{1,2,0:T(2,128)S(1)}, s32[1,16,2]{1,2,0:T(2,128)}, u32[]{:S(2)}) copy-start(s32[1,16,2]{1,2,0:T(2,128)} %param.25) | copy-start | bytes 388
  0.7 94.7 %copy-start.1 = (bf16[2048,8]{0,1:T(8,128)(2,1)S(1)}, bf16[2048,8]{0,1:T(8,128)(2,1)}, u32[]{:S(2)}) copy-start(bf16[2048,8]{0,1:T(8,128)(2,1)} %param.24) | copy-start | bytes 98308
  0.7 94.7 %copy-start.2 = (f32[2048]{0:T(1024)S(1)}, f32[2048]{0:T(1024)}, u32[]{:S(2)}) copy-start(f32[2048]{0:T(1024)} %param.18) | copy-start | bytes 24580
  0.7 19.2 %collective-permute-start = (bf16[256,1024]{1,0:T(8,128)(2,1)}, bf16[256,1024]{1,0:T(8,128)(2,1)S(1)}, u32[]{:S(2)}, u32[]{:S(2)}) collective-permute-start(bf16[256,1024]{1,0:T(8,128)(2,1)} %side_ref.1), channel_id=1, source_target_pairs={{0,1},{1,0},{2,3},{3,2},{4,5},{5,4},{6,7},{7,6},{8,9},{9,8},{10,11... | collective-permute-start | bytes 1572872 | tf_op jit(solution)/shard_map/ppermute | solution.py:256
  3.2 16.7 %all-to-all-start = ((bf16[8,8,2176]{2,1,0:T(8,128)(2,1)}), bf16[8,8,2176]{2,1,0:T(8,128)(2,1)S(1)}, u32[]{:S(2)}, u32[]{:S(2)}) async-start(bf16[8,8,2176]{2,1,0:T(8,128)(2,1)} %get-tuple-element.30), calls=%async_computation | async-start | bytes 557056 | tf_op jit(solution)/shard_map/all_to_all | solution.py:260
  11.9 11.0 %collective-permute-start.4 = (bf16[128,512]{1,0:T(8,128)(2,1)S(1)}, bf16[128,512]{1,0:T(8,128)(2,1)S(1)}, u32[]{:S(2)}, u32[]{:S(2)}) collective-permute-start(bf16[128,512]{1,0:T(8,128)(2,1)S(1)} %get-tuple-element.33), channel_id=1, source_target_pairs={{0,2},{1,3},{2,0},{3,1},{4,6},{5,7},{6,4},{7,5},{8,10},{9,11},{10,... | collective-permute-start | bytes 393224 | tf_op jit(solution)/shard_map/ppermute | solution.py:256
  14.0 14.2 %collective-permute-start.5 = (bf16[128,512]{1,0:T(8,128)(2,1)S(1)}, bf16[128,512]{1,0:T(8,128)(2,1)S(1)}, u32[]{:S(2)}, u32[]{:S(2)}) collective-permute-start(bf16[128,512]{1,0:T(8,128)(2,1)S(1)} %get-tuple-element.34), channel_id=1, source_target_pairs={{0,4},{1,5},{2,6},{3,7},{4,0},{5,1},{6,2},{7,3},{8,12},{9,13},{10,... | collective-permute-start | bytes 393224 | tf_op jit(solution)/shard_map/ppermute | solution.py:256
  16.4 11.8 %collective-permute-start.6 = (bf16[128,512]{1,0:T(8,128)(2,1)S(1)}, bf16[128,512]{1,0:T(8,128)(2,1)S(1)}, u32[]{:S(2)}, u32[]{:S(2)}) collective-permute-start(bf16[128,512]{1,0:T(8,128)(2,1)S(1)} %get-tuple-element.35), channel_id=1, source_target_pairs={{0,6},{1,7},{2,4},{3,5},{4,2},{5,3},{6,0},{7,1},{8,14},{9,15},{10,... | collective-permute-start | bytes 393224 | tf_op jit(solution)/shard_map/ppermute | solution.py:256
  19.9 8.3 %collective-permute-start.3 = (bf16[64,512]{1,0:T(8,128)(2,1)S(1)}, bf16[64,512]{1,0:T(8,128)(2,1)S(1)}, u32[]{:S(2)}, u32[]{:S(2)}) collective-permute-start(bf16[64,512]{1,0:T(8,128)(2,1)S(1)} %own_tokens.1.refs_0_), channel_id=1, source_target_pairs={{0,24},{8,16},{16,8},{24,0},{1,25},{9,17},{17,9},{25,1},{2,26},{10... | collective-permute-start | bytes 196616 | tf_op jit(solution)/shard_map/ppermute | solution.py:256
  22.4 5.8 %collective-permute-start.2 = (bf16[64,512]{1,0:T(8,128)(2,1)S(1)}, bf16[64,512]{1,0:T(8,128)(2,1)S(1)}, u32[]{:S(2)}, u32[]{:S(2)}) collective-permute-start(bf16[64,512]{1,0:T(8,128)(2,1)S(1)} %own_tokens.1.refs_0_), channel_id=1, source_target_pairs={{0,16},{8,24},{16,0},{24,8},{1,17},{9,25},{17,1},{25,9},{2,18},{10... | collective-permute-start | bytes 196616 | tf_op jit(solution)/shard_map/ppermute | solution.py:256
  22.9 5.3 %collective-permute-start.1 = (bf16[64,512]{1,0:T(8,128)(2,1)S(1)}, bf16[64,512]{1,0:T(8,128)(2,1)S(1)}, u32[]{:S(2)}, u32[]{:S(2)}) collective-permute-start(bf16[64,512]{1,0:T(8,128)(2,1)S(1)} %own_tokens.1.refs_0_), channel_id=1, source_target_pairs={{0,8},{8,0},{16,24},{24,16},{1,9},{9,1},{17,25},{25,17},{2,10},{10... | collective-permute-start | bytes 196616 | tf_op jit(solution)/shard_map/ppermute | solution.py:256
  29.2 10.2 %collective-permute-start.7 = (bf16[256,256]{1,0:T(8,128)(2,1)S(1)}, bf16[256,256]{1,0:T(8,128)(2,1)S(1)}, u32[]{:S(2)}, u32[]{:S(2)}) collective-permute-start(bf16[256,256]{1,0:T(8,128)(2,1)S(1)} %get-tuple-element.37), channel_id=1, source_target_pairs={{0,2},{1,3},{2,0},{3,1},{4,6},{5,7},{6,4},{7,5},{8,10},{9,11},{10,... | collective-permute-start | bytes 393224 | tf_op jit(solution)/shard_map/ppermute | solution.py:256
  32.2 12.3 %collective-permute-start.8 = (bf16[256,256]{1,0:T(8,128)(2,1)S(1)}, bf16[256,256]{1,0:T(8,128)(2,1)S(1)}, u32[]{:S(2)}, u32[]{:S(2)}) collective-permute-start(bf16[256,256]{1,0:T(8,128)(2,1)S(1)} %get-tuple-element.38), channel_id=1, source_target_pairs={{0,4},{1,5},{2,6},{3,7},{4,0},{5,1},{6,2},{7,3},{8,12},{9,13},{10,... | collective-permute-start | bytes 393224 | tf_op jit(solution)/shard_map/ppermute | solution.py:256
  32.2 12.3 %collective-permute-start.9 = (bf16[256,256]{1,0:T(8,128)(2,1)S(1)}, bf16[256,256]{1,0:T(8,128)(2,1)S(1)}, u32[]{:S(2)}, u32[]{:S(2)}) collective-permute-start(bf16[256,256]{1,0:T(8,128)(2,1)S(1)} %get-tuple-element.39), channel_id=1, source_target_pairs={{0,6},{1,7},{2,4},{3,5},{4,2},{5,3},{6,0},{7,1},{8,14},{9,15},{10,... | collective-permute-start | bytes 393224 | tf_op jit(solution)/shard_map/ppermute | solution.py:256
  44.5 16.2 %all-to-all-start.1 = ((bf16[8,56,256]{2,1,0:T(8,128)(2,1)}), bf16[8,56,256]{2,1,0:T(8,128)(2,1)S(1)}, u32[]{:S(2)}, u32[]{:S(2)}) async-start(bf16[8,56,256]{2,1,0:T(8,128)(2,1)} %query_project.1.refs_4_), calls=%async_computation.1 | async-start | bytes 458752 | tf_op jit(solution)/shard_map/all_to_all | solution.py:260
  48.1 12.6 %collective-permute-start.14 = (bf16[256,512]{1,0:T(8,128)(2,1)S(1)}, bf16[256,512]{1,0:T(8,128)(2,1)S(1)}, u32[]{:S(2)}, u32[]{:S(2)}) collective-permute-start(bf16[256,512]{1,0:T(8,128)(2,1)S(1)} %cache_relay.1), channel_id=1, source_target_pairs={{0,1},{1,0},{2,3},{3,2},{4,5},{5,4},{6,7},{7,6},{8,9},{9,8},{10,11... | collective-permute-start | bytes 786440 | tf_op jit(solution)/shard_map/ppermute | solution.py:256
  49.3 9.8 %collective-permute-start.10 = (bf16[64,256]{1,0:T(8,128)(2,1)S(1)}, bf16[64,256]{1,0:T(8,128)(2,1)S(1)}, u32[]{:S(2)}, u32[]{:S(2)}) collective-permute-start(bf16[64,256]{1,0:T(8,128)(2,1)S(1)} %get-tuple-element.44), channel_id=1, source_target_pairs={{0,0},{1,8},{2,1},{3,9},{4,2},{5,10},{6,3},{7,11},{8,4},{9,12},{10... | collective-permute-start | bytes 98312 | tf_op jit(solution)/shard_map/ppermute | solution.py:256
  50.0 9.1 %collective-permute-start.11 = (bf16[64,256]{1,0:T(8,128)(2,1)S(1)}, bf16[64,256]{1,0:T(8,128)(2,1)S(1)}, u32[]{:S(2)}, u32[]{:S(2)}) collective-permute-start(bf16[64,256]{1,0:T(8,128)(2,1)S(1)} %get-tuple-element.45), channel_id=1, source_target_pairs={{0,8},{1,0},{2,9},{3,1},{4,10},{5,2},{6,11},{7,3},{8,12},{9,4},{10... | collective-permute-start | bytes 98312 | tf_op jit(solution)/shard_map/ppermute | solution.py:256
  55.3 3.9 %collective-permute-start.12 = (bf16[64,256]{1,0:T(8,128)(2,1)S(1)}, bf16[64,256]{1,0:T(8,128)(2,1)S(1)}, u32[]{:S(2)}, u32[]{:S(2)}) collective-permute-start(bf16[64,256]{1,0:T(8,128)(2,1)S(1)} %get-tuple-element.46), channel_id=1, source_target_pairs={{0,16},{1,24},{2,17},{3,25},{4,18},{5,26},{6,19},{7,27},{8,20},{9,... | collective-permute-start | bytes 98312 | tf_op jit(solution)/shard_map/ppermute | solution.py:256
  56.9 3.9 %collective-permute-start.13 = (bf16[64,256]{1,0:T(8,128)(2,1)S(1)}, bf16[64,256]{1,0:T(8,128)(2,1)S(1)}, u32[]{:S(2)}, u32[]{:S(2)}) collective-permute-start(bf16[64,256]{1,0:T(8,128)(2,1)S(1)} %get-tuple-element.47), channel_id=1, source_target_pairs={{0,24},{1,16},{2,25},{3,17},{4,26},{5,18},{6,27},{7,19},{8,28},{9,... | collective-permute-start | bytes 98312 | tf_op jit(solution)/shard_map/ppermute | solution.py:256

commit v5 on v4

--- a/solution.py
+++ b/solution.py
@@ -241,6 +241,7 @@
 PAD = 8
 LANES = 128
 FF_TILE = 512
+WIRE = 4
 
 
 def column_stream(source, buffers, sems, tile):
@@ -295,10 +296,10 @@
         one.wait()
 
 
-def padded_picks(routes, experts):
+def padded_picks(routes, experts, height):
     row_count = routes.shape[1]
-    row = iota((experts * PAD, row_count), 0)
-    expert, slot = row // PAD, row % PAD
+    row = iota((experts * height, row_count), 0)
+    expert, slot = row // height, row % height
     first, second = routes[0:1, :] == expert, routes[1:2, :] == expert
     named = jnp.where(first, 1.0, 0.0) + jnp.where(second, 1.0, 0.0)
     earlier = (iota((row_count, row_count), 0) < iota((row_count, row_count), 1)).astype(
@@ -339,11 +340,41 @@
     return jnp.dot(chosen, rows, preferred_element_type=jnp.float32)
 
 
-def spread(rows):
-    count = rows.shape[0] // CAP * PAD
-    one, two = iota((count, rows.shape[0]), 0), iota((count, rows.shape[0]), 1)
-    chosen = ((two // CAP) * PAD + two % CAP == one).astype(jnp.bfloat16)
-    return jnp.dot(chosen, rows, preferred_element_type=jnp.float32)
+def wire_order(blocks, columns):
+    total = blocks * columns * CAP
+    row = iota((total, total), 0)
+    block, column, slot = row // (columns * CAP), row // CAP % columns, row % CAP
+    return (column * (blocks * CAP) + block * CAP + slot == iota((total, total), 1)).astype(
+        jnp.bfloat16
+    )
+
+
+def pack(pieces, blocks):
+    columns, span = len(pieces), pieces[0].shape[1]
+    stacked = jnp.concatenate(pieces, axis=0)
+    moved = jnp.dot(wire_order(blocks, columns), stacked, preferred_element_type=jnp.float32)
+    return moved.reshape(blocks, columns * CAP, span).astype(jnp.bfloat16)
+
+
+def split_columns(rows):
+    span = rows.shape[1] // WIRE
+    return [rows[:, step * span : (step + 1) * span] for step in range(WIRE)]
+
+
+def unpack(values):
+    blocks, height, span = values.shape
+    columns = height // CAP
+    flat = values.astype(jnp.float32).reshape(blocks * height, span).astype(jnp.bfloat16)
+    moved = lax.dot_general(
+        wire_order(blocks, columns),
+        flat,
+        (((0,), (0,)), ((), ())),
+        preferred_element_type=jnp.float32,
+    ).astype(jnp.bfloat16)
+    rows = blocks * CAP
+    return jnp.concatenate(
+        [moved[step * rows : (step + 1) * rows] for step in range(columns)], axis=1
+    )
 
 
 def exact_mix(weights, rows):
@@ -383,7 +414,7 @@
         )
         route = route_ref[...]
         hidden = row_norm(act_ref[...].astype(jnp.float32), gain_ref[...])
-        picks, first = padded_picks(route, experts)
+        picks, _ = padded_picks(route, experts, PAD)
         wide[...] = pick_rows(picks, hidden)
         copy[...] = hidden.astype(jnp.float32)
         for dest in range(tok_count):
@@ -401,7 +432,8 @@
         out_ref[:, :, width:] = (
             pick_rows(picks, number).astype(jnp.bfloat16).reshape(tok_count, PAD, LANES)
         )
-        weight_ref[...] = gate_weights(hidden, router_ref[...], route, picks, first)
+        narrow, first = padded_picks(route, experts, CAP)
+        weight_ref[...] = gate_weights(hidden, router_ref[...], route, narrow, first)
 
     return pl.pallas_call(
         body,
@@ -409,7 +441,7 @@
         out_specs=[whole_spec()] * 2,
         out_shape=[
             jax.ShapeDtypeStruct((tok_count, PAD, width + LANES), jnp.bfloat16),
-            jax.ShapeDtypeStruct((tok_count * PAD, rows), jnp.float32),
+            jax.ShapeDtypeStruct((tok_count * CAP, rows), jnp.float32),
         ],
         scratch_shapes=[
             pltpu.VMEM((rows, width), activations.dtype),
@@ -700,33 +732,33 @@
     blocks, height, span = arrived.shape
     slots = blocks * CAP
     width = weight.shape[1]
-    tile = width // 4
+    tile = width // WIRE
 
     def body(in_ref, weight_ref, out_ref, fresh_ref, held, sems):
         copies = column_stream(weight_ref, held, sems, tile)
         for one in copies:
             one.start()
-        rows = []
+        rows, pieces = [], []
         for block in range(blocks):
             cols = slice(block * span, (block + 1) * span)
-            rows.append(spread(in_ref[block, :slots, :]).astype(jnp.bfloat16))
+            rows.append(in_ref[block, :slots, :])
             fresh_ref[:, cols] = in_ref[block, slots : slots + query_rows, :]
             fresh_ref[:, block * span + width : (block + 1) * span + width] = in_ref[
                 block, slots + query_rows :, :
             ]
         rows = jnp.concatenate(rows, axis=1)
         for step in range(width // tile):
-            cols = slice(step * tile, (step + 1) * tile)
             copies[step].wait()
             part = jnp.dot(rows, held[step], preferred_element_type=jnp.float32)
-            out_ref[:, :, cols] = part.astype(jnp.bfloat16).reshape(blocks, PAD, tile)
+            pieces.append(part.astype(jnp.bfloat16))
+        out_ref[...] = pack(pieces, blocks)
 
     return pl.pallas_call(
         body,
         in_specs=[whole_spec(), any_spec()],
         out_specs=[whole_spec()] * 2,
         out_shape=[
-            jax.ShapeDtypeStruct((blocks, PAD, width), jnp.bfloat16),
+            jax.ShapeDtypeStruct((blocks, WIRE * CAP, tile), jnp.bfloat16),
             jax.ShapeDtypeStruct((query_rows, 2 * width), jnp.bfloat16),
         ],
         scratch_shapes=[
@@ -745,14 +777,12 @@
 
     def body(act_ref, in_ref, old_ref, gain_ref, router_ref, route_ref, out_ref, mix_ref, new_ref):
         route = route_ref[...]
-        added = exact_mix(old_ref[...], in_ref[...].reshape(blocks * PAD, width))
+        added = exact_mix(old_ref[...], unpack(in_ref[...]))
         mixed = (act_ref[...].astype(jnp.float32) + added).astype(jnp.bfloat16)
         mix_ref[...] = mixed
         hidden = row_norm(mixed.astype(jnp.float32), gain_ref[...])
-        picks, first = padded_picks(route, experts)
-        out_ref[...] = (
-            pick_rows(picks, hidden).astype(jnp.bfloat16).reshape(blocks, PAD, width)
-        )
+        picks, first = padded_picks(route, experts, CAP)
+        out_ref[...] = pack(split_columns(pick_rows(picks, hidden).astype(jnp.bfloat16)), blocks)
         new_ref[...] = gate_weights(hidden, router_ref[...], route, picks, first)
 
     return pl.pallas_call(
@@ -760,9 +790,9 @@
         in_specs=[whole_spec()] * 6,
         out_specs=[whole_spec()] * 3,
         out_shape=[
-            jax.ShapeDtypeStruct((blocks, PAD, width), jnp.bfloat16),
+            jax.ShapeDtypeStruct(arrived.shape, jnp.bfloat16),
             jax.ShapeDtypeStruct((rows, width), jnp.bfloat16),
-            jax.ShapeDtypeStruct((blocks * PAD, rows), jnp.float32),
+            jax.ShapeDtypeStruct((blocks * CAP, rows), jnp.float32),
         ],
         compiler_params=pltpu.CompilerParams(vmem_limit_bytes=4 << 20),
         name="middle",
@@ -773,7 +803,7 @@
     rows, width = mixed.shape
 
     def body(mix_ref, in_ref, weight_ref, out_ref):
-        added = exact_mix(weight_ref[...], in_ref[...].reshape(-1, width))
+        added = exact_mix(weight_ref[...], unpack(in_ref[...]))
         out_ref[...] = (mix_ref[...].astype(jnp.float32) + added).astype(jnp.bfloat16)
 
     return pl.pallas_call(
@@ -787,7 +817,7 @@
 
 
 def feedforward(arrived, gate_piece, down_piece):
-    blocks, _, width = arrived.shape
+    blocks, width = arrived.shape[0], down_piece.shape[1]
     count = blocks * CAP
     units = down_piece.shape[0]
     tile = FF_TILE
@@ -814,7 +844,7 @@
         for step in range(slots):
             for one in copies(step):
                 one.start()
-        rows = compact(in_ref[...].reshape(blocks * PAD, width)).astype(jnp.bfloat16)
+        rows = unpack(in_ref[...])
         total = jnp.zeros((count, width), jnp.float32)
         for step in range(steps):
             slot = step % slots
@@ -829,9 +859,7 @@
             if step + slots < steps:
                 for one in copies(step + slots):
                     one.start()
-        out_ref[...] = (
-            spread(total.astype(jnp.bfloat16)).astype(jnp.bfloat16).reshape(blocks, PAD, width)
-        )
+        out_ref[...] = pack(split_columns(total.astype(jnp.bfloat16)), blocks)
 
     return pl.pallas_call(
         body,

time: 144 us -> 140 us (0.972)
  blocking collectives: 52.9 us -> 48.7 us
    all_to_all x4, blocking collectives: 52.9 us -> 48.7 us  [swap_all(): return lax.all_to_all(values, axis, split_axis=0, concat_axis=0, tiled=True)]
where the time goes in v5:
time: 140 us
  blocking collectives  48.7 us (35%)
  Pallas kernels  40.7 us (29%)
  starting transfers between devices  34.8 us (25%)
  waiting for transfers between devices  13.9 us (10%)
  between operations  1.45 us (1%)
    all_to_all x4, blocking collectives, swap_all(): return lax.all_to_all(values, axis, split_axis=0, concat_axis=0, tiled=True)  48.7 us
    ppermute x15, starting transfers between devices, permute(): return lax.ppermute(values, axis, pairs)  25.2 us
    pallas_call x1, Pallas kernels, feedforward(): pl.pallas_call(body, in_specs=[whole_spec(), any_spec(), any_spec()], out...  22.2 us
    ppermute x15, waiting for transfers between devices, permute(): return lax.ppermute(values, axis, pairs)  10.6 us
    all_to_all x2, starting transfers between devices, swap_all(): return lax.all_to_all(values, axis, split_axis=0, concat_axis=0, tiled=True)  9.62 us
    pallas_call x1, Pallas kernels, query_project(): pl.pallas_call(body, in_specs=[whole_spec(), any_spec()] + [any_spec()] *...  4.76 us
    pallas_call x1, Pallas kernels, output_project(): pl.pallas_call(body, in_specs=[whole_spec(), any_spec()], out_specs=[whol...  4.21 us
    all_to_all x2, waiting for transfers between devices, swap_all(): return lax.all_to_all(values, axis, split_axis=0, concat_axis=0, tiled=True)  3.37 us
  transfers between devices with their start and end apart: 17, of which 5 were waited for; matrix products, arithmetic and copies ran while one was open for 0% of the time, Pallas kernels for 7%

profile of v5, /device:TPU:0, one launch (start us, length us, event | category | flops | bytes accessed | tf_op | source)
XLA Modules:
  0.0 139.8 jit_solution(14936763256382120075)
XLA Ops:
  0.7 0.5 collective-permute-start
  1.2 2.0 %prepare.1 = (bf16[8,8,2176]{2,1,0:T(8,128)(2,1)}, f32[48,16]{1,0:T(8,128)S(1)}) custom-call(bf16[16,2048]{1,0:T(8,128)(2,1)} %bitcast.20, f32[1,2048]{1,0:T(1,128)} %bitcast.32, bf16[8,2048]{1,0:T(8,128)(2,1)} %bitcast.31, s32[2,16]{1,0:T(2,128)} %bitcast.33), custom_call_target="tpu_custom_call" | custom-call | tf_op jit(solution)/shard_map/prepare/pallas_call | solution.py:438
  3.2 6.0 %all-to-all-start = ((bf16[8,8,2176]{2,1,0:T(8,128)(2,1)}), bf16[8,8,2176]{2,1,0:T(8,128)(2,1)S(1)}, u32[]{:S(2)}, u32[]{:S(2)}) async-start(bf16[8,8,2176]{2,1,0:T(8,128)(2,1)} %get-tuple-element.30), calls=%async_computation | async-start | bytes 557056 | tf_op jit(solution)/shard_map/all_to_all | solution.py:261
  9.9 2.0 %cache_split.1 = (bf16[64,512]{1,0:T(8,128)(2,1)S(1)}, bf16[64,512]{1,0:T(8,128)(2,1)S(1)}, bf16[128,512]{1,0:T(8,128)(2,1)S(1)}, bf16[128,512]{1,0:T(8,128)(2,1...) custom-call(s32[3]{0:T(128)S(1)} %pad_add_fusion.index_ref.place_ref.scalar_ref, ...), custom_call_target="tpu_custom_call" | custom-call | tf_op jit(solution)/shard_map/cache_split/pallas_call | solution.py:483
  11.9 2.1 %collective-permute-start.4 = (bf16[128,512]{1,0:T(8,128)(2,1)S(1)}, bf16[128,512]{1,0:T(8,128)(2,1)S(1)}, u32[]{:S(2)}, u32[]{:S(2)}) collective-permute-start(bf16[128,512]{1,0:T(8,128)(2,1)S(1)} %get-tuple-element.33), channel_id=1, source_target_pairs={{0,2},{1,3},{2,0},{3,1},{4,6},{5,7},{6,4},{7,5},{8,10},{9,11},{10,... | collective-permute-start | bytes 393224 | tf_op jit(solution)/shard_map/ppermute | solution.py:257
  14.0 2.4 %collective-permute-start.5 = (bf16[128,512]{1,0:T(8,128)(2,1)S(1)}, bf16[128,512]{1,0:T(8,128)(2,1)S(1)}, u32[]{:S(2)}, u32[]{:S(2)}) collective-permute-start(bf16[128,512]{1,0:T(8,128)(2,1)S(1)} %get-tuple-element.34), channel_id=1, source_target_pairs={{0,4},{1,5},{2,6},{3,7},{4,0},{5,1},{6,2},{7,3},{8,12},{9,13},{10,... | collective-permute-start | bytes 393224 | tf_op jit(solution)/shard_map/ppermute | solution.py:257
  16.5 3.4 %all-to-all-done.in_ref = bf16[8,8,2176]{2,1,0:T(8,128)(2,1)S(1)} async-done(((bf16[8,8,2176]{2,1,0:T(8,128)(2,1)}), bf16[8,8,2176]{2,1,0:T(8,128)(2,1)S(1)}, u32[]{:S(2)}, u32[]{:S(2)}) %all-to-all-start) | async-done | bytes 278560 | tf_op jit(solution)/shard_map/all_to_all | solution.py:261
  19.9 2.5 %collective-permute-start.3 = (bf16[64,512]{1,0:T(8,128)(2,1)S(1)}, bf16[64,512]{1,0:T(8,128)(2,1)S(1)}, u32[]{:S(2)}, u32[]{:S(2)}) collective-permute-start(bf16[64,512]{1,0:T(8,128)(2,1)S(1)} %own_tokens.1.refs_0_), channel_id=1, source_target_pairs={{0,24},{8,16},{16,8},{24,0},{1,25},{9,17},{17,9},{25,1},{2,26},{10... | collective-permute-start | bytes 196616 | tf_op jit(solution)/shard_map/ppermute | solution.py:257
  22.9 1.4 collective-permute-start.1
  24.3 3.9 %collective-permute-done.5.refs_7_.refs_1_.refs_6_ = bf16[128,512]{1,0:T(8,128)(2,1)S(1)} collective-permute-done((bf16[128,512]{1,0:T(8,128)(2,1)S(1)}, bf16[128,512]{1,0:T(8,128)(2,1)S(1)}, u32[]{:S(2)}, u32[]{:S(2)}) %collective-permute-start.5) | collective-permute-done | bytes 131104 | tf_op jit(solution)/shard_map/ppermute | solution.py:257
  28.2 1.0 key_value_parts.1
  29.2 3.0 %collective-permute-start.7 = (bf16[256,256]{1,0:T(8,128)(2,1)S(1)}, bf16[256,256]{1,0:T(8,128)(2,1)S(1)}, u32[]{:S(2)}, u32[]{:S(2)}) collective-permute-start(bf16[256,256]{1,0:T(8,128)(2,1)S(1)} %get-tuple-element.37), channel_id=1, source_target_pairs={{0,2},{1,3},{2,0},{3,1},{4,6},{5,7},{6,4},{7,5},{8,10},{9,11},{10,... | collective-permute-start | bytes 393224 | tf_op jit(solution)/shard_map/ppermute | solution.py:257
  32.2 2.4 %collective-permute-start.9 = (bf16[256,256]{1,0:T(8,128)(2,1)S(1)}, bf16[256,256]{1,0:T(8,128)(2,1)S(1)}, u32[]{:S(2)}, u32[]{:S(2)}) collective-permute-start(bf16[256,256]{1,0:T(8,128)(2,1)S(1)} %get-tuple-element.39), channel_id=1, source_target_pairs={{0,6},{1,7},{2,4},{3,5},{4,2},{5,3},{6,0},{7,1},{8,14},{9,15},{10,... | collective-permute-start | bytes 393224 | tf_op jit(solution)/shard_map/ppermute | solution.py:257
  34.6 4.8 %query_project.1.refs_4_ = bf16[8,56,256]{2,1,0:T(8,128)(2,1)} custom-call(bf16[8,8,2176]{2,1,0:T(8,128)(2,1)S(1)} %all-to-all-done.in_ref, bf16[2048,2048]{1,0:T(8,128)(2,1)} %bitcast.27, f32[256,256]{1,0:T(8,128)S(1)} %get-tuple-element.36.rest_0_.refs_0_), custom_call_target="tpu_custom_call" | custom-call | bytes 41943040 | tf_op jit(solution)/shard_map/query_project/pallas_call | solution.py:573
  39.4 5.1 %collective-permute-done.8.refs_2_ = bf16[256,256]{1,0:T(8,128)(2,1)S(1)} collective-permute-done((bf16[256,256]{1,0:T(8,128)(2,1)S(1)}, bf16[256,256]{1,0:T(8,128)(2,1)S(1)}, u32[]{:S(2)}, u32[]{:S(2)}) %collective-permute-start.8) | collective-permute-done | bytes 131104 | tf_op jit(solution)/shard_map/ppermute | solution.py:257
  44.5 3.6 %all-to-all-start.1 = ((bf16[8,56,256]{2,1,0:T(8,128)(2,1)}), bf16[8,56,256]{2,1,0:T(8,128)(2,1)S(1)}, u32[]{:S(2)}, u32[]{:S(2)}) async-start(bf16[8,56,256]{2,1,0:T(8,128)(2,1)} %query_project.1.refs_4_), calls=%async_computation.1 | async-start | bytes 458752 | tf_op jit(solution)/shard_map/all_to_all | solution.py:261
  48.1 0.6 collective-permute-start.14
  48.7 0.6 key_value_sum.1
  49.3 0.7 collective-permute-start.10
  50.0 5.3 %collective-permute-start.11 = (bf16[64,256]{1,0:T(8,128)(2,1)S(1)}, bf16[64,256]{1,0:T(8,128)(2,1)S(1)}, u32[]{:S(2)}, u32[]{:S(2)}) collective-permute-start(bf16[64,256]{1,0:T(8,128)(2,1)S(1)} %get-tuple-element.45), channel_id=1, source_target_pairs={{0,8},{1,0},{2,9},{3,1},{4,10},{5,2},{6,11},{7,3},{8,12},{9,4},{10... | collective-permute-start | bytes 98312 | tf_op jit(solution)/shard_map/ppermute | solution.py:257
  55.3 1.5 %collective-permute-start.12 = (bf16[64,256]{1,0:T(8,128)(2,1)S(1)}, bf16[64,256]{1,0:T(8,128)(2,1)S(1)}, u32[]{:S(2)}, u32[]{:S(2)}) collective-permute-start(bf16[64,256]{1,0:T(8,128)(2,1)S(1)} %get-tuple-element.46), channel_id=1, source_target_pairs={{0,16},{1,24},{2,17},{3,25},{4,18},{5,26},{6,19},{7,27},{8,20},{9,... | collective-permute-start | bytes 98312 | tf_op jit(solution)/shard_map/ppermute | solution.py:257
  56.9 2.3 %collective-permute-start.13 = (bf16[64,256]{1,0:T(8,128)(2,1)S(1)}, bf16[64,256]{1,0:T(8,128)(2,1)S(1)}, u32[]{:S(2)}, u32[]{:S(2)}) collective-permute-start(bf16[64,256]{1,0:T(8,128)(2,1)S(1)} %get-tuple-element.47), channel_id=1, source_target_pairs={{0,24},{1,16},{2,25},{3,17},{4,26},{5,18},{6,27},{7,19},{8,28},{9,... | collective-permute-start | bytes 98312 | tf_op jit(solution)/shard_map/ppermute | solution.py:257
  59.3 1.5 %collective-permute-done.13.refs_3_ = bf16[64,256]{1,0:T(8,128)(2,1)S(1)} collective-permute-done((bf16[64,256]{1,0:T(8,128)(2,1)S(1)}, bf16[64,256]{1,0:T(8,128)(2,1)S(1)}, u32[]{:S(2)}, u32[]{:S(2)}) %collective-permute-start.13) | collective-permute-done | bytes 32800 | tf_op jit(solution)/shard_map/ppermute | solution.py:257
  60.7 1.8 %attention.1 = bf16[8,80,256]{2,1,0:T(8,128)(2,1)S(1)} custom-call(s32[3]{0:T(128)S(1)} %pad_add_fusion.index_ref.place_ref.scalar_ref, bf16[8,56,256]{2,1,0:T(8,128)(2,1)S(1)} %all-to-all-done.1.in_ref, bf16[64,256]{1,0:T(8,128)(2,1)S(1)} %collective-permute-done.10.refs_0_, bf16[64,256]{1,0:T(8,128)(2,1)S(1)} %collective-permute-done.11.refs_1_, ...), custom_call_target="tpu_custom_call" | custom-call | tf_op jit(solution)/shard_map/attention/pallas_call | solution.py:721
  62.5 16.5 %all_to_all.30.in_ref = bf16[8,80,256]{2,1,0:T(8,128)(2,1)S(1)} all-to-all(bf16[8,80,256]{2,1,0:T(8,128)(2,1)S(1)} %attention.1), channel_id=1, replica_groups=mesh['req'=4,'tok'=8] {'tok'}, dimensions={0} | all-to-all | bytes 655360 | tf_op jit(solution)/shard_map/all_to_all | solution.py:261
  79.0 4.2 %output_project.1 = (bf16[8,24,512]{2,1,0:T(8,128)(2,1)S(1)}, bf16[16,4096]{1,0:T(8,128)(2,1)}) custom-call(bf16[8,80,256]{2,1,0:T(8,128)(2,1)S(1)} %all_to_all.30.in_ref, bf16[2048,2048]{1,0:T(8,128)(2,1)} %bitcast.28), custom_call_target="tpu_custom_call" | custom-call | tf_op jit(solution)/shard_map/output_project/pallas_call | solution.py:756
  83.2 10.7 %all_to_all.31.in_ref = bf16[8,24,512]{2,1,0:T(8,128)(2,1)S(1)} all-to-all(bf16[8,24,512]{2,1,0:T(8,128)(2,1)S(1)} %get-tuple-element.53), channel_id=1, replica_groups=mesh['req'=4,'tok'=8] {'tok'}, dimensions={0} | all-to-all | bytes 393216 | tf_op jit(solution)/shard_map/all_to_all | solution.py:261
  94.0 1.0 middle.1
  95.0 10.7 %all_to_all.32.in_ref = bf16[8,24,512]{2,1,0:T(8,128)(2,1)S(1)} all-to-all(bf16[8,24,512]{2,1,0:T(8,128)(2,1)S(1)} %get-tuple-element.55), channel_id=1, replica_groups=mesh['req'=4,'tok'=8] {'tok'}, dimensions={0} | all-to-all | bytes 393216 | tf_op jit(solution)/shard_map/all_to_all | solution.py:261
  105.7 22.2 %feedforward.1 = bf16[8,24,512]{2,1,0:T(8,128)(2,1)S(1)} custom-call(bf16[8,24,512]{2,1,0:T(8,128)(2,1)S(1)} %all_to_all.32.in_ref, bf16[2048,11264]{1,0:T(8,128)(2,1)} %bitcast.25, bf16[5632,2048]{1,0:T(8,128)(2,1)} %bitcast.26), custom_call_target="tpu_custom_call" | custom-call | tf_op jit(solution)/shard_map/feedforward/pallas_call | solution.py:864
  127.9 10.7 %all_to_all.33.in_ref = bf16[8,24,512]{2,1,0:T(8,128)(2,1)S(1)} all-to-all(bf16[8,24,512]{2,1,0:T(8,128)(2,1)S(1)} %feedforward.1), channel_id=1, replica_groups=mesh['req'=4,'tok'=8] {'tok'}, dimensions={0} | all-to-all | bytes 393216 | tf_op jit(solution)/shard_map/all_to_all | solution.py:261
  138.7 1.1 finish.1
  (27 shorter events, 0.9 us)
Async XLA Ops:
  0.6 93.3 %copy-start = (bf16[1,16,2048]{2,1,0:T(8,128)(2,1)S(1)}, bf16[1,16,2048]{2,1,0:T(8,128)(2,1)}, u32[]{:S(2)}) copy-start(bf16[1,16,2048]{2,1,0:T(8,128)(2,1)} %param.14) | copy-start | bytes 196612
  0.6 93.3 %copy-start.3 = (s32[1,16,2]{1,2,0:T(2,128)S(1)}, s32[1,16,2]{1,2,0:T(2,128)}, u32[]{:S(2)}) copy-start(s32[1,16,2]{1,2,0:T(2,128)} %param.25) | copy-start | bytes 388
  0.7 93.3 %copy-start.1 = (bf16[2048,8]{0,1:T(8,128)(2,1)S(1)}, bf16[2048,8]{0,1:T(8,128)(2,1)}, u32[]{:S(2)}) copy-start(bf16[2048,8]{0,1:T(8,128)(2,1)} %param.24) | copy-start | bytes 98308
  0.7 93.3 %copy-start.2 = (f32[2048]{0:T(1024)S(1)}, f32[2048]{0:T(1024)}, u32[]{:S(2)}) copy-start(f32[2048]{0:T(1024)} %param.18) | copy-start | bytes 24580
  0.7 19.2 %collective-permute-start = (bf16[256,1024]{1,0:T(8,128)(2,1)}, bf16[256,1024]{1,0:T(8,128)(2,1)S(1)}, u32[]{:S(2)}, u32[]{:S(2)}) collective-permute-start(bf16[256,1024]{1,0:T(8,128)(2,1)} %side_ref.1), channel_id=1, source_target_pairs={{0,1},{1,0},{2,3},{3,2},{4,5},{5,4},{6,7},{7,6},{8,9},{9,8},{10,11... | collective-permute-start | bytes 1572872 | tf_op jit(solution)/shard_map/ppermute | solution.py:257
  3.2 16.7 %all-to-all-start = ((bf16[8,8,2176]{2,1,0:T(8,128)(2,1)}), bf16[8,8,2176]{2,1,0:T(8,128)(2,1)S(1)}, u32[]{:S(2)}, u32[]{:S(2)}) async-start(bf16[8,8,2176]{2,1,0:T(8,128)(2,1)} %get-tuple-element.30), calls=%async_computation | async-start | bytes 557056 | tf_op jit(solution)/shard_map/all_to_all | solution.py:261
  11.9 11.0 %collective-permute-start.4 = (bf16[128,512]{1,0:T(8,128)(2,1)S(1)}, bf16[128,512]{1,0:T(8,128)(2,1)S(1)}, u32[]{:S(2)}, u32[]{:S(2)}) collective-permute-start(bf16[128,512]{1,0:T(8,128)(2,1)S(1)} %get-tuple-element.33), channel_id=1, source_target_pairs={{0,2},{1,3},{2,0},{3,1},{4,6},{5,7},{6,4},{7,5},{8,10},{9,11},{10,... | collective-permute-start | bytes 393224 | tf_op jit(solution)/shard_map/ppermute | solution.py:257
  14.0 14.2 %collective-permute-start.5 = (bf16[128,512]{1,0:T(8,128)(2,1)S(1)}, bf16[128,512]{1,0:T(8,128)(2,1)S(1)}, u32[]{:S(2)}, u32[]{:S(2)}) collective-permute-start(bf16[128,512]{1,0:T(8,128)(2,1)S(1)} %get-tuple-element.34), channel_id=1, source_target_pairs={{0,4},{1,5},{2,6},{3,7},{4,0},{5,1},{6,2},{7,3},{8,12},{9,13},{10,... | collective-permute-start | bytes 393224 | tf_op jit(solution)/shard_map/ppermute | solution.py:257
  16.4 11.8 %collective-permute-start.6 = (bf16[128,512]{1,0:T(8,128)(2,1)S(1)}, bf16[128,512]{1,0:T(8,128)(2,1)S(1)}, u32[]{:S(2)}, u32[]{:S(2)}) collective-permute-start(bf16[128,512]{1,0:T(8,128)(2,1)S(1)} %get-tuple-element.35), channel_id=1, source_target_pairs={{0,6},{1,7},{2,4},{3,5},{4,2},{5,3},{6,0},{7,1},{8,14},{9,15},{10,... | collective-permute-start | bytes 393224 | tf_op jit(solution)/shard_map/ppermute | solution.py:257
  19.9 8.3 %collective-permute-start.3 = (bf16[64,512]{1,0:T(8,128)(2,1)S(1)}, bf16[64,512]{1,0:T(8,128)(2,1)S(1)}, u32[]{:S(2)}, u32[]{:S(2)}) collective-permute-start(bf16[64,512]{1,0:T(8,128)(2,1)S(1)} %own_tokens.1.refs_0_), channel_id=1, source_target_pairs={{0,24},{8,16},{16,8},{24,0},{1,25},{9,17},{17,9},{25,1},{2,26},{10... | collective-permute-start | bytes 196616 | tf_op jit(solution)/shard_map/ppermute | solution.py:257
  22.4 5.8 %collective-permute-start.2 = (bf16[64,512]{1,0:T(8,128)(2,1)S(1)}, bf16[64,512]{1,0:T(8,128)(2,1)S(1)}, u32[]{:S(2)}, u32[]{:S(2)}) collective-permute-start(bf16[64,512]{1,0:T(8,128)(2,1)S(1)} %own_tokens.1.refs_0_), channel_id=1, source_target_pairs={{0,16},{8,24},{16,0},{24,8},{1,17},{9,25},{17,1},{25,9},{2,18},{10... | collective-permute-start | bytes 196616 | tf_op jit(solution)/shard_map/ppermute | solution.py:257
  22.9 5.3 %collective-permute-start.1 = (bf16[64,512]{1,0:T(8,128)(2,1)S(1)}, bf16[64,512]{1,0:T(8,128)(2,1)S(1)}, u32[]{:S(2)}, u32[]{:S(2)}) collective-permute-start(bf16[64,512]{1,0:T(8,128)(2,1)S(1)} %own_tokens.1.refs_0_), channel_id=1, source_target_pairs={{0,8},{8,0},{16,24},{24,16},{1,9},{9,1},{17,25},{25,17},{2,10},{10... | collective-permute-start | bytes 196616 | tf_op jit(solution)/shard_map/ppermute | solution.py:257
  29.2 10.2 %collective-permute-start.7 = (bf16[256,256]{1,0:T(8,128)(2,1)S(1)}, bf16[256,256]{1,0:T(8,128)(2,1)S(1)}, u32[]{:S(2)}, u32[]{:S(2)}) collective-permute-start(bf16[256,256]{1,0:T(8,128)(2,1)S(1)} %get-tuple-element.37), channel_id=1, source_target_pairs={{0,2},{1,3},{2,0},{3,1},{4,6},{5,7},{6,4},{7,5},{8,10},{9,11},{10,... | collective-permute-start | bytes 393224 | tf_op jit(solution)/shard_map/ppermute | solution.py:257
  32.2 12.3 %collective-permute-start.8 = (bf16[256,256]{1,0:T(8,128)(2,1)S(1)}, bf16[256,256]{1,0:T(8,128)(2,1)S(1)}, u32[]{:S(2)}, u32[]{:S(2)}) collective-permute-start(bf16[256,256]{1,0:T(8,128)(2,1)S(1)} %get-tuple-element.38), channel_id=1, source_target_pairs={{0,4},{1,5},{2,6},{3,7},{4,0},{5,1},{6,2},{7,3},{8,12},{9,13},{10,... | collective-permute-start | bytes 393224 | tf_op jit(solution)/shard_map/ppermute | solution.py:257
  32.2 12.3 %collective-permute-start.9 = (bf16[256,256]{1,0:T(8,128)(2,1)S(1)}, bf16[256,256]{1,0:T(8,128)(2,1)S(1)}, u32[]{:S(2)}, u32[]{:S(2)}) collective-permute-start(bf16[256,256]{1,0:T(8,128)(2,1)S(1)} %get-tuple-element.39), channel_id=1, source_target_pairs={{0,6},{1,7},{2,4},{3,5},{4,2},{5,3},{6,0},{7,1},{8,14},{9,15},{10,... | collective-permute-start | bytes 393224 | tf_op jit(solution)/shard_map/ppermute | solution.py:257
  44.5 16.2 %all-to-all-start.1 = ((bf16[8,56,256]{2,1,0:T(8,128)(2,1)}), bf16[8,56,256]{2,1,0:T(8,128)(2,1)S(1)}, u32[]{:S(2)}, u32[]{:S(2)}) async-start(bf16[8,56,256]{2,1,0:T(8,128)(2,1)} %query_project.1.refs_4_), calls=%async_computation.1 | async-start | bytes 458752 | tf_op jit(solution)/shard_map/all_to_all | solution.py:261
  48.1 12.6 %collective-permute-start.14 = (bf16[256,512]{1,0:T(8,128)(2,1)S(1)}, bf16[256,512]{1,0:T(8,128)(2,1)S(1)}, u32[]{:S(2)}, u32[]{:S(2)}) collective-permute-start(bf16[256,512]{1,0:T(8,128)(2,1)S(1)} %cache_relay.1), channel_id=1, source_target_pairs={{0,1},{1,0},{2,3},{3,2},{4,5},{5,4},{6,7},{7,6},{8,9},{9,8},{10,11... | collective-permute-start | bytes 786440 | tf_op jit(solution)/shard_map/ppermute | solution.py:257
  49.3 9.8 %collective-permute-start.10 = (bf16[64,256]{1,0:T(8,128)(2,1)S(1)}, bf16[64,256]{1,0:T(8,128)(2,1)S(1)}, u32[]{:S(2)}, u32[]{:S(2)}) collective-permute-start(bf16[64,256]{1,0:T(8,128)(2,1)S(1)} %get-tuple-element.44), channel_id=1, source_target_pairs={{0,0},{1,8},{2,1},{3,9},{4,2},{5,10},{6,3},{7,11},{8,4},{9,12},{10... | collective-permute-start | bytes 98312 | tf_op jit(solution)/shard_map/ppermute | solution.py:257
  50.0 9.1 %collective-permute-start.11 = (bf16[64,256]{1,0:T(8,128)(2,1)S(1)}, bf16[64,256]{1,0:T(8,128)(2,1)S(1)}, u32[]{:S(2)}, u32[]{:S(2)}) collective-permute-start(bf16[64,256]{1,0:T(8,128)(2,1)S(1)} %get-tuple-element.45), channel_id=1, source_target_pairs={{0,8},{1,0},{2,9},{3,1},{4,10},{5,2},{6,11},{7,3},{8,12},{9,4},{10... | collective-permute-start | bytes 98312 | tf_op jit(solution)/shard_map/ppermute | solution.py:257
  55.3 3.9 %collective-permute-start.12 = (bf16[64,256]{1,0:T(8,128)(2,1)S(1)}, bf16[64,256]{1,0:T(8,128)(2,1)S(1)}, u32[]{:S(2)}, u32[]{:S(2)}) collective-permute-start(bf16[64,256]{1,0:T(8,128)(2,1)S(1)} %get-tuple-element.46), channel_id=1, source_target_pairs={{0,16},{1,24},{2,17},{3,25},{4,18},{5,26},{6,19},{7,27},{8,20},{9,... | collective-permute-start | bytes 98312 | tf_op jit(solution)/shard_map/ppermute | solution.py:257
  56.9 3.9 %collective-permute-start.13 = (bf16[64,256]{1,0:T(8,128)(2,1)S(1)}, bf16[64,256]{1,0:T(8,128)(2,1)S(1)}, u32[]{:S(2)}, u32[]{:S(2)}) collective-permute-start(bf16[64,256]{1,0:T(8,128)(2,1)S(1)} %get-tuple-element.47), channel_id=1, source_target_pairs={{0,24},{1,16},{2,25},{3,17},{4,26},{5,18},{6,27},{7,19},{8,28},{9,... | collective-permute-start | bytes 98312 | tf_op jit(solution)/shard_map/ppermute | solution.py:257

commit v6 on v5

--- a/solution.py
+++ b/solution.py
@@ -245,11 +245,13 @@
 
 
 def column_stream(source, buffers, sems, tile):
+    count = buffers.shape[0]
+    skipped = source.shape[1] // tile - count
     return [
         pltpu.make_async_copy(
-            source.at[:, pl.ds(step * tile, tile)], buffers.at[step], sems.at[step]
+            source.at[:, pl.ds((skipped + step) * tile, tile)], buffers.at[step], sems.at[step]
         )
-        for step in range(buffers.shape[0])
+        for step in range(count)
     ]
 
 
@@ -647,7 +649,7 @@
     )(place, *parts, after)
 
 
-def attention(message, scalars, fresh_blocks, own, turned, relayed):
+def attention(message, scalars, fresh_blocks, own, turned, relayed, weight):
     blocks, _, span = message.shape
     heads = span // HEAD_DIM
     slots = blocks * CAP
@@ -656,10 +658,13 @@
     cache_rows = own.shape[0]
     scale = 1.0 / math.sqrt(HEAD_DIM)
     contract = (((1,), (1,)), ((), ()))
+    tile = weight.shape[1] // WIRE
 
     def body(scalar_ref, in_ref, *refs):
         fresh_refs, own_ref, turned_refs, relay_ref = refs[:4], refs[4], refs[5:8], refs[8]
-        out_ref = refs[9]
+        weight_ref, out_ref, held_ref, sem = refs[9:]
+        fetch = pltpu.make_async_copy(weight_ref.at[:, pl.ds(0, tile)], held_ref, sem)
+        fetch.start()
         limit, req, tok = scalar_ref[0], scalar_ref[1], scalar_ref[2]
         pieces = []
         for source in range(4):
@@ -717,24 +722,29 @@
                 out_ref[:, start : start + half, :] = pieces[2 * kind + part].reshape(
                     blocks, half, span
                 )
-
-    return pl.pallas_call(
-        body,
-        in_specs=[index_spec()] + [whole_spec()] * 10,
-        out_specs=whole_spec(),
-        out_shape=jax.ShapeDtypeStruct((blocks, slots + 4 * half, span), jnp.bfloat16),
+        fetch.wait()
+
+    return pl.pallas_call(
+        body,
+        in_specs=[index_spec()] + [whole_spec()] * 10 + [any_spec()],
+        out_specs=[whole_spec()] * 2,
+        out_shape=[
+            jax.ShapeDtypeStruct((blocks, slots + 4 * half, span), jnp.bfloat16),
+            pltpu.VMEM((weight.shape[0], tile), jnp.bfloat16),
+        ],
+        scratch_shapes=[pltpu.SemaphoreType.DMA(())],
         compiler_params=pltpu.CompilerParams(vmem_limit_bytes=14 << 20),
         name="attention",
-    )(scalars, message, *fresh_blocks, own, *turned, relayed)
-
-
-def output_project(arrived, weight, query_rows):
+    )(scalars, message, *fresh_blocks, own, *turned, relayed, *in_hbm(weight))
+
+
+def output_project(arrived, weight, ready, query_rows):
     blocks, height, span = arrived.shape
     slots = blocks * CAP
     width = weight.shape[1]
     tile = width // WIRE
 
-    def body(in_ref, weight_ref, out_ref, fresh_ref, held, sems):
+    def body(in_ref, weight_ref, ready_ref, out_ref, fresh_ref, held, sems):
         copies = column_stream(weight_ref, held, sems, tile)
         for one in copies:
             one.start()
@@ -748,34 +758,41 @@
             ]
         rows = jnp.concatenate(rows, axis=1)
         for step in range(width // tile):
-            copies[step].wait()
-            part = jnp.dot(rows, held[step], preferred_element_type=jnp.float32)
+            if step:
+                copies[step - 1].wait()
+            tile_weight = held[step - 1] if step else ready_ref[...]
+            part = jnp.dot(rows, tile_weight, preferred_element_type=jnp.float32)
             pieces.append(part.astype(jnp.bfloat16))
         out_ref[...] = pack(pieces, blocks)
 
     return pl.pallas_call(
         body,
-        in_specs=[whole_spec(), any_spec()],
+        in_specs=[whole_spec(), any_spec(), whole_spec()],
         out_specs=[whole_spec()] * 2,
         out_shape=[
             jax.ShapeDtypeStruct((blocks, WIRE * CAP, tile), jnp.bfloat16),
             jax.ShapeDtypeStruct((query_rows, 2 * width), jnp.bfloat16),
         ],
         scratch_shapes=[
-            pltpu.VMEM((width // tile, blocks * span, tile), jnp.bfloat16),
-            pltpu.SemaphoreType.DMA((width // tile,)),
+            pltpu.VMEM((width // tile - 1, blocks * span, tile), jnp.bfloat16),
+            pltpu.SemaphoreType.DMA((width // tile - 1,)),
         ],
         compiler_params=pltpu.CompilerParams(vmem_limit_bytes=14 << 20),
         name="output_project",
-    )(arrived, *in_hbm(weight))
-
-
-def middle(activations, arrived, weights, gain, router, routes):
+    )(arrived, *in_hbm(weight), *in_vmem(ready))
+
+
+def middle(activations, arrived, weights, gain, router, routes, gate_piece):
     rows, width = activations.shape
     blocks = arrived.shape[0]
     experts = router.shape[0]
 
-    def body(act_ref, in_ref, old_ref, gain_ref, router_ref, route_ref, out_ref, mix_ref, new_ref):
+    def body(
+        act_ref, in_ref, old_ref, gain_ref, router_ref, route_ref, gate_ref,
+        out_ref, mix_ref, new_ref, held_ref, sem,
+    ):
+        fetch = pltpu.make_async_copy(gate_ref.at[:, pl.ds(0, FF_TILE)], held_ref, sem)
+        fetch.start()
         route = route_ref[...]
         added = exact_mix(old_ref[...], unpack(in_ref[...]))
         mixed = (act_ref[...].astype(jnp.float32) + added).astype(jnp.bfloat16)
@@ -784,19 +801,22 @@
         picks, first = padded_picks(route, experts, CAP)
         out_ref[...] = pack(split_columns(pick_rows(picks, hidden).astype(jnp.bfloat16)), blocks)
         new_ref[...] = gate_weights(hidden, router_ref[...], route, picks, first)
-
-    return pl.pallas_call(
-        body,
-        in_specs=[whole_spec()] * 6,
-        out_specs=[whole_spec()] * 3,
+        fetch.wait()
+
+    return pl.pallas_call(
+        body,
+        in_specs=[whole_spec()] * 6 + [any_spec()],
+        out_specs=[whole_spec()] * 4,
         out_shape=[
             jax.ShapeDtypeStruct(arrived.shape, jnp.bfloat16),
             jax.ShapeDtypeStruct((rows, width), jnp.bfloat16),
             jax.ShapeDtypeStruct((blocks * CAP, rows), jnp.float32),
+            pltpu.VMEM((width, FF_TILE), jnp.bfloat16),
         ],
+        scratch_shapes=[pltpu.SemaphoreType.DMA(())],
         compiler_params=pltpu.CompilerParams(vmem_limit_bytes=4 << 20),
         name="middle",
-    )(activations, arrived, weights, gain.reshape(1, width), router, routes)
+    )(activations, arrived, weights, gain.reshape(1, width), router, routes, *in_hbm(gate_piece))
 
 
 def finish(mixed, arrived, weights):
@@ -816,7 +836,7 @@
     )(mixed, arrived, weights)
 
 
-def feedforward(arrived, gate_piece, down_piece):
+def feedforward(arrived, gate_piece, down_piece, ready):
     blocks, width = arrived.shape[0], down_piece.shape[1]
     count = blocks * CAP
     units = down_piece.shape[0]
@@ -824,7 +844,7 @@
     steps = units // tile
     slots = 4
 
-    def body(in_ref, gate_ref, down_ref, out_ref, gates, ups, downs, sems):
+    def body(in_ref, gate_ref, down_ref, ready_ref, out_ref, gates, ups, downs, sems):
         def copies(step):
             slot = step % slots
             return [
@@ -842,15 +862,17 @@
             ]
 
         for step in range(slots):
-            for one in copies(step):
+            for one in copies(step)[0 if step else 1 :]:
                 one.start()
         rows = unpack(in_ref[...])
         total = jnp.zeros((count, width), jnp.float32)
         for step in range(steps):
             slot = step % slots
             gate_copy, up_copy, down_copy = copies(step)
-            gate_copy.wait()
-            gate = jnp.dot(rows, gates[slot], preferred_element_type=jnp.float32)
+            if step:
+                gate_copy.wait()
+            gate_tile = gates[slot] if step else ready_ref[...]
+            gate = jnp.dot(rows, gate_tile, preferred_element_type=jnp.float32)
             up_copy.wait()
             up = jnp.dot(rows, ups[slot], preferred_element_type=jnp.float32)
             active = (gate / (1.0 + jnp.exp(-gate)) * up).astype(jnp.bfloat16)
@@ -863,7 +885,7 @@
 
     return pl.pallas_call(
         body,
-        in_specs=[whole_spec(), any_spec(), any_spec()],
+        in_specs=[whole_spec(), any_spec(), any_spec(), whole_spec()],
         out_specs=whole_spec(),
         out_shape=jax.ShapeDtypeStruct(arrived.shape, jnp.bfloat16),
         scratch_shapes=[
@@ -874,7 +896,7 @@
         ],
         compiler_params=pltpu.CompilerParams(vmem_limit_bytes=32 << 20),
         name="feedforward",
-    )(arrived, *in_hbm(gate_piece, down_piece))
+    )(arrived, *in_hbm(gate_piece, down_piece), *in_vmem(ready))
 
 
 def local_heads(
@@ -939,20 +961,25 @@
             dest = ((r // 2) * 2 + t % 2) ^ turn
             pairs.append((one, dest * tok_count + 4 * (r % 2) + t // 2))
         fresh_blocks.append(permute(sums[turn], ("req", "tok"), pairs))
-    attended = attention(queries, place, fresh_blocks, own_block, turned, relayed)
+    attended, output_ready = attention(
+        queries, place, fresh_blocks, own_block, turned, relayed, output_weight[0]
+    )
     attended = swap_all(attended, "tok")
-    parts_out, new_keys_values = output_project(attended, output_weight[0], query_rows)
+    parts_out, new_keys_values = output_project(
+        attended, output_weight[0], output_ready, query_rows
+    )
     output_back = swap_all(parts_out, "tok")
-    ffn_send, mixed_rows, ffn_weights = middle(
+    ffn_send, mixed_rows, ffn_weights, gate_ready = middle(
         activations[0],
         output_back,
         attn_weights,
         feedforward_gain,
         feedforward_router.T,
         ffn_routes,
+        gate_up[0],
     )
     received = swap_all(ffn_send, "tok")
-    expert_parts = feedforward(received, gate_up[0], down_weight[0])
+    expert_parts = feedforward(received, gate_up[0], down_weight[0], gate_ready)
     expert_back = swap_all(expert_parts, "tok")
     layer_output = finish(mixed_rows, expert_back, ffn_weights)
     return (layer_output[None], new_keys_values[None])

time: 140 us -> 141 us (level)
  no operation moved by 1% of the time
where the time goes in v6:
time: 141 us
  blocking collectives  48.7 us (35%)
  Pallas kernels  41.8 us (30%)
  starting transfers between devices  34.8 us (25%)
  waiting for transfers between devices  14 us (10%)
  between operations  1.44 us (1%)
    all_to_all x4, blocking collectives, swap_all(): return lax.all_to_all(values, axis, split_axis=0, concat_axis=0, tiled=True)  48.7 us
    ppermute x15, starting transfers between devices, permute(): return lax.ppermute(values, axis, pairs)  25.2 us
    pallas_call x1, Pallas kernels, feedforward(): pl.pallas_call(body, in_specs=[whole_spec(), any_spec(), any_spec(), whol...  22.1 us
    ppermute x15, waiting for transfers between devices, permute(): return lax.ppermute(values, axis, pairs)  10.6 us
    all_to_all x2, starting transfers between devices, swap_all(): return lax.all_to_all(values, axis, split_axis=0, concat_axis=0, tiled=True)  9.61 us
    pallas_call x1, Pallas kernels, query_project(): pl.pallas_call(body, in_specs=[whole_spec(), any_spec()] + [any_spec()] *...  4.75 us
    pallas_call x1, Pallas kernels, output_project(): pl.pallas_call(body, in_specs=[whole_spec(), any_spec(), whole_spec()], o...  3.86 us
    all_to_all x2, waiting for transfers between devices, swap_all(): return lax.all_to_all(values, axis, split_axis=0, concat_axis=0, tiled=True)  3.37 us
  transfers between devices with their start and end apart: 17, of which 5 were waited for; matrix products, arithmetic and copies ran while one was open for 0% of the time, Pallas kernels for 7%

profile of v6, /device:TPU:0, one launch (start us, length us, event | category | flops | bytes accessed | tf_op | source)
XLA Modules:
  0.0 140.8 jit_solution(6855842567078795450)
XLA Ops:
  0.6 0.5 collective-permute-start
  1.1 2.0 %prepare.1 = (bf16[8,8,2176]{2,1,0:T(8,128)(2,1)}, f32[48,16]{1,0:T(8,128)S(1)}) custom-call(bf16[16,2048]{1,0:T(8,128)(2,1)} %bitcast.20, f32[1,2048]{1,0:T(1,128)} %bitcast.34, bf16[8,2048]{1,0:T(8,128)(2,1)} %bitcast.33, s32[2,16]{1,0:T(2,128)} %bitcast.35), custom_call_target="tpu_custom_call" | custom-call | tf_op jit(solution)/shard_map/prepare/pallas_call | solution.py:440
  3.1 6.0 %all-to-all-start = ((bf16[8,8,2176]{2,1,0:T(8,128)(2,1)}), bf16[8,8,2176]{2,1,0:T(8,128)(2,1)S(1)}, u32[]{:S(2)}, u32[]{:S(2)}) async-start(bf16[8,8,2176]{2,1,0:T(8,128)(2,1)} %get-tuple-element.33), calls=%async_computation | async-start | bytes 557056 | tf_op jit(solution)/shard_map/all_to_all | solution.py:263
  9.9 2.0 %cache_split.1 = (bf16[64,512]{1,0:T(8,128)(2,1)S(1)}, bf16[64,512]{1,0:T(8,128)(2,1)S(1)}, bf16[128,512]{1,0:T(8,128)(2,1)S(1)}, bf16[128,512]{1,0:T(8,128)(2,1...) custom-call(s32[3]{0:T(128)S(1)} %pad_add_fusion.index_ref.place_ref.scalar_ref, ...), custom_call_target="tpu_custom_call" | custom-call | tf_op jit(solution)/shard_map/cache_split/pallas_call | solution.py:485
  11.9 2.1 %collective-permute-start.4 = (bf16[128,512]{1,0:T(8,128)(2,1)S(1)}, bf16[128,512]{1,0:T(8,128)(2,1)S(1)}, u32[]{:S(2)}, u32[]{:S(2)}) collective-permute-start(bf16[128,512]{1,0:T(8,128)(2,1)S(1)} %get-tuple-element.36), channel_id=1, source_target_pairs={{0,2},{1,3},{2,0},{3,1},{4,6},{5,7},{6,4},{7,5},{8,10},{9,11},{10,... | collective-permute-start | bytes 393224 | tf_op jit(solution)/shard_map/ppermute | solution.py:259
  14.0 2.4 %collective-permute-start.5 = (bf16[128,512]{1,0:T(8,128)(2,1)S(1)}, bf16[128,512]{1,0:T(8,128)(2,1)S(1)}, u32[]{:S(2)}, u32[]{:S(2)}) collective-permute-start(bf16[128,512]{1,0:T(8,128)(2,1)S(1)} %get-tuple-element.37), channel_id=1, source_target_pairs={{0,4},{1,5},{2,6},{3,7},{4,0},{5,1},{6,2},{7,3},{8,12},{9,13},{10,... | collective-permute-start | bytes 393224 | tf_op jit(solution)/shard_map/ppermute | solution.py:259
  16.4 3.4 %all-to-all-done.in_ref = bf16[8,8,2176]{2,1,0:T(8,128)(2,1)S(1)} async-done(((bf16[8,8,2176]{2,1,0:T(8,128)(2,1)}), bf16[8,8,2176]{2,1,0:T(8,128)(2,1)S(1)}, u32[]{:S(2)}, u32[]{:S(2)}) %all-to-all-start) | async-done | bytes 278560 | tf_op jit(solution)/shard_map/all_to_all | solution.py:263
  19.9 2.5 %collective-permute-start.3 = (bf16[64,512]{1,0:T(8,128)(2,1)S(1)}, bf16[64,512]{1,0:T(8,128)(2,1)S(1)}, u32[]{:S(2)}, u32[]{:S(2)}) collective-permute-start(bf16[64,512]{1,0:T(8,128)(2,1)S(1)} %own_tokens.1.refs_0_), channel_id=1, source_target_pairs={{0,24},{8,16},{16,8},{24,0},{1,25},{9,17},{17,9},{25,1},{2,26},{10... | collective-permute-start | bytes 196616 | tf_op jit(solution)/shard_map/ppermute | solution.py:259
  22.9 1.4 collective-permute-start.1
  24.3 3.9 %collective-permute-done.5.refs_7_.refs_1_.refs_6_ = bf16[128,512]{1,0:T(8,128)(2,1)S(1)} collective-permute-done((bf16[128,512]{1,0:T(8,128)(2,1)S(1)}, bf16[128,512]{1,0:T(8,128)(2,1)S(1)}, u32[]{:S(2)}, u32[]{:S(2)}) %collective-permute-start.5) | collective-permute-done | bytes 131104 | tf_op jit(solution)/shard_map/ppermute | solution.py:259
  28.2 1.0 key_value_parts.1
  29.2 2.9 %collective-permute-start.7 = (bf16[256,256]{1,0:T(8,128)(2,1)S(1)}, bf16[256,256]{1,0:T(8,128)(2,1)S(1)}, u32[]{:S(2)}, u32[]{:S(2)}) collective-permute-start(bf16[256,256]{1,0:T(8,128)(2,1)S(1)} %get-tuple-element.40), channel_id=1, source_target_pairs={{0,2},{1,3},{2,0},{3,1},{4,6},{5,7},{6,4},{7,5},{8,10},{9,11},{10,... | collective-permute-start | bytes 393224 | tf_op jit(solution)/shard_map/ppermute | solution.py:259
  32.2 2.4 %collective-permute-start.9 = (bf16[256,256]{1,0:T(8,128)(2,1)S(1)}, bf16[256,256]{1,0:T(8,128)(2,1)S(1)}, u32[]{:S(2)}, u32[]{:S(2)}) collective-permute-start(bf16[256,256]{1,0:T(8,128)(2,1)S(1)} %get-tuple-element.42), channel_id=1, source_target_pairs={{0,6},{1,7},{2,4},{3,5},{4,2},{5,3},{6,0},{7,1},{8,14},{9,15},{10,... | collective-permute-start | bytes 393224 | tf_op jit(solution)/shard_map/ppermute | solution.py:259
  34.6 4.8 %query_project.1.refs_4_ = bf16[8,56,256]{2,1,0:T(8,128)(2,1)} custom-call(bf16[8,8,2176]{2,1,0:T(8,128)(2,1)S(1)} %all-to-all-done.in_ref, bf16[2048,2048]{1,0:T(8,128)(2,1)} %bitcast.30, f32[256,256]{1,0:T(8,128)S(1)} %get-tuple-element.39.rest_0_.refs_0_), custom_call_target="tpu_custom_call" | custom-call | bytes 41943040 | tf_op jit(solution)/shard_map/query_project/pallas_call | solution.py:575
  39.4 5.1 %collective-permute-done.8.refs_2_ = bf16[256,256]{1,0:T(8,128)(2,1)S(1)} collective-permute-done((bf16[256,256]{1,0:T(8,128)(2,1)S(1)}, bf16[256,256]{1,0:T(8,128)(2,1)S(1)}, u32[]{:S(2)}, u32[]{:S(2)}) %collective-permute-start.8) | collective-permute-done | bytes 131104 | tf_op jit(solution)/shard_map/ppermute | solution.py:259
  44.5 3.6 %all-to-all-start.1 = ((bf16[8,56,256]{2,1,0:T(8,128)(2,1)}), bf16[8,56,256]{2,1,0:T(8,128)(2,1)S(1)}, u32[]{:S(2)}, u32[]{:S(2)}) async-start(bf16[8,56,256]{2,1,0:T(8,128)(2,1)} %query_project.1.refs_4_), calls=%async_computation.1 | async-start | bytes 458752 | tf_op jit(solution)/shard_map/all_to_all | solution.py:263
  48.1 0.6 collective-permute-start.14
  48.7 0.6 key_value_sum.1
  49.3 0.7 collective-permute-start.10
  50.0 5.3 %collective-permute-start.11 = (bf16[64,256]{1,0:T(8,128)(2,1)S(1)}, bf16[64,256]{1,0:T(8,128)(2,1)S(1)}, u32[]{:S(2)}, u32[]{:S(2)}) collective-permute-start(bf16[64,256]{1,0:T(8,128)(2,1)S(1)} %get-tuple-element.48), channel_id=1, source_target_pairs={{0,8},{1,0},{2,9},{3,1},{4,10},{5,2},{6,11},{7,3},{8,12},{9,4},{10... | collective-permute-start | bytes 98312 | tf_op jit(solution)/shard_map/ppermute | solution.py:259
  55.3 1.5 %collective-permute-start.12 = (bf16[64,256]{1,0:T(8,128)(2,1)S(1)}, bf16[64,256]{1,0:T(8,128)(2,1)S(1)}, u32[]{:S(2)}, u32[]{:S(2)}) collective-permute-start(bf16[64,256]{1,0:T(8,128)(2,1)S(1)} %get-tuple-element.49), channel_id=1, source_target_pairs={{0,16},{1,24},{2,17},{3,25},{4,18},{5,26},{6,19},{7,27},{8,20},{9,... | collective-permute-start | bytes 98312 | tf_op jit(solution)/shard_map/ppermute | solution.py:259
  56.8 2.3 %collective-permute-start.13 = (bf16[64,256]{1,0:T(8,128)(2,1)S(1)}, bf16[64,256]{1,0:T(8,128)(2,1)S(1)}, u32[]{:S(2)}, u32[]{:S(2)}) collective-permute-start(bf16[64,256]{1,0:T(8,128)(2,1)S(1)} %get-tuple-element.50), channel_id=1, source_target_pairs={{0,24},{1,16},{2,25},{3,17},{4,26},{5,18},{6,27},{7,19},{8,28},{9,... | collective-permute-start | bytes 98312 | tf_op jit(solution)/shard_map/ppermute | solution.py:259
  59.2 1.5 %collective-permute-done.13.refs_3_ = bf16[64,256]{1,0:T(8,128)(2,1)S(1)} collective-permute-done((bf16[64,256]{1,0:T(8,128)(2,1)S(1)}, bf16[64,256]{1,0:T(8,128)(2,1)S(1)}, u32[]{:S(2)}, u32[]{:S(2)}) %collective-permute-start.13) | collective-permute-done | bytes 32800 | tf_op jit(solution)/shard_map/ppermute | solution.py:259
  60.7 2.5 %attention.1 = (bf16[8,80,256]{2,1,0:T(8,128)(2,1)S(1)}, bf16[2048,512]{1,0:T(8,128)(2,1)S(1)}) custom-call(s32[3]{0:T(128)S(1)} %pad_add_fusion.index_ref.place_ref.scalar_ref, bf16[8,56,256]{2,1,0:T(8,128)(2,1)S(1)} %all-to-all-done.1.in_ref, bf16[64,256]{1,0:T(8,128)(2,1)S(1)} %collective-permute-done.10.refs_0_, ...), custom_call_target="tpu_custom_call" | custom-call | tf_op jit(solution)/shard_map/attention/pallas_call | solution.py:727
  63.3 16.5 %all_to_all.30.in_ref = bf16[8,80,256]{2,1,0:T(8,128)(2,1)S(1)} all-to-all(bf16[8,80,256]{2,1,0:T(8,128)(2,1)S(1)} %get-tuple-element.56), channel_id=1, replica_groups=mesh['req'=4,'tok'=8] {'tok'}, dimensions={0} | all-to-all | bytes 655360 | tf_op jit(solution)/shard_map/all_to_all | solution.py:263
  79.8 3.9 %output_project.1 = (bf16[8,24,512]{2,1,0:T(8,128)(2,1)S(1)}, bf16[16,4096]{1,0:T(8,128)(2,1)}) custom-call(bf16[8,80,256]{2,1,0:T(8,128)(2,1)S(1)} %all_to_all.30.in_ref, bf16[2048,2048]{1,0:T(8,128)(2,1)} %bitcast.28, bf16[2048,512]{1,0:T(8,128)(2,1)S(1)} %get-tuple-element.57.ready_ref), custom_call_target="tpu_custom_call" | custom-call | tf_op jit(solution)/shard_map/output_project/pallas_call | solution.py:768
  83.7 10.7 %all_to_all.31.in_ref = bf16[8,24,512]{2,1,0:T(8,128)(2,1)S(1)} all-to-all(bf16[8,24,512]{2,1,0:T(8,128)(2,1)S(1)} %get-tuple-element.58), channel_id=1, replica_groups=mesh['req'=4,'tok'=8] {'tok'}, dimensions={0} | all-to-all | bytes 393216 | tf_op jit(solution)/shard_map/all_to_all | solution.py:263
  94.4 1.8 %middle.1 = (bf16[8,24,512]{2,1,0:T(8,128)(2,1)S(1)}, bf16[16,2048]{1,0:T(8,128)(2,1)S(1)}, f32[48,16]{1,0:T(8,128)S(1)}, bf16[2048,512]{1,0:T(8,128)(2,1)S(1)}) custom-call(bf16[16,2048]{1,0:T(8,128)(2,1)S(1)} %bitcast.21, bf16[8,24,512]{2,1,0:T(8,128)(2,1)S(1)} %all_to_all.31.in_ref, f32[48,16]{1,0:T(8,128)S(1)} %get-tuple-element.34.after_ref.old_ref, ...), custom_call_target="tpu_custom_call" | custom-call | tf_op jit(solution)/shard_map/middle/pallas_call | solution.py:806
  96.2 10.7 %all_to_all.32.in_ref = bf16[8,24,512]{2,1,0:T(8,128)(2,1)S(1)} all-to-all(bf16[8,24,512]{2,1,0:T(8,128)(2,1)S(1)} %get-tuple-element.60), channel_id=1, replica_groups=mesh['req'=4,'tok'=8] {'tok'}, dimensions={0} | all-to-all | bytes 393216 | tf_op jit(solution)/shard_map/all_to_all | solution.py:263
  106.9 22.1 %feedforward.1 = bf16[8,24,512]{2,1,0:T(8,128)(2,1)S(1)} custom-call(bf16[8,24,512]{2,1,0:T(8,128)(2,1)S(1)} %all_to_all.32.in_ref, bf16[2048,11264]{1,0:T(8,128)(2,1)} %bitcast.26, bf16[5632,2048]{1,0:T(8,128)(2,1)} %bitcast.29, bf16[2048,512]{1,0:T(8,128)(2,1)S(1)} %get-tuple-element.61.ready_ref), custom_call_target="tpu_custom_call" | custom-call | tf_op jit(solution)/shard_map/feedforward/pallas_call | solution.py:886
  129.0 10.7 %all_to_all.33.in_ref = bf16[8,24,512]{2,1,0:T(8,128)(2,1)S(1)} all-to-all(bf16[8,24,512]{2,1,0:T(8,128)(2,1)S(1)} %feedforward.1), channel_id=1, replica_groups=mesh['req'=4,'tok'=8] {'tok'}, dimensions={0} | all-to-all | bytes 393216 | tf_op jit(solution)/shard_map/all_to_all | solution.py:263
  139.7 1.1 finish.1
  (27 shorter events, 0.9 us)
Async XLA Ops:
  0.6 19.2 %collective-permute-start = (bf16[256,1024]{1,0:T(8,128)(2,1)}, bf16[256,1024]{1,0:T(8,128)(2,1)S(1)}, u32[]{:S(2)}, u32[]{:S(2)}) collective-permute-start(bf16[256,1024]{1,0:T(8,128)(2,1)} %side_ref.1), channel_id=1, source_target_pairs={{0,1},{1,0},{2,3},{3,2},{4,5},{5,4},{6,7},{7,6},{8,9},{9,8},{10,11... | collective-permute-start | bytes 1572872 | tf_op jit(solution)/shard_map/ppermute | solution.py:259
  3.1 16.7 %all-to-all-start = ((bf16[8,8,2176]{2,1,0:T(8,128)(2,1)}), bf16[8,8,2176]{2,1,0:T(8,128)(2,1)S(1)}, u32[]{:S(2)}, u32[]{:S(2)}) async-start(bf16[8,8,2176]{2,1,0:T(8,128)(2,1)} %get-tuple-element.33), calls=%async_computation | async-start | bytes 557056 | tf_op jit(solution)/shard_map/all_to_all | solution.py:263
  11.9 11.0 %collective-permute-start.4 = (bf16[128,512]{1,0:T(8,128)(2,1)S(1)}, bf16[128,512]{1,0:T(8,128)(2,1)S(1)}, u32[]{:S(2)}, u32[]{:S(2)}) collective-permute-start(bf16[128,512]{1,0:T(8,128)(2,1)S(1)} %get-tuple-element.36), channel_id=1, source_target_pairs={{0,2},{1,3},{2,0},{3,1},{4,6},{5,7},{6,4},{7,5},{8,10},{9,11},{10,... | collective-permute-start | bytes 393224 | tf_op jit(solution)/shard_map/ppermute | solution.py:259
  14.0 14.2 %collective-permute-start.5 = (bf16[128,512]{1,0:T(8,128)(2,1)S(1)}, bf16[128,512]{1,0:T(8,128)(2,1)S(1)}, u32[]{:S(2)}, u32[]{:S(2)}) collective-permute-start(bf16[128,512]{1,0:T(8,128)(2,1)S(1)} %get-tuple-element.37), channel_id=1, source_target_pairs={{0,4},{1,5},{2,6},{3,7},{4,0},{5,1},{6,2},{7,3},{8,12},{9,13},{10,... | collective-permute-start | bytes 393224 | tf_op jit(solution)/shard_map/ppermute | solution.py:259
  16.4 11.8 %collective-permute-start.6 = (bf16[128,512]{1,0:T(8,128)(2,1)S(1)}, bf16[128,512]{1,0:T(8,128)(2,1)S(1)}, u32[]{:S(2)}, u32[]{:S(2)}) collective-permute-start(bf16[128,512]{1,0:T(8,128)(2,1)S(1)} %get-tuple-element.38), channel_id=1, source_target_pairs={{0,6},{1,7},{2,4},{3,5},{4,2},{5,3},{6,0},{7,1},{8,14},{9,15},{10,... | collective-permute-start | bytes 393224 | tf_op jit(solution)/shard_map/ppermute | solution.py:259
  19.9 8.3 %collective-permute-start.3 = (bf16[64,512]{1,0:T(8,128)(2,1)S(1)}, bf16[64,512]{1,0:T(8,128)(2,1)S(1)}, u32[]{:S(2)}, u32[]{:S(2)}) collective-permute-start(bf16[64,512]{1,0:T(8,128)(2,1)S(1)} %own_tokens.1.refs_0_), channel_id=1, source_target_pairs={{0,24},{8,16},{16,8},{24,0},{1,25},{9,17},{17,9},{25,1},{2,26},{10... | collective-permute-start | bytes 196616 | tf_op jit(solution)/shard_map/ppermute | solution.py:259
  22.4 5.8 %collective-permute-start.2 = (bf16[64,512]{1,0:T(8,128)(2,1)S(1)}, bf16[64,512]{1,0:T(8,128)(2,1)S(1)}, u32[]{:S(2)}, u32[]{:S(2)}) collective-permute-start(bf16[64,512]{1,0:T(8,128)(2,1)S(1)} %own_tokens.1.refs_0_), channel_id=1, source_target_pairs={{0,16},{8,24},{16,0},{24,8},{1,17},{9,25},{17,1},{25,9},{2,18},{10... | collective-permute-start | bytes 196616 | tf_op jit(solution)/shard_map/ppermute | solution.py:259
  22.9 5.3 %collective-permute-start.1 = (bf16[64,512]{1,0:T(8,128)(2,1)S(1)}, bf16[64,512]{1,0:T(8,128)(2,1)S(1)}, u32[]{:S(2)}, u32[]{:S(2)}) collective-permute-start(bf16[64,512]{1,0:T(8,128)(2,1)S(1)} %own_tokens.1.refs_0_), channel_id=1, source_target_pairs={{0,8},{8,0},{16,24},{24,16},{1,9},{9,1},{17,25},{25,17},{2,10},{10... | collective-permute-start | bytes 196616 | tf_op jit(solution)/shard_map/ppermute | solution.py:259
  29.2 10.1 %collective-permute-start.7 = (bf16[256,256]{1,0:T(8,128)(2,1)S(1)}, bf16[256,256]{1,0:T(8,128)(2,1)S(1)}, u32[]{:S(2)}, u32[]{:S(2)}) collective-permute-start(bf16[256,256]{1,0:T(8,128)(2,1)S(1)} %get-tuple-element.40), channel_id=1, source_target_pairs={{0,2},{1,3},{2,0},{3,1},{4,6},{5,7},{6,4},{7,5},{8,10},{9,11},{10,... | collective-permute-start | bytes 393224 | tf_op jit(solution)/shard_map/ppermute | solution.py:259
  32.2 12.3 %collective-permute-start.8 = (bf16[256,256]{1,0:T(8,128)(2,1)S(1)}, bf16[256,256]{1,0:T(8,128)(2,1)S(1)}, u32[]{:S(2)}, u32[]{:S(2)}) collective-permute-start(bf16[256,256]{1,0:T(8,128)(2,1)S(1)} %get-tuple-element.41), channel_id=1, source_target_pairs={{0,4},{1,5},{2,6},{3,7},{4,0},{5,1},{6,2},{7,3},{8,12},{9,13},{10,... | collective-permute-start | bytes 393224 | tf_op jit(solution)/shard_map/ppermute | solution.py:259
  32.2 12.3 %collective-permute-start.9 = (bf16[256,256]{1,0:T(8,128)(2,1)S(1)}, bf16[256,256]{1,0:T(8,128)(2,1)S(1)}, u32[]{:S(2)}, u32[]{:S(2)}) collective-permute-start(bf16[256,256]{1,0:T(8,128)(2,1)S(1)} %get-tuple-element.42), channel_id=1, source_target_pairs={{0,6},{1,7},{2,4},{3,5},{4,2},{5,3},{6,0},{7,1},{8,14},{9,15},{10,... | collective-permute-start | bytes 393224 | tf_op jit(solution)/shard_map/ppermute | solution.py:259
  44.5 16.2 %all-to-all-start.1 = ((bf16[8,56,256]{2,1,0:T(8,128)(2,1)}), bf16[8,56,256]{2,1,0:T(8,128)(2,1)S(1)}, u32[]{:S(2)}, u32[]{:S(2)}) async-start(bf16[8,56,256]{2,1,0:T(8,128)(2,1)} %query_project.1.refs_4_), calls=%async_computation.1 | async-start | bytes 458752 | tf_op jit(solution)/shard_map/all_to_all | solution.py:263
  48.1 12.6 %collective-permute-start.14 = (bf16[256,512]{1,0:T(8,128)(2,1)S(1)}, bf16[256,512]{1,0:T(8,128)(2,1)S(1)}, u32[]{:S(2)}, u32[]{:S(2)}) collective-permute-start(bf16[256,512]{1,0:T(8,128)(2,1)S(1)} %cache_relay.1), channel_id=1, source_target_pairs={{0,1},{1,0},{2,3},{3,2},{4,5},{5,4},{6,7},{7,6},{8,9},{9,8},{10,11... | collective-permute-start | bytes 786440 | tf_op jit(solution)/shard_map/ppermute | solution.py:259
  49.3 9.8 %collective-permute-start.10 = (bf16[64,256]{1,0:T(8,128)(2,1)S(1)}, bf16[64,256]{1,0:T(8,128)(2,1)S(1)}, u32[]{:S(2)}, u32[]{:S(2)}) collective-permute-start(bf16[64,256]{1,0:T(8,128)(2,1)S(1)} %get-tuple-element.47), channel_id=1, source_target_pairs={{0,0},{1,8},{2,1},{3,9},{4,2},{5,10},{6,3},{7,11},{8,4},{9,12},{10... | collective-permute-start | bytes 98312 | tf_op jit(solution)/shard_map/ppermute | solution.py:259
  50.0 9.1 %collective-permute-start.11 = (bf16[64,256]{1,0:T(8,128)(2,1)S(1)}, bf16[64,256]{1,0:T(8,128)(2,1)S(1)}, u32[]{:S(2)}, u32[]{:S(2)}) collective-permute-start(bf16[64,256]{1,0:T(8,128)(2,1)S(1)} %get-tuple-element.48), channel_id=1, source_target_pairs={{0,8},{1,0},{2,9},{3,1},{4,10},{5,2},{6,11},{7,3},{8,12},{9,4},{10... | collective-permute-start | bytes 98312 | tf_op jit(solution)/shard_map/ppermute | solution.py:259
  55.3 3.9 %collective-permute-start.12 = (bf16[64,256]{1,0:T(8,128)(2,1)S(1)}, bf16[64,256]{1,0:T(8,128)(2,1)S(1)}, u32[]{:S(2)}, u32[]{:S(2)}) collective-permute-start(bf16[64,256]{1,0:T(8,128)(2,1)S(1)} %get-tuple-element.49), channel_id=1, source_target_pairs={{0,16},{1,24},{2,17},{3,25},{4,18},{5,26},{6,19},{7,27},{8,20},{9,... | collective-permute-start | bytes 98312 | tf_op jit(solution)/shard_map/ppermute | solution.py:259
  56.8 3.9 %collective-permute-start.13 = (bf16[64,256]{1,0:T(8,128)(2,1)S(1)}, bf16[64,256]{1,0:T(8,128)(2,1)S(1)}, u32[]{:S(2)}, u32[]{:S(2)}) collective-permute-start(bf16[64,256]{1,0:T(8,128)(2,1)S(1)} %get-tuple-element.50), channel_id=1, source_target_pairs={{0,24},{1,16},{2,25},{3,17},{4,26},{5,18},{6,27},{7,19},{8,28},{9,... | collective-permute-start | bytes 98312 | tf_op jit(solution)/shard_map/ppermute | solution.py:259
  60.7 33.7 %copy-start = (bf16[1,16,2048]{2,1,0:T(8,128)(2,1)S(1)}, bf16[1,16,2048]{2,1,0:T(8,128)(2,1)}, u32[]{:S(2)}) copy-start(bf16[1,16,2048]{2,1,0:T(8,128)(2,1)} %param.14) | copy-start | bytes 196612
  60.7 33.7 %copy-start.1 = (bf16[2048,8]{0,1:T(8,128)(2,1)S(1)}, bf16[2048,8]{0,1:T(8,128)(2,1)}, u32[]{:S(2)}) copy-start(bf16[2048,8]{0,1:T(8,128)(2,1)} %param.24) | copy-start | bytes 98308
  60.7 33.7 %copy-start.2 = (f32[2048]{0:T(1024)S(1)}, f32[2048]{0:T(1024)}, u32[]{:S(2)}) copy-start(f32[2048]{0:T(1024)} %param.18) | copy-start | bytes 24580
  60.7 33.7 %copy-start.3 = (s32[1,16,2]{1,2,0:T(2,128)S(1)}, s32[1,16,2]{1,2,0:T(2,128)}, u32[]{:S(2)}) copy-start(s32[1,16,2]{1,2,0:T(2,128)} %param.25) | copy-start | bytes 388

commit v7 on v5

--- a/solution.py
+++ b/solution.py
@@ -492,7 +492,7 @@
     )(place, *in_hbm(cache_part, side), after)
 
 
-def cache_relay(near, turned):
+def cache_relay(near, turned, after):
     rows, width = near.shape
 
     def body(near_ref, *refs):
@@ -503,12 +503,12 @@
 
     return pl.pallas_call(
         body,
-        in_specs=[whole_spec()] * 4,
+        in_specs=[whole_spec()] * 4 + [any_spec()],
         out_specs=whole_spec(),
         out_shape=jax.ShapeDtypeStruct((4 * rows, width), near.dtype),
         compiler_params=pltpu.CompilerParams(vmem_limit_bytes=3 << 20),
         name="cache_relay",
-    )(near, *turned)
+    )(near, *turned, after)
 
 
 def own_tokens(arrived, after, tok_count, width):
@@ -930,7 +930,7 @@
     parts[1:], turned = gate[:3], gate[3:]
     sums = key_value_sum(parts, place, projected)
     queries = swap_all(projected, "tok")
-    relayed = permute(cache_relay(near, turned), "tok", pair)
+    relayed = permute(cache_relay(near, turned, sums[0]), "tok", pair)
     fresh_blocks = []
     for turn in range(4):
         pairs = []

time: 140 us -> 140 us (level)
  starting transfers between devices: 34.8 us -> 32.1 us
  waiting for transfers between devices: 13.9 us -> 15.7 us
    ppermute x15, starting transfers between devices: 25.2 us -> 22.5 us  [permute(): return lax.ppermute(values, axis, pairs)]
    all_to_all x2, waiting for transfers between devices: 3.37 us -> 5.75 us  [swap_all(): return lax.all_to_all(values, axis, split_axis=0, concat_axis=0, tiled=True)]
where the time goes in v7:
time: 140 us; the launch traced here: 139 us
  blocking collectives  48.9 us (35%)
  Pallas kernels  40.7 us (29%)
  starting transfers between devices  32.1 us (23%)
  waiting for transfers between devices  15.7 us (11%)
  between operations  1.47 us (1%)
    all_to_all x4, blocking collectives, swap_all(): return lax.all_to_all(values, axis, split_axis=0, concat_axis=0, tiled=True)  48.9 us
    ppermute x15, starting transfers between devices, permute(): return lax.ppermute(values, axis, pairs)  22.5 us
    pallas_call x1, Pallas kernels, feedforward(): pl.pallas_call(body, in_specs=[whole_spec(), any_spec(), any_spec()], out...  22.2 us
    ppermute x15, waiting for transfers between devices, permute(): return lax.ppermute(values, axis, pairs)  9.91 us
    all_to_all x2, starting transfers between devices, swap_all(): return lax.all_to_all(values, axis, split_axis=0, concat_axis=0, tiled=True)  9.62 us
    all_to_all x2, waiting for transfers between devices, swap_all(): return lax.all_to_all(values, axis, split_axis=0, concat_axis=0, tiled=True)  5.75 us
    pallas_call x1, Pallas kernels, query_project(): pl.pallas_call(body, in_specs=[whole_spec(), any_spec()] + [any_spec()] *...  4.76 us
    pallas_call x1, Pallas kernels, output_project(): pl.pallas_call(body, in_specs=[whole_spec(), any_spec()], out_specs=[whol...  4.21 us
  transfers between devices with their start and end apart: 17, of which 5 were waited for; matrix products, arithmetic and copies ran while one was open for 0% of the time, Pallas kernels for 7%

profile of v7, /device:TPU:0, one launch (start us, length us, event | category | flops | bytes accessed | tf_op | source)
XLA Modules:
  0.0 139.0 jit_solution(9467961229648443803)
XLA Ops:
  1.2 2.0 %prepare.1 = (bf16[8,8,2176]{2,1,0:T(8,128)(2,1)}, f32[48,16]{1,0:T(8,128)S(1)}) custom-call(bf16[16,2048]{1,0:T(8,128)(2,1)} %bitcast.20, f32[1,2048]{1,0:T(1,128)} %bitcast.32, bf16[8,2048]{1,0:T(8,128)(2,1)} %bitcast.31, s32[2,16]{1,0:T(2,128)} %bitcast.33), custom_call_target="tpu_custom_call" | custom-call | tf_op jit(solution)/shard_map/prepare/pallas_call | solution.py:438
  3.2 6.0 %all-to-all-start = ((bf16[8,8,2176]{2,1,0:T(8,128)(2,1)}), bf16[8,8,2176]{2,1,0:T(8,128)(2,1)S(1)}, u32[]{:S(2)}, u32[]{:S(2)}) async-start(bf16[8,8,2176]{2,1,0:T(8,128)(2,1)} %get-tuple-element.30), calls=%async_computation | async-start | bytes 557056 | tf_op jit(solution)/shard_map/all_to_all | solution.py:261
  9.9 2.0 %cache_split.1 = (bf16[64,512]{1,0:T(8,128)(2,1)S(1)}, bf16[64,512]{1,0:T(8,128)(2,1)S(1)}, bf16[128,512]{1,0:T(8,128)(2,1)S(1)}, bf16[128,512]{1,0:T(8,128)(2,1...) custom-call(s32[3]{0:T(128)S(1)} %pad_add_fusion.index_ref.place_ref.scalar_ref, ...), custom_call_target="tpu_custom_call" | custom-call | tf_op jit(solution)/shard_map/cache_split/pallas_call | solution.py:483
  11.9 2.1 %collective-permute-start.4 = (bf16[128,512]{1,0:T(8,128)(2,1)S(1)}, bf16[128,512]{1,0:T(8,128)(2,1)S(1)}, u32[]{:S(2)}, u32[]{:S(2)}) collective-permute-start(bf16[128,512]{1,0:T(8,128)(2,1)S(1)} %get-tuple-element.33), channel_id=1, source_target_pairs={{0,2},{1,3},{2,0},{3,1},{4,6},{5,7},{6,4},{7,5},{8,10},{9,11},{10,... | collective-permute-start | bytes 393224 | tf_op jit(solution)/shard_map/ppermute | solution.py:257
  14.0 2.4 %collective-permute-start.5 = (bf16[128,512]{1,0:T(8,128)(2,1)S(1)}, bf16[128,512]{1,0:T(8,128)(2,1)S(1)}, u32[]{:S(2)}, u32[]{:S(2)}) collective-permute-start(bf16[128,512]{1,0:T(8,128)(2,1)S(1)} %get-tuple-element.34), channel_id=1, source_target_pairs={{0,4},{1,5},{2,6},{3,7},{4,0},{5,1},{6,2},{7,3},{8,12},{9,13},{10,... | collective-permute-start | bytes 393224 | tf_op jit(solution)/shard_map/ppermute | solution.py:257
  16.5 3.4 %all-to-all-done.in_ref = bf16[8,8,2176]{2,1,0:T(8,128)(2,1)S(1)} async-done(((bf16[8,8,2176]{2,1,0:T(8,128)(2,1)}), bf16[8,8,2176]{2,1,0:T(8,128)(2,1)S(1)}, u32[]{:S(2)}, u32[]{:S(2)}) %all-to-all-start) | async-done | bytes 278560 | tf_op jit(solution)/shard_map/all_to_all | solution.py:261
  19.9 2.5 %collective-permute-start.3 = (bf16[64,512]{1,0:T(8,128)(2,1)S(1)}, bf16[64,512]{1,0:T(8,128)(2,1)S(1)}, u32[]{:S(2)}, u32[]{:S(2)}) collective-permute-start(bf16[64,512]{1,0:T(8,128)(2,1)S(1)} %own_tokens.1.refs_0_), channel_id=1, source_target_pairs={{0,24},{8,16},{16,8},{24,0},{1,25},{9,17},{17,9},{25,1},{2,26},{10... | collective-permute-start | bytes 196616 | tf_op jit(solution)/shard_map/ppermute | solution.py:257
  22.9 1.4 %collective-permute-start.1 = (bf16[64,512]{1,0:T(8,128)(2,1)S(1)}, bf16[64,512]{1,0:T(8,128)(2,1)S(1)}, u32[]{:S(2)}, u32[]{:S(2)}) collective-permute-start(bf16[64,512]{1,0:T(8,128)(2,1)S(1)} %own_tokens.1.refs_0_), channel_id=1, source_target_pairs={{0,8},{8,0},{16,24},{24,16},{1,9},{9,1},{17,25},{25,17},{2,10},{10... | collective-permute-start | bytes 196616 | tf_op jit(solution)/shard_map/ppermute | solution.py:257
  24.3 3.9 %collective-permute-done.5.refs_7_.refs_1_.refs_6_ = bf16[128,512]{1,0:T(8,128)(2,1)S(1)} collective-permute-done((bf16[128,512]{1,0:T(8,128)(2,1)S(1)}, bf16[128,512]{1,0:T(8,128)(2,1)S(1)}, u32[]{:S(2)}, u32[]{:S(2)}) %collective-permute-start.5) | collective-permute-done | bytes 131104 | tf_op jit(solution)/shard_map/ppermute | solution.py:257
  28.2 1.0 key_value_parts.1
  29.2 3.0 %collective-permute-start.7 = (bf16[256,256]{1,0:T(8,128)(2,1)S(1)}, bf16[256,256]{1,0:T(8,128)(2,1)S(1)}, u32[]{:S(2)}, u32[]{:S(2)}) collective-permute-start(bf16[256,256]{1,0:T(8,128)(2,1)S(1)} %get-tuple-element.37), channel_id=1, source_target_pairs={{0,2},{1,3},{2,0},{3,1},{4,6},{5,7},{6,4},{7,5},{8,10},{9,11},{10,... | collective-permute-start | bytes 393224 | tf_op jit(solution)/shard_map/ppermute | solution.py:257
  32.2 2.4 %collective-permute-start.9 = (bf16[256,256]{1,0:T(8,128)(2,1)S(1)}, bf16[256,256]{1,0:T(8,128)(2,1)S(1)}, u32[]{:S(2)}, u32[]{:S(2)}) collective-permute-start(bf16[256,256]{1,0:T(8,128)(2,1)S(1)} %get-tuple-element.39), channel_id=1, source_target_pairs={{0,6},{1,7},{2,4},{3,5},{4,2},{5,3},{6,0},{7,1},{8,14},{9,15},{10,... | collective-permute-start | bytes 393224 | tf_op jit(solution)/shard_map/ppermute | solution.py:257
  34.6 4.8 %query_project.1.refs_4_ = bf16[8,56,256]{2,1,0:T(8,128)(2,1)} custom-call(bf16[8,8,2176]{2,1,0:T(8,128)(2,1)S(1)} %all-to-all-done.in_ref, bf16[2048,2048]{1,0:T(8,128)(2,1)} %bitcast.27, f32[256,256]{1,0:T(8,128)S(1)} %get-tuple-element.36.rest_0_.refs_0_), custom_call_target="tpu_custom_call" | custom-call | bytes 41943040 | tf_op jit(solution)/shard_map/query_project/pallas_call | solution.py:573
  39.4 5.1 %collective-permute-done.8.refs_2_ = bf16[256,256]{1,0:T(8,128)(2,1)S(1)} collective-permute-done((bf16[256,256]{1,0:T(8,128)(2,1)S(1)}, bf16[256,256]{1,0:T(8,128)(2,1)S(1)}, u32[]{:S(2)}, u32[]{:S(2)}) %collective-permute-start.8) | collective-permute-done | bytes 131104 | tf_op jit(solution)/shard_map/ppermute | solution.py:257
  44.5 3.6 %all-to-all-start.1 = ((bf16[8,56,256]{2,1,0:T(8,128)(2,1)}), bf16[8,56,256]{2,1,0:T(8,128)(2,1)S(1)}, u32[]{:S(2)}, u32[]{:S(2)}) async-start(bf16[8,56,256]{2,1,0:T(8,128)(2,1)} %query_project.1.refs_4_), calls=%async_computation.1 | async-start | bytes 458752 | tf_op jit(solution)/shard_map/all_to_all | solution.py:261
  48.1 0.6 key_value_sum.1
  48.8 0.6 collective-permute-start.14
  49.3 1.5 %collective-permute-start.11 = (bf16[64,256]{1,0:T(8,128)(2,1)S(1)}, bf16[64,256]{1,0:T(8,128)(2,1)S(1)}, u32[]{:S(2)}, u32[]{:S(2)}) collective-permute-start(bf16[64,256]{1,0:T(8,128)(2,1)S(1)} %get-tuple-element.45), channel_id=1, source_target_pairs={{0,8},{1,0},{2,9},{3,1},{4,10},{5,2},{6,11},{7,3},{8,12},{9,4},{10... | collective-permute-start | bytes 98312 | tf_op jit(solution)/shard_map/ppermute | solution.py:257
  50.8 1.5 %collective-permute-start.12 = (bf16[64,256]{1,0:T(8,128)(2,1)S(1)}, bf16[64,256]{1,0:T(8,128)(2,1)S(1)}, u32[]{:S(2)}, u32[]{:S(2)}) collective-permute-start(bf16[64,256]{1,0:T(8,128)(2,1)S(1)} %get-tuple-element.46), channel_id=1, source_target_pairs={{0,16},{1,24},{2,17},{3,25},{4,18},{5,26},{6,19},{7,27},{8,20},{9,... | collective-permute-start | bytes 98312 | tf_op jit(solution)/shard_map/ppermute | solution.py:257
  52.4 3.4 %collective-permute-start.13 = (bf16[64,256]{1,0:T(8,128)(2,1)S(1)}, bf16[64,256]{1,0:T(8,128)(2,1)S(1)}, u32[]{:S(2)}, u32[]{:S(2)}) collective-permute-start(bf16[64,256]{1,0:T(8,128)(2,1)S(1)} %get-tuple-element.47), channel_id=1, source_target_pairs={{0,24},{1,16},{2,25},{3,17},{4,26},{5,18},{6,27},{7,19},{8,28},{9,... | collective-permute-start | bytes 98312 | tf_op jit(solution)/shard_map/ppermute | solution.py:257
  55.8 0.7 collective-permute-start.10
  56.4 0.9 collective-permute-done.13.refs_3_
  57.4 2.4 %all-to-all-done.1.in_ref = bf16[8,56,256]{2,1,0:T(8,128)(2,1)S(1)} async-done(((bf16[8,56,256]{2,1,0:T(8,128)(2,1)}), bf16[8,56,256]{2,1,0:T(8,128)(2,1)S(1)}, u32[]{:S(2)}, u32[]{:S(2)}) %all-to-all-start.1) | async-done | bytes 229408 | tf_op jit(solution)/shard_map/all_to_all | solution.py:261
  59.7 1.8 %attention.1 = bf16[8,80,256]{2,1,0:T(8,128)(2,1)S(1)} custom-call(s32[3]{0:T(128)S(1)} %pad_add_fusion.index_ref.place_ref.scalar_ref, bf16[8,56,256]{2,1,0:T(8,128)(2,1)S(1)} %all-to-all-done.1.in_ref, bf16[64,256]{1,0:T(8,128)(2,1)S(1)} %collective-permute-done.10.refs_0_, bf16[64,256]{1,0:T(8,128)(2,1)S(1)} %collective-permute-done.11.refs_1_, ...), custom_call_target="tpu_custom_call" | custom-call | tf_op jit(solution)/shard_map/attention/pallas_call | solution.py:721
  61.5 16.7 %all_to_all.30.in_ref = bf16[8,80,256]{2,1,0:T(8,128)(2,1)S(1)} all-to-all(bf16[8,80,256]{2,1,0:T(8,128)(2,1)S(1)} %attention.1), channel_id=1, replica_groups=mesh['req'=4,'tok'=8] {'tok'}, dimensions={0} | all-to-all | bytes 655360 | tf_op jit(solution)/shard_map/all_to_all | solution.py:261
  78.2 4.2 %output_project.1 = (bf16[8,24,512]{2,1,0:T(8,128)(2,1)S(1)}, bf16[16,4096]{1,0:T(8,128)(2,1)}) custom-call(bf16[8,80,256]{2,1,0:T(8,128)(2,1)S(1)} %all_to_all.30.in_ref, bf16[2048,2048]{1,0:T(8,128)(2,1)} %bitcast.28), custom_call_target="tpu_custom_call" | custom-call | tf_op jit(solution)/shard_map/output_project/pallas_call | solution.py:756
  82.4 10.7 %all_to_all.31.in_ref = bf16[8,24,512]{2,1,0:T(8,128)(2,1)S(1)} all-to-all(bf16[8,24,512]{2,1,0:T(8,128)(2,1)S(1)} %get-tuple-element.53), channel_id=1, replica_groups=mesh['req'=4,'tok'=8] {'tok'}, dimensions={0} | all-to-all | bytes 393216 | tf_op jit(solution)/shard_map/all_to_all | solution.py:261
  93.2 1.0 middle.1
  94.2 10.7 %all_to_all.32.in_ref = bf16[8,24,512]{2,1,0:T(8,128)(2,1)S(1)} all-to-all(bf16[8,24,512]{2,1,0:T(8,128)(2,1)S(1)} %get-tuple-element.55), channel_id=1, replica_groups=mesh['req'=4,'tok'=8] {'tok'}, dimensions={0} | all-to-all | bytes 393216 | tf_op jit(solution)/shard_map/all_to_all | solution.py:261
  105.0 22.2 %feedforward.1 = bf16[8,24,512]{2,1,0:T(8,128)(2,1)S(1)} custom-call(bf16[8,24,512]{2,1,0:T(8,128)(2,1)S(1)} %all_to_all.32.in_ref, bf16[2048,11264]{1,0:T(8,128)(2,1)} %bitcast.25, bf16[5632,2048]{1,0:T(8,128)(2,1)} %bitcast.26), custom_call_target="tpu_custom_call" | custom-call | tf_op jit(solution)/shard_map/feedforward/pallas_call | solution.py:864
  127.1 10.7 %all_to_all.33.in_ref = bf16[8,24,512]{2,1,0:T(8,128)(2,1)S(1)} all-to-all(bf16[8,24,512]{2,1,0:T(8,128)(2,1)S(1)} %feedforward.1), channel_id=1, replica_groups=mesh['req'=4,'tok'=8] {'tok'}, dimensions={0} | all-to-all | bytes 393216 | tf_op jit(solution)/shard_map/all_to_all | solution.py:261
  137.9 1.1 finish.1
  (27 shorter events, 1.3 us)
Async XLA Ops:
  0.6 92.5 %copy-start = (bf16[1,16,2048]{2,1,0:T(8,128)(2,1)S(1)}, bf16[1,16,2048]{2,1,0:T(8,128)(2,1)}, u32[]{:S(2)}) copy-start(bf16[1,16,2048]{2,1,0:T(8,128)(2,1)} %param.14) | copy-start | bytes 196612
  0.6 92.5 %copy-start.3 = (s32[1,16,2]{1,2,0:T(2,128)S(1)}, s32[1,16,2]{1,2,0:T(2,128)}, u32[]{:S(2)}) copy-start(s32[1,16,2]{1,2,0:T(2,128)} %param.25) | copy-start | bytes 388
  0.7 92.5 %copy-start.1 = (bf16[2048,8]{0,1:T(8,128)(2,1)S(1)}, bf16[2048,8]{0,1:T(8,128)(2,1)}, u32[]{:S(2)}) copy-start(bf16[2048,8]{0,1:T(8,128)(2,1)} %param.24) | copy-start | bytes 98308
  0.7 92.5 %copy-start.2 = (f32[2048]{0:T(1024)S(1)}, f32[2048]{0:T(1024)}, u32[]{:S(2)}) copy-start(f32[2048]{0:T(1024)} %param.18) | copy-start | bytes 24580
  0.7 19.2 %collective-permute-start = (bf16[256,1024]{1,0:T(8,128)(2,1)}, bf16[256,1024]{1,0:T(8,128)(2,1)S(1)}, u32[]{:S(2)}, u32[]{:S(2)}) collective-permute-start(bf16[256,1024]{1,0:T(8,128)(2,1)} %side_ref.1), channel_id=1, source_target_pairs={{0,1},{1,0},{2,3},{3,2},{4,5},{5,4},{6,7},{7,6},{8,9},{9,8},{10,11... | collective-permute-start | bytes 1572872 | tf_op jit(solution)/shard_map/ppermute | solution.py:257
  3.2 16.7 %all-to-all-start = ((bf16[8,8,2176]{2,1,0:T(8,128)(2,1)}), bf16[8,8,2176]{2,1,0:T(8,128)(2,1)S(1)}, u32[]{:S(2)}, u32[]{:S(2)}) async-start(bf16[8,8,2176]{2,1,0:T(8,128)(2,1)} %get-tuple-element.30), calls=%async_computation | async-start | bytes 557056 | tf_op jit(solution)/shard_map/all_to_all | solution.py:261
  11.9 11.0 %collective-permute-start.4 = (bf16[128,512]{1,0:T(8,128)(2,1)S(1)}, bf16[128,512]{1,0:T(8,128)(2,1)S(1)}, u32[]{:S(2)}, u32[]{:S(2)}) collective-permute-start(bf16[128,512]{1,0:T(8,128)(2,1)S(1)} %get-tuple-element.33), channel_id=1, source_target_pairs={{0,2},{1,3},{2,0},{3,1},{4,6},{5,7},{6,4},{7,5},{8,10},{9,11},{10,... | collective-permute-start | bytes 393224 | tf_op jit(solution)/shard_map/ppermute | solution.py:257
  14.0 14.2 %collective-permute-start.5 = (bf16[128,512]{1,0:T(8,128)(2,1)S(1)}, bf16[128,512]{1,0:T(8,128)(2,1)S(1)}, u32[]{:S(2)}, u32[]{:S(2)}) collective-permute-start(bf16[128,512]{1,0:T(8,128)(2,1)S(1)} %get-tuple-element.34), channel_id=1, source_target_pairs={{0,4},{1,5},{2,6},{3,7},{4,0},{5,1},{6,2},{7,3},{8,12},{9,13},{10,... | collective-permute-start | bytes 393224 | tf_op jit(solution)/shard_map/ppermute | solution.py:257
  16.4 11.8 %collective-permute-start.6 = (bf16[128,512]{1,0:T(8,128)(2,1)S(1)}, bf16[128,512]{1,0:T(8,128)(2,1)S(1)}, u32[]{:S(2)}, u32[]{:S(2)}) collective-permute-start(bf16[128,512]{1,0:T(8,128)(2,1)S(1)} %get-tuple-element.35), channel_id=1, source_target_pairs={{0,6},{1,7},{2,4},{3,5},{4,2},{5,3},{6,0},{7,1},{8,14},{9,15},{10,... | collective-permute-start | bytes 393224 | tf_op jit(solution)/shard_map/ppermute | solution.py:257
  19.9 8.3 %collective-permute-start.3 = (bf16[64,512]{1,0:T(8,128)(2,1)S(1)}, bf16[64,512]{1,0:T(8,128)(2,1)S(1)}, u32[]{:S(2)}, u32[]{:S(2)}) collective-permute-start(bf16[64,512]{1,0:T(8,128)(2,1)S(1)} %own_tokens.1.refs_0_), channel_id=1, source_target_pairs={{0,24},{8,16},{16,8},{24,0},{1,25},{9,17},{17,9},{25,1},{2,26},{10... | collective-permute-start | bytes 196616 | tf_op jit(solution)/shard_map/ppermute | solution.py:257
  22.4 5.8 %collective-permute-start.2 = (bf16[64,512]{1,0:T(8,128)(2,1)S(1)}, bf16[64,512]{1,0:T(8,128)(2,1)S(1)}, u32[]{:S(2)}, u32[]{:S(2)}) collective-permute-start(bf16[64,512]{1,0:T(8,128)(2,1)S(1)} %own_tokens.1.refs_0_), channel_id=1, source_target_pairs={{0,16},{8,24},{16,0},{24,8},{1,17},{9,25},{17,1},{25,9},{2,18},{10... | collective-permute-start | bytes 196616 | tf_op jit(solution)/shard_map/ppermute | solution.py:257
  22.9 5.3 %collective-permute-start.1 = (bf16[64,512]{1,0:T(8,128)(2,1)S(1)}, bf16[64,512]{1,0:T(8,128)(2,1)S(1)}, u32[]{:S(2)}, u32[]{:S(2)}) collective-permute-start(bf16[64,512]{1,0:T(8,128)(2,1)S(1)} %own_tokens.1.refs_0_), channel_id=1, source_target_pairs={{0,8},{8,0},{16,24},{24,16},{1,9},{9,1},{17,25},{25,17},{2,10},{10... | collective-permute-start | bytes 196616 | tf_op jit(solution)/shard_map/ppermute | solution.py:257
  29.2 10.2 %collective-permute-start.7 = (bf16[256,256]{1,0:T(8,128)(2,1)S(1)}, bf16[256,256]{1,0:T(8,128)(2,1)S(1)}, u32[]{:S(2)}, u32[]{:S(2)}) collective-permute-start(bf16[256,256]{1,0:T(8,128)(2,1)S(1)} %get-tuple-element.37), channel_id=1, source_target_pairs={{0,2},{1,3},{2,0},{3,1},{4,6},{5,7},{6,4},{7,5},{8,10},{9,11},{10,... | collective-permute-start | bytes 393224 | tf_op jit(solution)/shard_map/ppermute | solution.py:257
  32.2 12.3 %collective-permute-start.8 = (bf16[256,256]{1,0:T(8,128)(2,1)S(1)}, bf16[256,256]{1,0:T(8,128)(2,1)S(1)}, u32[]{:S(2)}, u32[]{:S(2)}) collective-permute-start(bf16[256,256]{1,0:T(8,128)(2,1)S(1)} %get-tuple-element.38), channel_id=1, source_target_pairs={{0,4},{1,5},{2,6},{3,7},{4,0},{5,1},{6,2},{7,3},{8,12},{9,13},{10,... | collective-permute-start | bytes 393224 | tf_op jit(solution)/shard_map/ppermute | solution.py:257
  32.2 12.3 %collective-permute-start.9 = (bf16[256,256]{1,0:T(8,128)(2,1)S(1)}, bf16[256,256]{1,0:T(8,128)(2,1)S(1)}, u32[]{:S(2)}, u32[]{:S(2)}) collective-permute-start(bf16[256,256]{1,0:T(8,128)(2,1)S(1)} %get-tuple-element.39), channel_id=1, source_target_pairs={{0,6},{1,7},{2,4},{3,5},{4,2},{5,3},{6,0},{7,1},{8,14},{9,15},{10,... | collective-permute-start | bytes 393224 | tf_op jit(solution)/shard_map/ppermute | solution.py:257
  44.5 15.2 %all-to-all-start.1 = ((bf16[8,56,256]{2,1,0:T(8,128)(2,1)}), bf16[8,56,256]{2,1,0:T(8,128)(2,1)S(1)}, u32[]{:S(2)}, u32[]{:S(2)}) async-start(bf16[8,56,256]{2,1,0:T(8,128)(2,1)} %query_project.1.refs_4_), calls=%async_computation.1 | async-start | bytes 458752 | tf_op jit(solution)/shard_map/all_to_all | solution.py:261
  48.8 8.6 %collective-permute-start.14 = (bf16[256,512]{1,0:T(8,128)(2,1)S(1)}, bf16[256,512]{1,0:T(8,128)(2,1)S(1)}, u32[]{:S(2)}, u32[]{:S(2)}) collective-permute-start(bf16[256,512]{1,0:T(8,128)(2,1)S(1)} %cache_relay.1), channel_id=1, source_target_pairs={{0,1},{1,0},{2,3},{3,2},{4,5},{5,4},{6,7},{7,6},{8,9},{9,8},{10,11... | collective-permute-start | bytes 786440 | tf_op jit(solution)/shard_map/ppermute | solution.py:257
  49.3 7.1 %collective-permute-start.11 = (bf16[64,256]{1,0:T(8,128)(2,1)S(1)}, bf16[64,256]{1,0:T(8,128)(2,1)S(1)}, u32[]{:S(2)}, u32[]{:S(2)}) collective-permute-start(bf16[64,256]{1,0:T(8,128)(2,1)S(1)} %get-tuple-element.45), channel_id=1, source_target_pairs={{0,8},{1,0},{2,9},{3,1},{4,10},{5,2},{6,11},{7,3},{8,12},{9,4},{10... | collective-permute-start | bytes 98312 | tf_op jit(solution)/shard_map/ppermute | solution.py:257
  50.8 5.6 %collective-permute-start.12 = (bf16[64,256]{1,0:T(8,128)(2,1)S(1)}, bf16[64,256]{1,0:T(8,128)(2,1)S(1)}, u32[]{:S(2)}, u32[]{:S(2)}) collective-permute-start(bf16[64,256]{1,0:T(8,128)(2,1)S(1)} %get-tuple-element.46), channel_id=1, source_target_pairs={{0,16},{1,24},{2,17},{3,25},{4,18},{5,26},{6,19},{7,27},{8,20},{9,... | collective-permute-start | bytes 98312 | tf_op jit(solution)/shard_map/ppermute | solution.py:257
  52.4 5.0 %collective-permute-start.13 = (bf16[64,256]{1,0:T(8,128)(2,1)S(1)}, bf16[64,256]{1,0:T(8,128)(2,1)S(1)}, u32[]{:S(2)}, u32[]{:S(2)}) collective-permute-start(bf16[64,256]{1,0:T(8,128)(2,1)S(1)} %get-tuple-element.47), channel_id=1, source_target_pairs={{0,24},{1,16},{2,25},{3,17},{4,26},{5,18},{6,27},{7,19},{8,28},{9,... | collective-permute-start | bytes 98312 | tf_op jit(solution)/shard_map/ppermute | solution.py:257
  55.8 1.6 %collective-permute-start.10 = (bf16[64,256]{1,0:T(8,128)(2,1)S(1)}, bf16[64,256]{1,0:T(8,128)(2,1)S(1)}, u32[]{:S(2)}, u32[]{:S(2)}) collective-permute-start(bf16[64,256]{1,0:T(8,128)(2,1)S(1)} %get-tuple-element.44.refs_3_), channel_id=1, source_target_pairs={{0,0},{1,8},{2,1},{3,9},{4,2},{5,10},{6,3},{7,11},{8,4},{9,12},{10... | collective-permute-start | bytes 98312 | tf_op jit(solution)/shard_map/ppermute | solution.py:257
